TPU v7x, 32 devices: a whole 2x2x4 slice. The times are simulated.
32 devices in a mesh: grp: 4 (over y, x), img: 8 (over z, core).
Axes of the slice: x: 2, y: 2, z: 4, core: 2. Of those that a mesh axis runs over, the one named last changes fastest.
Arguments:
- pixels: bfloat16 [128, 8, 196, 256], P(('grp', 'img')), may hold values from -6 to 6
- cotangent: bfloat16 [128, 196, 768], P(('grp', 'img')), may hold values from -6 to 6
- band_count: int32 [4], P('grp'), may hold values from 2 to 8, as said below
- wave_index: int32 [4, 8], P('grp'), may hold values from 0 to 255
- weight_tokens: float32 [128, 128], replicated, may hold values from -6 to 6
- bias_token: float32 [128], replicated, may hold values from -6 to 6
- hyper_qkv: float32 [128, 384], replicated, may hold values from -0.5 to 0.5
- hyper_qv_bias: float32 [256], replicated, may hold values from -3 to 3
- hyper_out: float32 [128, 128], replicated, may hold values from -1.5 to 1.5
- hyper_out_bias: float32 [128], replicated, may hold values from -3 to 3
- hyper_norm1_gain: float32 [128], replicated, may hold values from 0.1 to 1.9
- hyper_norm1_bias: float32 [128], replicated, may hold values from -3 to 3
- hyper_ff1: float32 [128, 2048], replicated, may hold values from -0.5 to 0.5
- hyper_ff1_bias: float32 [2048], replicated, may hold values from -3 to 3
- hyper_ff2: float32 [2048, 128], replicated, may hold values from -0.125 to 0.125
- hyper_ff2_bias: float32 [128], replicated, may hold values from -3 to 3
- hyper_norm2_gain: float32 [128], replicated, may hold values from 0.1 to 1.9
- hyper_norm2_bias: float32 [128], replicated, may hold values from -3 to 3
- kernel_gen: bfloat16 [256, 768, 128], P('img'), may hold values from -0.01171875 to 0.01171875
- kernel_gen_bias: bfloat16 [256, 768], P('img'), may hold values from -0.119628906 to 0.119628906
- conv_bias_gen: bfloat16 [768, 128], P('img'), may hold values from -0.5 to 0.5
- conv_bias_gen_bias: bfloat16 [768], P('img'), may hold values from -3 to 3
- norm1_gain: bfloat16 [768], P('img'), may hold values from 0.099609375 to 1.8984375
- norm1_bias: bfloat16 [768], P('img'), may hold values from -2 to 2
- qkv_weight: bfloat16 [768, 2304], P('img'), may hold values from -0.21875 to 0.21875
- qv_bias: bfloat16 [1536], P('img'), may hold values from -2 to 2
- proj_weight: bfloat16 [768, 768], P('img'), may hold values from -1.75 to 1.75
- proj_bias: bfloat16 [768], P('img'), may hold values from -2 to 2
- norm2_gain: bfloat16 [768], P('img'), may hold values from 0.099609375 to 1.8984375
- norm2_bias: bfloat16 [768], P('img'), may hold values from -2 to 2
- fc1_weight: bfloat16 [768, 3072], P('img'), may hold values from -0.21875 to 0.21875
- fc1_bias: bfloat16 [3072], P('img'), may hold values from -2 to 2
- fc2_weight: bfloat16 [3072, 768], P('img'), may hold values from -0.109375 to 0.109375
- fc2_bias: bfloat16 [768], P('img'), may hold values from -2 to 2
Outputs:
- block_out: float32 [128, 196, 768], P(('grp', 'img'))
- pixel_grad: float32 [128, 8, 196, 256], P(('grp', 'img'))
- grad_weight_tokens: float32 [128, 128], replicated
- grad_bias_token: float32 [128], replicated
- grad_hyper_qkv: float32 [128, 384], replicated
- grad_hyper_qv_bias: float32 [256], replicated
- grad_hyper_out: float32 [128, 128], replicated
- grad_hyper_out_bias: float32 [128], replicated
- grad_hyper_norm1_gain: float32 [128], replicated
- grad_hypernet_norm1_bias: float32 [128], replicated
- grad_hyper_ff1: float32 [128, 2048], replicated
- grad_hyper_ff1_bias: float32 [2048], replicated
- grad_hyper_ff2: float32 [2048, 128], replicated
- grad_hyper_ff2_bias: float32 [128], replicated
- grad_hyper_norm2_gain: float32 [128], replicated
- grad_hyper_norm2_bias: float32 [128], replicated
- grad_kernel_gen: float32 [256, 768, 128], P('img', 'grp')
- grad_kernel_gen_bias: float32 [256, 768], P('img', 'grp')
- grad_conv_bias_gen: float32 [768, 128], P(('grp', 'img'))
- grad_conv_bias_gen_bias: float32 [768], P(('grp', 'img'))
- grad_norm1_gain: float32 [768], P(('grp', 'img'))
- grad_norm1_bias: float32 [768], P(('grp', 'img'))
- grad_qkv_weight: float32 [768, 2304], P(('grp', 'img'))
- grad_qv_bias: float32 [1536], P(('grp', 'img'))
- grad_proj_weight: float32 [768, 768], P(('grp', 'img'))
- grad_proj_bias: float32 [768], P(('grp', 'img'))
- grad_norm2_gain: float32 [768], P(('grp', 'img'))
- grad_norm2_bias: float32 [768], P(('grp', 'img'))
- grad_fc1_weight: float32 [768, 3072], P(('grp', 'img'))
- grad_fc1_bias: float32 [3072], P(('grp', 'img'))
- grad_fc2_weight: float32 [3072, 768], P(('grp', 'img'))
- grad_fc2_bias: float32 [768], P(('grp', 'img'))
Inputs may be any that keep to these rules, and one draw needn't show every extreme that they name: Group g's bands fill its first band_count[g] slots; one group has all 8 slots, each other group at most 4. `wave_index`: rows of a table of 256 wavelengths evenly spaced from 400 to 2500 nanometres.
All inputs are finite; a program needn't handle non-finite values.
Results may differ from a plain program's by a relative error of at most 0.015.
Values may be sent and summed in bfloat16 or wider, within the bound.
No kernel may reach another device: no remote copies, remote signals or barrier semaphores. Data moves between devices by JAX's collectives and lax.ppermute only.
A program may use at most 256 MiB of HBM per device.

v0:
```python
import jax
import jax.numpy as jnp
from jax import lax
from jax.sharding import PartitionSpec as P

HEADS = 12
WHEADS = 4
WAVES = 256


norm_eps = 1e-06
hyper_eps = 1e-05
highest_precision = lax.Precision.HIGHEST


def layer_norm(values, norm_gain, norm_shift, epsilon):
    centre = values - jnp.mean(values, axis=-1, keepdims=True)
    spread = jnp.mean(centre * centre, axis=-1, keepdims=True)
    return centre * lax.rsqrt(spread + epsilon) * norm_gain + norm_shift


def gelu_exact(values):
    return jax.nn.gelu(values, approximate=False)


def wave_embed(indices, hyper_width):
    half_model_width = hyper_width // 2
    wavelength = 400.0 + 2100.0 * indices.astype(jnp.float32) / (WAVES - 1)
    frequency = 1.0 / 10000.0 ** (
        jnp.arange(half_model_width, dtype=jnp.float32) / half_model_width
    )
    angles = wavelength[:, None] * frequency[None, :]
    return jnp.concatenate([jnp.sin(angles), jnp.cos(angles)], axis=-1)


def hyper_forward(params, indices, band_total):
    (
        tokens,
        bias_tok,
        qkv_w,
        qv_b,
        out_w,
        out_b,
        gain_one,
        shift_one,
        ff_in,
        ff_in_b,
        ff_out,
        ff_out_b,
        gain_two,
        shift_two,
    ) = params
    hyper_width = tokens.shape[1]
    slot_count = indices.shape[0]
    token_rows = tokens.shape[0]
    head_dim = hyper_width // WHEADS
    waves = wave_embed(indices, hyper_width)
    joined = jnp.concatenate([tokens, waves, bias_tok[None, :]], axis=0)
    query_rows = joined[token_rows:]
    queries = (
        jnp.dot(query_rows, qkv_w[:, :hyper_width], precision=highest_precision)
        + qv_b[:hyper_width]
    ).reshape(slot_count + 1, WHEADS, head_dim)
    key_rows = jnp.dot(
        joined, qkv_w[:, hyper_width : 2 * hyper_width], precision=highest_precision
    ).reshape(-1, WHEADS, head_dim)
    values = (
        jnp.dot(joined, qkv_w[:, 2 * hyper_width :], precision=highest_precision)
        + qv_b[hyper_width:]
    ).reshape(-1, WHEADS, head_dim)
    scores = jnp.einsum(
        "qhd,khd->hqk", queries, key_rows, precision=highest_precision
    ) * head_dim ** (-0.5)
    offsets = jnp.arange(joined.shape[0]) - token_rows
    usable = (offsets < band_total) | (offsets == slot_count)
    scores = jnp.where(usable[None, None, :], scores, -1e30)
    weights = jax.nn.softmax(scores, axis=-1)
    mixture = jnp.einsum("hqk,khd->qhd", weights, values, precision=highest_precision).reshape(
        slot_count + 1, hyper_width
    )
    normed_one = layer_norm(
        query_rows + jnp.dot(mixture, out_w, precision=highest_precision) + out_b,
        gain_one,
        shift_one,
        hyper_eps,
    )
    hidden = gelu_exact(jnp.dot(normed_one, ff_in, precision=highest_precision) + ff_in_b)
    normed_two = layer_norm(
        normed_one + jnp.dot(hidden, ff_out, precision=highest_precision) + ff_out_b,
        gain_two,
        shift_two,
        hyper_eps,
    )
    return (normed_two[:slot_count] + waves, normed_two[slot_count])


def local(
    pixels,
    cotangent,
    band_count,
    wave_index,
    weight_tokens,
    bias_token,
    hyper_qkv,
    hyper_qv_bias,
    hyper_out,
    hyper_out_bias,
    hyper_norm1_gain,
    hyper_norm1_bias,
    hyper_ff1,
    hyper_ff1_bias,
    hyper_ff2,
    hyper_ff2_bias,
    hyper_norm2_gain,
    hyper_norm2_bias,
    kernel_gen,
    kernel_gen_bias,
    conv_bias_gen,
    conv_bias_gen_bias,
    norm1_gain,
    norm1_bias,
    qkv_weight,
    qv_bias,
    proj_weight,
    proj_bias,
    norm2_gain,
    norm2_bias,
    fc1_weight,
    fc1_bias,
    fc2_weight,
    fc2_bias,
):
    (
        cb_weight,
        cb_shift,
        gain_one,
        shift_one,
        qkv_full,
        qv_full,
        proj_full,
        proj_shift,
        gain_two,
        shift_two,
        fc1_full,
        fc1_shift,
        fc2_full,
        fc2_shift,
    ) = (
        lax.all_gather(conv_bias_gen, "img", axis=0, tiled=True),
        lax.all_gather(conv_bias_gen_bias, "img", axis=0, tiled=True),
        lax.all_gather(norm1_gain, "img", axis=0, tiled=True),
        lax.all_gather(norm1_bias, "img", axis=0, tiled=True),
        lax.all_gather(qkv_weight, "img", axis=0, tiled=True),
        lax.all_gather(qv_bias, "img", axis=0, tiled=True),
        lax.all_gather(proj_weight, "img", axis=0, tiled=True),
        lax.all_gather(proj_bias, "img", axis=0, tiled=True),
        lax.all_gather(norm2_gain, "img", axis=0, tiled=True),
        lax.all_gather(norm2_bias, "img", axis=0, tiled=True),
        lax.all_gather(fc1_weight, "img", axis=0, tiled=True),
        lax.all_gather(fc1_bias, "img", axis=0, tiled=True),
        lax.all_gather(fc2_weight, "img", axis=0, tiled=True),
        lax.all_gather(fc2_bias, "img", axis=0, tiled=True),
    )
    images = pixels.shape[0]
    slot_count = pixels.shape[1]
    tokens = pixels.shape[2]
    model_width = cotangent.shape[2]
    head_dim = model_width // HEADS
    score_scale = head_dim ** (-0.5)
    row_count = images * tokens
    band_total = band_count[0]
    band_mask = (jnp.arange(slot_count) < band_total).astype(jnp.float32)
    hyper_params = (
        weight_tokens,
        bias_token,
        hyper_qkv,
        hyper_qv_bias,
        hyper_out,
        hyper_out_bias,
        hyper_norm1_gain,
        hyper_norm1_bias,
        hyper_ff1,
        hyper_ff1_bias,
        hyper_ff2,
        hyper_ff2_bias,
        hyper_norm2_gain,
        hyper_norm2_bias,
    )
    (hidden, bias_row), hyper_pull = jax.vjp(
        lambda params: hyper_forward(params, wave_index[0], band_total), hyper_params
    )
    hidden_low = hidden.astype(jnp.bfloat16)
    kernel_rows = (
        jnp.einsum(
            "be,pde->bpd",
            hidden_low,
            lax.all_gather(kernel_gen, "img", axis=0, tiled=True),
            preferred_element_type=jnp.float32,
        )
        + lax.all_gather(kernel_gen_bias, "img", axis=0, tiled=True).astype(jnp.float32)[None]
    )
    patch_kernels = (kernel_rows * band_mask[:, None, None]).astype(jnp.bfloat16)
    conv_shift = jnp.dot(
        cb_weight.astype(jnp.float32), bias_row, precision=highest_precision
    ) + cb_shift.astype(jnp.float32)
    embedded_tokens = jnp.einsum(
        "lfhz,fzp->lhp", pixels, patch_kernels, preferred_element_type=jnp.float32
    )
    stream = (embedded_tokens + conv_shift).reshape(row_count, model_width)
    normed_one, norm_one_pull = jax.vjp(
        lambda values, norm_gain, norm_shift: layer_norm(values, norm_gain, norm_shift, norm_eps),
        stream,
        gain_one.astype(jnp.float32),
        shift_one.astype(jnp.float32),
    )
    normed_low = normed_one.astype(jnp.bfloat16)
    full_bias = jnp.concatenate(
        [
            qv_full[:model_width].astype(jnp.float32),
            jnp.zeros((model_width,), jnp.float32),
            qv_full[model_width:].astype(jnp.float32),
        ]
    )
    projected = (
        jnp.dot(normed_low, qkv_full, preferred_element_type=jnp.float32) + full_bias
    ).astype(jnp.bfloat16)
    shaped = projected.reshape(images, tokens, 3, HEADS, head_dim)
    queries = shaped[:, :, 0]
    key_rows = shaped[:, :, 1]
    value_rows = shaped[:, :, 2]
    scores = (
        jnp.einsum("ithd,ishd->ihts", queries, key_rows, preferred_element_type=jnp.float32)
        * score_scale
    )
    row_peak = jnp.max(scores, axis=-1, keepdims=True)
    log_total = row_peak + jnp.log(jnp.sum(jnp.exp(scores - row_peak), axis=-1, keepdims=True))
    attn_probs = jnp.exp(scores - log_total)
    attended = (
        jnp.einsum(
            "ihts,ishd->ithd",
            attn_probs.astype(jnp.bfloat16),
            value_rows,
            preferred_element_type=jnp.float32,
        )
        .reshape(row_count, model_width)
        .astype(jnp.bfloat16)
    )
    middle = (
        stream
        + jnp.dot(attended, proj_full, preferred_element_type=jnp.float32)
        + proj_shift.astype(jnp.float32)
    )
    normed_two, norm_two_pull = jax.vjp(
        lambda values, norm_gain, norm_shift: layer_norm(values, norm_gain, norm_shift, norm_eps),
        middle,
        gain_two.astype(jnp.float32),
        shift_two.astype(jnp.float32),
    )
    normed_two_low = normed_two.astype(jnp.bfloat16)
    gate_in = jnp.dot(
        normed_two_low, fc1_full, preferred_element_type=jnp.float32
    ) + fc1_shift.astype(jnp.float32)
    activated, gelu_pull = jax.vjp(gelu_exact, gate_in)
    activated_low = activated.astype(jnp.bfloat16)
    block_out = (
        middle
        + jnp.dot(activated_low, fc2_full, preferred_element_type=jnp.float32)
        + fc2_shift.astype(jnp.float32)
    )
    upstream = cotangent.astype(jnp.float32).reshape(row_count, model_width)
    upstream_low = upstream.astype(jnp.bfloat16)
    grad_fc2_shift = jnp.sum(upstream_low.astype(jnp.float32), axis=0)
    grad_fc2 = jnp.einsum(
        "tf,td->fd", activated_low, upstream_low, preferred_element_type=jnp.float32
    )
    grad_activated = jnp.einsum(
        "td,fd->tf", upstream_low, fc2_full, preferred_element_type=jnp.float32
    )
    (grad_gate,) = gelu_pull(grad_activated)
    gate_low = grad_gate.astype(jnp.bfloat16)
    grad_fc1_shift = jnp.sum(gate_low.astype(jnp.float32), axis=0)
    grad_fc1 = jnp.einsum("td,tf->df", normed_two_low, gate_low, preferred_element_type=jnp.float32)
    grad_normed_two = jnp.einsum(
        "tf,df->td", gate_low, fc1_full, preferred_element_type=jnp.float32
    )
    grad_middle_part, grad_gain_two, grad_shift_two = norm_two_pull(grad_normed_two)
    grad_middle = upstream + grad_middle_part
    middle_low = grad_middle.astype(jnp.bfloat16)
    grad_proj_shift = jnp.sum(middle_low.astype(jnp.float32), axis=0)
    grad_proj = jnp.einsum("td,te->de", attended, middle_low, preferred_element_type=jnp.float32)
    grad_attended = (
        jnp.einsum("te,de->td", middle_low, proj_full, preferred_element_type=jnp.float32)
        .astype(jnp.bfloat16)
        .reshape(images, tokens, HEADS, head_dim)
    )
    scores_again = (
        jnp.einsum("ithd,ishd->ihts", queries, key_rows, preferred_element_type=jnp.float32)
        * score_scale
    )
    probs_again = jnp.exp(scores_again - log_total)
    grad_values = jnp.einsum(
        "ihts,ithd->ishd",
        probs_again.astype(jnp.bfloat16),
        grad_attended,
        preferred_element_type=jnp.float32,
    )
    grad_probs = jnp.einsum(
        "ithd,ishd->ihts", grad_attended, value_rows, preferred_element_type=jnp.float32
    )
    grad_scores = (
        probs_again * (grad_probs - jnp.sum(grad_probs * probs_again, axis=-1, keepdims=True))
    ).astype(jnp.bfloat16)
    grad_queries = (
        jnp.einsum("ihts,ishd->ithd", grad_scores, key_rows, preferred_element_type=jnp.float32)
        * score_scale
    )
    grad_keys = (
        jnp.einsum("ihts,ithd->ishd", grad_scores, queries, preferred_element_type=jnp.float32)
        * score_scale
    )
    grad_projected = (
        jnp.stack([grad_queries, grad_keys, grad_values], axis=2)
        .reshape(row_count, 3 * model_width)
        .astype(jnp.bfloat16)
    )
    projected_sums = jnp.sum(grad_projected.astype(jnp.float32), axis=0)
    grad_qv = jnp.concatenate([projected_sums[:model_width], projected_sums[2 * model_width :]])
    grad_qkv = jnp.einsum(
        "td,te->de", normed_low, grad_projected, preferred_element_type=jnp.float32
    )
    grad_normed_one = jnp.einsum(
        "te,de->td", grad_projected, qkv_full, preferred_element_type=jnp.float32
    )
    grad_stream_part, grad_gain_one, grad_shift_one = norm_one_pull(grad_normed_one)
    residual_reduced = (
        (grad_middle + grad_stream_part).astype(jnp.bfloat16).reshape(images, tokens, model_width)
    )
    grad_conv_shift = jnp.sum(residual_reduced.astype(jnp.float32), axis=(0, 1))
    grad_kernels = jnp.einsum(
        "mrny,mnu->ryu", pixels, residual_reduced, preferred_element_type=jnp.float32
    )
    grad_pixels = jnp.einsum(
        "ucv,whv->uwch", residual_reduced, patch_kernels, preferred_element_type=jnp.float32
    )
    grad_cb_weight = grad_conv_shift[:, None] * bias_row[None, :]
    grad_bias_row_part = jnp.dot(
        grad_conv_shift, cb_weight.astype(jnp.float32), precision=highest_precision
    )
    group_kernels = lax.psum_scatter(grad_kernels, "img", scatter_dimension=1, tiled=True)
    grad_pre = group_kernels * band_mask[:, None, None]
    grad_hidden_part = jnp.einsum(
        "bpd,pde->be", grad_pre, kernel_gen.astype(jnp.float32), precision=highest_precision
    )
    grad_hidden, grad_bias_row = lax.psum((grad_hidden_part, grad_bias_row_part), "img")
    (hyper_local,) = hyper_pull((grad_hidden, grad_bias_row))
    hyper_total = (
        lax.psum(hyper_local[0].astype(jnp.bfloat16), "grp").astype(jnp.float32),
        lax.psum(hyper_local[1].astype(jnp.bfloat16), "grp").astype(jnp.float32),
        lax.psum(hyper_local[2].astype(jnp.bfloat16), "grp").astype(jnp.float32),
        lax.psum(hyper_local[3].astype(jnp.bfloat16), "grp").astype(jnp.float32),
        lax.psum(hyper_local[4].astype(jnp.bfloat16), "grp").astype(jnp.float32),
        lax.psum(hyper_local[5].astype(jnp.bfloat16), "grp").astype(jnp.float32),
        lax.psum(hyper_local[6].astype(jnp.bfloat16), "grp").astype(jnp.float32),
        lax.psum(hyper_local[7].astype(jnp.bfloat16), "grp").astype(jnp.float32),
        lax.psum(hyper_local[8].astype(jnp.bfloat16), "grp").astype(jnp.float32),
        lax.psum(hyper_local[9].astype(jnp.bfloat16), "grp").astype(jnp.float32),
        lax.psum(hyper_local[10].astype(jnp.bfloat16), "grp").astype(jnp.float32),
        lax.psum(hyper_local[11].astype(jnp.bfloat16), "grp").astype(jnp.float32),
        lax.psum(hyper_local[12].astype(jnp.bfloat16), "grp").astype(jnp.float32),
        lax.psum(hyper_local[13].astype(jnp.bfloat16), "grp").astype(jnp.float32),
    )
    grad_gen_part = jnp.einsum(
        "bpd,be->pde", grad_pre, hidden_low.astype(jnp.float32), precision=highest_precision
    )
    grad_gen_shift_part = jnp.sum(grad_pre, axis=0)
    grad_gen, grad_gen_shift = (
        lax.psum_scatter(
            grad_gen_part.astype(jnp.bfloat16), "grp", scatter_dimension=1, tiled=True
        ).astype(jnp.float32),
        lax.psum_scatter(
            grad_gen_shift_part.astype(jnp.bfloat16), "grp", scatter_dimension=1, tiled=True
        ).astype(jnp.float32),
    )
    reduced = (
        lax.psum_scatter(grad_cb_weight, ("grp", "img"), scatter_dimension=0, tiled=True),
        lax.psum_scatter(grad_conv_shift, ("grp", "img"), scatter_dimension=0, tiled=True),
        lax.psum_scatter(grad_gain_one, ("grp", "img"), scatter_dimension=0, tiled=True),
        lax.psum_scatter(grad_shift_one, ("grp", "img"), scatter_dimension=0, tiled=True),
        lax.psum_scatter(grad_qkv, ("grp", "img"), scatter_dimension=0, tiled=True),
        lax.psum_scatter(grad_qv, ("grp", "img"), scatter_dimension=0, tiled=True),
        lax.psum_scatter(grad_proj, ("grp", "img"), scatter_dimension=0, tiled=True),
        lax.psum_scatter(grad_proj_shift, ("grp", "img"), scatter_dimension=0, tiled=True),
        lax.psum_scatter(grad_gain_two, ("grp", "img"), scatter_dimension=0, tiled=True),
        lax.psum_scatter(grad_shift_two, ("grp", "img"), scatter_dimension=0, tiled=True),
        lax.psum_scatter(grad_fc1, ("grp", "img"), scatter_dimension=0, tiled=True),
        lax.psum_scatter(grad_fc1_shift, ("grp", "img"), scatter_dimension=0, tiled=True),
        lax.psum_scatter(grad_fc2, ("grp", "img"), scatter_dimension=0, tiled=True),
        lax.psum_scatter(grad_fc2_shift, ("grp", "img"), scatter_dimension=0, tiled=True),
    )
    return (
        block_out.reshape(images, tokens, model_width),
        grad_pixels,
        hyper_total[0],
        hyper_total[1],
        hyper_total[2],
        hyper_total[3],
        hyper_total[4],
        hyper_total[5],
        hyper_total[6],
        hyper_total[7],
        hyper_total[8],
        hyper_total[9],
        hyper_total[10],
        hyper_total[11],
        hyper_total[12],
        hyper_total[13],
        grad_gen,
        grad_gen_shift,
        reduced[0],
        reduced[1],
        reduced[2],
        reduced[3],
        reduced[4],
        reduced[5],
        reduced[6],
        reduced[7],
        reduced[8],
        reduced[9],
        reduced[10],
        reduced[11],
        reduced[12],
        reduced[13],
    )


def solution(mesh):
    return jax.shard_map(
        local,
        mesh=mesh,
        in_specs=(
            P(("grp", "img"), None, None, None),
            P(("grp", "img"), None, None),
            P("grp"),
            P("grp", None),
            P(),
            P(),
            P(),
            P(),
            P(),
            P(),
            P(),
            P(),
            P(),
            P(),
            P(),
            P(),
            P(),
            P(),
            P("img", None, None),
            P("img", None),
            P("img", None),
            P("img"),
            P("img"),
            P("img"),
            P("img", None),
            P("img"),
            P("img", None),
            P("img"),
            P("img"),
            P("img"),
            P("img", None),
            P("img"),
            P("img", None),
            P("img"),
        ),
        out_specs=(
            P(("grp", "img"), None, None),
            P(("grp", "img"), None, None, None),
            P(),
            P(),
            P(),
            P(),
            P(),
            P(),
            P(),
            P(),
            P(),
            P(),
            P(),
            P(),
            P(),
            P(),
            P("img", "grp", None),
            P("img", "grp"),
            P(("grp", "img"), None),
            P(("grp", "img")),
            P(("grp", "img")),
            P(("grp", "img")),
            P(("grp", "img"), None),
            P(("grp", "img")),
            P(("grp", "img"), None),
            P(("grp", "img")),
            P(("grp", "img")),
            P(("grp", "img")),
            P(("grp", "img"), None),
            P(("grp", "img")),
            P(("grp", "img"), None),
            P(("grp", "img")),
        ),
        check_vma=False,
    )
```

profile of v0, /device:TPU:0, one launch (start us, length us, event | category | flops | bytes accessed | tf_op | source)
XLA Modules:
  0.0 1654.2 jit_solution(9655170553381524002)
XLA Ops:
  15.5 31.5 %all-reduce.27 = (bf16[768]{0:T(1024)(128)(2,1)S(1)}, bf16[1536]{0:T(1024)(128)(2,1)S(1)}, bf16[768]{0:T(1024)(128)(2,1)S(1)}, bf16[768]{0:T(1024)(128)(2,1)S(1)...) all-reduce(bf16[768]{0:T(1024)(128)(2,1)S(1)} %dynamic-update-slice, ...), channel_id=1, replica_groups=mesh['grp'=4,'img'=8] {'img'}, use_global_device_ids=true, to_apply=%add.8 | all-reduce | flops 6912 | bytes 27648
  48.1 23.9 %all-gather = bf16[8,1,384]{2,1,0:T(2,128)(2,1)S(1)} all-gather(bf16[1,1,384]{2,1,0:T(2,128)(2,1)S(1)} %reshape.409), channel_id=1, replica_groups=mesh['grp'=4,'img'=8] {'img'}, dimensions={0}, use_global_device_ids=true | all-gather | bytes 6912 | tf_op jit(solution)/shard_map/all_gather | solution.py:160
  77.5 29.0 %all_gather.50 = bf16[768,128]{1,0:T(8,128)(2,1)S(1)} all-gather(bf16[96,128]{1,0:T(8,128)(2,1)S(1)} %copy-done.63), channel_id=1, replica_groups=mesh['grp'=4,'img'=8] {'img'}, dimensions={0}, use_global_device_ids=true | all-gather | bytes 221184 | tf_op jit(solution)/shard_map/all_gather | solution.py:149
  107.4 34.8 %all_gather.49 = bf16[256,768]{1,0:T(8,128)(2,1)S(1)} all-gather(bf16[32,768]{1,0:T(8,128)(2,1)S(1)} %copy-done.53), channel_id=1, replica_groups=mesh['grp'=4,'img'=8] {'img'}, dimensions={0}, use_global_device_ids=true | all-gather | bytes 442368 | tf_op jit(solution)/shard_map/all_gather | solution.py:200
  146.2 8.1 copy.153
  155.0 290.2 %all-gather.7.cloned.1.call-done = bf16[256,768,128]{2,1,0:T(8,128)(2,1)} async-done(((bf16[32,768,128]{2,1,0:T(8,128)(2,1)}), bf16[256,768,128]{2,1,0:T(8,128)(2,1)}) %all-gather.7.cloned.1.call-update) | async-done | bytes 50331664 | tf_op jit(solution)/shard_map/all_gather | solution.py:197
  445.2 21.3 %fusion.9 = bf16[8,256,768,1]{2,0,1,3:T(8,128)(2,1)} fusion(f32[8]{0:T(128)S(1)} %compare_convert_fusion, f32[256,768]{1,0:T(8,128)S(1)} %copy-done.21, bf16[8,128,1]{1,0,2:T(8,128)(2,1)S(1)} %fusion.102, bf16[256,768,128]{2,1,0:T(8,128)(2,1)} %all-gather.7.cloned.1.call-done), kind=kOutput, calls=%fused_computation.33 | convolution fusion | flops 407371776 | bytes 54265888 | tf_op jit(solution)/shard_map/be,pde->bpd/dot_general | solution.py:194
  466.5 5.9 fusion.132
  475.3 11.3 all-gather.9.cloned.1.call-done
  486.6 7.7 add_convert_fusion.1
  494.3 11.8 reshape.442
  506.1 7.0 fusion.126
  513.2 4.8 copy.196
  518.0 4.0 copy.195
  522.0 6.0 copy.197
  528.0 3.4 multiply_reduce_fusion.1
  531.4 2.1 exponential_reduce_fusion
  535.2 2.0 fusion.27
  538.4 2.0 convert_element_type.250
  540.5 3.7 fusion.133
  544.7 18.1 %all-gather.13.cloned.1.call-done = bf16[768,3072]{1,0:T(8,128)(2,1)} async-done(((bf16[96,3072]{1,0:T(8,128)(2,1)}), bf16[768,3072]{1,0:T(8,128)(2,1)}) %all-gather.13.cloned.1.call-update) | async-done | bytes 4718608 | tf_op jit(solution)/shard_map/all_gather | solution.py:159
  562.8 28.4 %multiply_convert_fusion.1 = (bf16[784,3072]{1,0:T(8,128)(2,1)}, f32[784,3072]{1,0:T(8,128)}, f32[784,3072]{1,0:T(8,128)}) fusion(f32[3072]{0:T(1024)S(1)} %bitcast.174, bf16[768,3072]{1,0:T(8,128)(2,1)} %all-gather.13.cloned.1.call-done, f32[784,768]{1,0:T(8,128)S(1)} %get-tuple-element.243, f32[768]{0:T(1024)S(1)} %convert_element_type.253, ...), kind=kOutput, calls=%fused_computation.8 | convolution fusion | flops 3861344256 | bytes 31236224 | tf_op jit(solution)/shard_map/dot_general | solution.py:260
  591.2 23.6 %all-gather.15.cloned.1.call-done = bf16[3072,768]{1,0:T(8,128)(2,1)} async-done(((bf16[384,768]{1,0:T(8,128)(2,1)}), bf16[3072,768]{1,0:T(8,128)(2,1)}) %all-gather.15.cloned.1.call-update) | async-done | bytes 4718608 | tf_op jit(solution)/shard_map/all_gather | solution.py:161
  614.8 14.5 convert_reduce_fusion
  629.3 8.4 multiply_reduce_fusion.3
  642.2 3.1 reshape.443
  645.2 3.9 copy.162
  649.2 7.0 convolution_bitcast_fusion
  656.2 7.8 multiply_reduce_fusion
  664.0 11.7 multiply_convert_fusion
  675.7 4.2 multiply_bitcast_fusion
  681.4 1.8 convert_reduce_fusion.1
  683.3 6.7 copy.167
  689.9 9.9 convert_element_type.265
  699.9 8.0 multiply_reduce_fusion.4
  711.1 7.8 fusion.15
  718.8 6.8 copy.170
  726.9 67.6 %reduce-scatter.13.cloned.1.call-done = f32[8,32,768]{2,0,1:T(8,128)} async-done(((f32[8,256,768]{2,0,1:T(8,128)}), f32[8,32,768]{2,0,1:T(8,128)}) %reduce-scatter.13.cloned.1.call-update) | async-done | bytes 786448 | tf_op jit(solution)/shard_map/reduce_scatter | solution.py:349
  794.4 5.6 convolution_bitcast_fusion.3
  800.2 14.3 psum.128
  816.1 1.8 fusion.135
  826.5 1.9 convolution_convert_fusion.2
  828.4 2.8 convolution_convert_fusion.1
  833.9 11.9 convolution_convert_fusion
  847.8 4.6 fusion.138
  855.4 8.2 fusion.137
  865.3 10.2 fusion.118
  876.1 9.9 fusion.43
  886.7 1.8 convert_reduce_fusion.4
  888.5 9.2 add_add_fusion.3
  897.7 1.8 reshape.377
  899.5 2.4 copy.176
  902.1 39.2 %all-reduce.26 = (f32[768]{0:T(1024)S(1)}, f32[768]{0:T(1024)S(1)}, f32[768]{0:T(1024)S(1)}, f32[1536]{0:T(1024)S(1)}, f32[768]{0:T(1024)S(1)}, /*index=5*/f32[7...) all-reduce(f32[768]{0:T(1024)S(1)} %get-tuple-element.211, ...), channel_id=6, replica_groups=mesh['grp'=4,'img'=8] {'grp','img'}, use_global_device_ids=true, to_apply=%region_53.54.clone | all-reduce | flops 9984 | bytes 79872
  945.3 5.0 fusion.12
  950.3 6.5 copy.177
  974.4 2.1 convert_element_type.284
  976.5 2.1 convert_element_type.288
  978.6 56.2 %reduce-scatter.15.cloned.1.call-done = bf16[32,192,128]{2,1,0:T(8,128)(2,1)} async-done(((bf16[32,768,128]{2,1,0:T(8,128)(2,1)}), bf16[32,192,128]{2,1,0:T(8,128)(2,1)}) %reduce-scatter.15.cloned.1.call-update) | async-done | bytes 1572880 | tf_op jit(solution)/shard_map/reduce_scatter | solution.py:377
  1034.8 3.4 convert_element_type.296
  1038.2 96.9 %reduce-scatter.27.cloned.1.call-done = f32[24,128]{1,0:T(8,128)} async-done(((f32[768,128]{1,0:T(8,128)}), f32[24,128]{1,0:T(8,128)}) %reduce-scatter.27.cloned.1.call-update) | async-done | bytes 12304
  1135.1 104.8 %reduce-scatter.19.cloned.1.call-done = f32[24,768]{1,0:T(8,128)} async-done(((f32[768,768]{1,0:T(8,128)}), f32[24,768]{1,0:T(8,128)}) %reduce-scatter.19.cloned.1.call-update) | async-done | bytes 73744 | tf_op jit(solution)/shard_map/reduce_scatter | solution.py:391
  1239.9 124.4 %reduce-scatter.17.cloned.1.call-done = f32[24,2304]{1,0:T(8,128)} async-done(((f32[768,2304]{1,0:T(8,128)}), f32[24,2304]{1,0:T(8,128)}) %reduce-scatter.17.cloned.1.call-update) | async-done | bytes 221200 | tf_op jit(solution)/shard_map/reduce_scatter | solution.py:389
  1364.2 142.2 %reduce-scatter.21.cloned.1.call-done = f32[24,3072]{1,0:T(8,128)} async-done(((f32[768,3072]{1,0:T(8,128)}), f32[24,3072]{1,0:T(8,128)}) %reduce-scatter.21.cloned.1.call-update) | async-done | bytes 294928 | tf_op jit(solution)/shard_map/reduce_scatter | solution.py:395
  1506.4 141.1 %reduce-scatter.23.cloned.1.call-done = f32[96,768]{1,0:T(8,128)} async-done(((f32[3072,768]{1,0:T(8,128)}), f32[96,768]{1,0:T(8,128)}) %reduce-scatter.23.cloned.1.call-update) | async-done | bytes 294928 | tf_op jit(solution)/shard_map/reduce_scatter | solution.py:397
  (432 shorter events, 76.5 us)
Async XLA Ops:
  7.2 68.7 %copy-start = (f32[2048,128]{1,0:T(8,128)S(1)}, f32[2048,128]{1,0:T(8,128)}, u32[]{:S(2)}) copy-start(f32[2048,128]{1,0:T(8,128)} %param.48) | copy-start | bytes 3145732
  7.4 40.4 %copy-start.28 = (f32[128,384]{1,0:T(8,128)S(1)}, f32[128,384]{1,0:T(8,128)}, u32[]{:S(2)}) copy-start(f32[128,384]{1,0:T(8,128)} %param.40) | copy-start | bytes 589828
  7.4 40.4 %copy-start.61 = (f32[128]{0:T(128)S(1)}, f32[128]{0:T(128)}, u32[]{:S(2)}) copy-start(f32[128]{0:T(128)} %param.39) | copy-start | bytes 1540
  7.4 65.3 %copy-start.26 = (f32[128,128]{1,0:T(8,128)S(1)}, f32[128,128]{1,0:T(8,128)}, u32[]{:S(2)}) copy-start(f32[128,128]{1,0:T(8,128)} %param.38) | copy-start | bytes 196612
  7.4 67.4 %copy-start.42 = (f32[128,128]{1,0:T(8,128)S(1)}, f32[128,128]{1,0:T(8,128)}, u32[]{:S(2)}) copy-start(f32[128,128]{1,0:T(8,128)} %param.42) | copy-start | bytes 196612
  7.4 67.3 %copy-start.103 = (f32[128]{0:T(128)S(1)}, f32[128]{0:T(128)}, u32[]{:S(2)}) copy-start(f32[128]{0:T(128)} %param.43) | copy-start | bytes 1540
  7.4 67.9 %copy-start.80 = (f32[128]{0:T(128)S(1)}, f32[128]{0:T(128)}, u32[]{:S(2)}) copy-start(f32[128]{0:T(128)} %param.44) | copy-start | bytes 1540
  7.4 67.9 %copy-start.99 = (f32[128]{0:T(128)S(1)}, f32[128]{0:T(128)}, u32[]{:S(2)}) copy-start(f32[128]{0:T(128)} %param.45) | copy-start | bytes 1540
  7.4 67.9 %copy-start.19 = (f32[128,2048]{1,0:T(8,128)S(1)}, f32[128,2048]{1,0:T(8,128)}, u32[]{:S(2)}) copy-start(f32[128,2048]{1,0:T(8,128)} %param.46) | copy-start | bytes 3145732
  7.4 67.9 %copy-start.84 = (f32[2048]{0:T(1024)S(1)}, f32[2048]{0:T(1024)}, u32[]{:S(2)}) copy-start(f32[2048]{0:T(1024)} %param.47) | copy-start | bytes 24580
  7.5 437.7 %all-gather.7.cloned.1.call-start = ((), (), s32[]{:S(2)}) async-start(), calls=%async_computation.8 | async-start | bytes 56623104 | tf_op jit(solution)/shard_map/all_gather | solution.py:197
  8.2 67.8 %copy-start.121 = (f32[128]{0:T(128)S(1)}, f32[128]{0:T(128)}, u32[]{:S(2)}) copy-start(f32[128]{0:T(128)} %param.49) | copy-start | bytes 1540
  8.2 478.4 %all-gather.9.cloned.1.call-start = ((), (), s32[]{:S(2)}) async-start(), calls=%async_computation.9 | async-start | bytes 3981312 | tf_op jit(solution)/shard_map/all_gather | solution.py:153
  8.9 531.5 %all-gather.11.cloned.1.call-start = ((), (), s32[]{:S(2)}) async-start(), calls=%async_computation.10 | async-start | bytes 1327104 | tf_op jit(solution)/shard_map/all_gather | solution.py:155
  9.7 67.6 %copy-start.91 = (f32[128]{0:T(128)S(1)}, f32[128]{0:T(128)}, u32[]{:S(2)}) copy-start(f32[128]{0:T(128)} %param.50) | copy-start | bytes 1540
  9.7 67.6 %copy-start.106 = (f32[128]{0:T(128)S(1)}, f32[128]{0:T(128)}, u32[]{:S(2)}) copy-start(f32[128]{0:T(128)} %param.51) | copy-start | bytes 1540
  9.7 67.7 %copy-start.63 = (bf16[96,128]{1,0:T(8,128)(2,1)S(1)}, bf16[96,128]{1,0:T(8,128)(2,1)}, u32[]{:S(2)}) copy-start(bf16[96,128]{1,0:T(8,128)(2,1)} %param.54) | copy-start | bytes 73732
  9.7 553.1 %all-gather.13.cloned.1.call-start = ((), (), s32[]{:S(2)}) async-start(), calls=%async_computation.11 | async-start | bytes 5308416 | tf_op jit(solution)/shard_map/all_gather | solution.py:159
  10.3 97.1 %copy-start.53 = (bf16[32,768]{1,0:T(8,128)(2,1)S(1)}, bf16[32,768]{1,0:T(8,128)(2,1)}, u32[]{:S(2)}) copy-start(bf16[32,768]{1,0:T(8,128)(2,1)} %param.53) | copy-start | bytes 147460
  10.3 604.5 %all-gather.15.cloned.1.call-start = ((), (), s32[]{:S(2)}) async-start(), calls=%async_computation.12 | async-start | bytes 5308416 | tf_op jit(solution)/shard_map/all_gather | solution.py:161
  10.9 783.5 %reduce-scatter.13.cloned.1.call-start = ((), (), s32[]{:S(2)}) async-start(), calls=%async_computation.13 | async-start | bytes 7077888 | tf_op jit(solution)/shard_map/reduce_scatter | solution.py:349
  13.5 431.7 %copy-start.89 = (f32[8]{0:T(128)}, f32[8]{0:T(128)S(1)}, u32[]{:S(2)}) copy-start(f32[8]{0:T(128)S(1)} %compare_convert_fusion) | copy-start | bytes 100
  13.6 128.6 %copy-start.104 = (pred[137]{0:T(512)(128)(4,1)}, pred[137]{0:T(512)(128)(4,1)S(1)}, u32[]{:S(2)}) copy-start(pred[137]{0:T(512)(128)(4,1)S(1)} %compare_or_fusion) | copy-start | bytes 415
  47.0 439.5 %copy-start.54 = (f32[768]{0:T(1024)}, f32[768]{0:T(1024)S(1)}, u32[]{:S(2)}) copy-start(f32[768]{0:T(1024)S(1)} %convert_element_type.241) | copy-start | bytes 9220
  47.0 439.5 %copy-start.69 = (f32[768]{0:T(1024)}, f32[768]{0:T(1024)S(1)}, u32[]{:S(2)}) copy-start(f32[768]{0:T(1024)S(1)} %convert_element_type.242) | copy-start | bytes 9220
  47.8 94.4 %copy-start.36 = (f32[8,64]{1,0:T(8,128)}, f32[8,64]{1,0:T(8,128)S(1)}, u32[]{:S(2)}) copy-start(f32[8,64]{1,0:T(8,128)S(1)} %get-tuple-element.230) | copy-start | bytes 6148
  47.8 94.4 %copy-start.38 = (f32[8,64]{1,0:T(8,128)}, f32[8,64]{1,0:T(8,128)S(1)}, u32[]{:S(2)}) copy-start(f32[8,64]{1,0:T(8,128)S(1)} %get-tuple-element.231) | copy-start | bytes 6148
  48.1 94.1 %copy-start.44 = (f32[9,4,32]{2,1,0:T(4,128)}, f32[9,4,32]{2,1,0:T(4,128)S(1)}, u32[]{:S(2)}) copy-start(f32[9,4,32]{2,1,0:T(4,128)S(1)} %reshape.372) | copy-start | bytes 13828
  73.0 69.2 %copy-start.32 = (f32[137,128]{0,1:T(8,128)}, f32[137,128]{0,1:T(8,128)S(1)}, u32[]{:S(2)}) copy-start(f32[137,128]{0,1:T(8,128)S(1)} %fusion.59) | copy-start | bytes 210436
  73.4 68.8 %copy-start.34 = (f32[137,128]{0,1:T(8,128)}, f32[137,128]{0,1:T(8,128)S(1)}, u32[]{:S(2)}) copy-start(f32[137,128]{0,1:T(8,128)S(1)} %copy.149) | copy-start | bytes 210436
  75.0 67.2 %copy-start.40 = (f32[9,128]{1,0:T(8,128)}, f32[9,128]{1,0:T(8,128)S(1)}, u32[]{:S(2)}) copy-start(f32[9,128]{1,0:T(8,128)S(1)} %get-tuple-element.235) | copy-start | bytes 13828
  75.2 67.0 %copy-start.107 = (f32[9]{0:T(128)}, f32[9]{0:T(128)S(1)}, u32[]{:S(2)}) copy-start(f32[9]{0:T(128)S(1)} %multiply_reduce_fusion.15) | copy-start | bytes 112
  76.0 66.3 %copy-start.46 = (f32[9,2048]{1,0:T(8,128)}, f32[9,2048]{1,0:T(8,128)S(1)}, u32[]{:S(2)}) copy-start(f32[9,2048]{1,0:T(8,128)S(1)} %convolution_add_fusion) | copy-start | bytes 221188
  77.0 65.2 %copy-start.48 = (f32[9,128]{1,0:T(8,128)}, f32[9,128]{1,0:T(8,128)S(1)}, u32[]{:S(2)}) copy-start(f32[9,128]{1,0:T(8,128)S(1)} %get-tuple-element.237) | copy-start | bytes 13828
  77.0 65.2 %copy-start.85 = (f32[9]{0:T(128)}, f32[9]{0:T(128)S(1)}, u32[]{:S(2)}) copy-start(f32[9]{0:T(128)S(1)} %broadcast_multiply_fusion.3) | copy-start | bytes 112
  77.2 65.0 %copy-start.109 = (f32[9]{0:T(128)}, f32[9]{0:T(128)S(1)}, u32[]{:S(2)}) copy-start(f32[9]{0:T(128)S(1)} %multiply_reduce_fusion.14) | copy-start | bytes 112
  77.3 65.0 %copy-start.93 = (f32[9]{0:T(128)}, f32[9]{0:T(128)S(1)}, u32[]{:S(2)}) copy-start(f32[9]{0:T(128)S(1)} %fusion.106) | copy-start | bytes 112
  77.4 68.9 %copy-start.58 = (f32[9,128]{1,0:T(8,128)}, f32[9,128]{1,0:T(8,128)S(1)}, u32[]{:S(2)}) copy-start(f32[9,128]{1,0:T(8,128)S(1)} %multiply_add_fusion.1) | copy-start | bytes 13828
  77.4 367.7 %copy-start.66 = (bf16[8,128,1]{1,0,2:T(8,128)(2,1)}, bf16[8,128,1]{1,0,2:T(8,128)(2,1)S(1)}, u32[]{:S(2)}) copy-start(bf16[8,128,1]{1,0,2:T(8,128)(2,1)S(1)} %fusion.102) | copy-start | bytes 6148
  146.2 298.9 %copy-start.21 = (f32[256,768]{1,0:T(8,128)S(1)}, f32[256,768]{1,0:T(8,128)}, u32[]{:S(2)}) copy-start(f32[256,768]{1,0:T(8,128)} %convert_element_type.237) | copy-start | bytes 2359300
  544.2 93.5 %copy-start.5 = (f32[784,768]{1,0:T(8,128)}, f32[784,768]{1,0:T(8,128)S(1)}, u32[]{:S(2)}) copy-start(f32[784,768]{1,0:T(8,128)S(1)} %get-tuple-element.243) | copy-start | bytes 7225348
  725.6 68.8 %copy-start.90 = (f32[8]{0:T(128)S(1)}, f32[8]{0:T(128)}, u32[]{:S(2)}) copy-start(f32[8]{0:T(128)} %copy-done.89) | copy-start | bytes 100
  725.6 232.3 %all-reduce.33.cloned.1.call-start = ((), (), s32[]{:S(2)}) async-start(), calls=%async_computation.21 | async-start | bytes 147456 | tf_op jit(solution)/shard_map/psum | solution.py:357
  726.7 87.8 %copy-start.49 = (f32[9,128]{1,0:T(8,128)S(1)}, f32[9,128]{1,0:T(8,128)}, u32[]{:S(2)}) copy-start(f32[9,128]{1,0:T(8,128)} %copy-done.48) | copy-start | bytes 13828
  726.7 87.8 %copy-start.86 = (f32[9]{0:T(128)S(1)}, f32[9]{0:T(128)}, u32[]{:S(2)}) copy-start(f32[9]{0:T(128)} %copy-done.85) | copy-start | bytes 112
  726.7 87.8 %copy-start.92 = (f32[128]{0:T(128)S(1)}, f32[128]{0:T(128)}, u32[]{:S(2)}) copy-start(f32[128]{0:T(128)} %param.50) | copy-start | bytes 1540
  726.8 87.8 %copy-start.94 = (f32[9]{0:T(128)S(1)}, f32[9]{0:T(128)}, u32[]{:S(2)}) copy-start(f32[9]{0:T(128)} %copy-done.93) | copy-start | bytes 112
  726.8 88.5 %copy-start.110 = (f32[9]{0:T(128)S(1)}, f32[9]{0:T(128)}, u32[]{:S(2)}) copy-start(f32[9]{0:T(128)} %copy-done.109) | copy-start | bytes 112
  726.8 89.3 %copy-start.47 = (f32[9,2048]{1,0:T(8,128)S(1)}, f32[9,2048]{1,0:T(8,128)}, u32[]{:S(2)}) copy-start(f32[9,2048]{1,0:T(8,128)} %copy-done.46) | copy-start | bytes 221188
  726.8 91.1 %copy-start.20 = (f32[128,2048]{1,0:T(8,128)S(1)}, f32[128,2048]{1,0:T(8,128)}, u32[]{:S(2)}) copy-start(f32[128,2048]{1,0:T(8,128)} %param.46) | copy-start | bytes 3145732
  726.8 91.1 %copy-start.41 = (f32[9,128]{1,0:T(8,128)S(1)}, f32[9,128]{1,0:T(8,128)}, u32[]{:S(2)}) copy-start(f32[9,128]{1,0:T(8,128)} %copy-done.40) | copy-start | bytes 13828
  726.8 91.1 %copy-start.76 = (f32[9]{0:T(128)S(1)}, f32[9]{0:T(128)}, u32[]{:S(2)}) copy-start(f32[9]{0:T(128)} %copy-done.75) | copy-start | bytes 112
  726.8 91.0 %copy-start.81 = (f32[128]{0:T(128)S(1)}, f32[128]{0:T(128)}, u32[]{:S(2)}) copy-start(f32[128]{0:T(128)} %param.44) | copy-start | bytes 1540
  726.8 91.0 %copy-start.83 = (f32[9]{0:T(128)S(1)}, f32[9]{0:T(128)}, u32[]{:S(2)}) copy-start(f32[9]{0:T(128)} %copy-done.82) | copy-start | bytes 112
  800.2 23.1 %copy-start.39 = (f32[8,64]{1,0:T(8,128)S(1)}, f32[8,64]{1,0:T(8,128)}, u32[]{:S(2)}) copy-start(f32[8,64]{1,0:T(8,128)} %copy-done.38) | copy-start | bytes 6148
  800.2 23.5 %copy-start.27 = (f32[128,128]{1,0:T(8,128)S(1)}, f32[128,128]{1,0:T(8,128)}, u32[]{:S(2)}) copy-start(f32[128,128]{1,0:T(8,128)} %param.38) | copy-start | bytes 196612
  831.9 139.4 %reduce-scatter.25.cloned.1.call-start = ((), (), s32[]{:S(2)}) async-start(), calls=%async_computation.19 | async-start | bytes 245760
  833.1 139.7 %all-reduce.35.cloned.1.call-start = ((), (), s32[]{:S(2)}) async-start(), calls=%async_computation.22 | async-start | bytes 2293760 | tf_op jit(solution)/shard_map/psum | solution.py:359
  833.8 201.0 %reduce-scatter.15.cloned.1.call-start = ((), (), s32[]{:S(2)}) async-start(), calls=%async_computation.14 | async-start | bytes 7864320 | tf_op jit(solution)/shard_map/reduce_scatter | solution.py:377
  845.8 289.3 %reduce-scatter.27.cloned.1.call-start = ((), (), s32[]{:S(2)}) async-start(), calls=%async_computation.20 | async-start | bytes 405504
  847.5 392.4 %reduce-scatter.19.cloned.1.call-start = ((), (), s32[]{:S(2)}) async-start(), calls=%async_computation.16 | async-start | bytes 2433024 | tf_op jit(solution)/shard_map/reduce_scatter | solution.py:391
  852.5 511.8 %reduce-scatter.17.cloned.1.call-start = ((), (), s32[]{:S(2)}) async-start(), calls=%async_computation.15 | async-start | bytes 7299072 | tf_op jit(solution)/shard_map/reduce_scatter | solution.py:389
  863.7 642.8 %reduce-scatter.21.cloned.1.call-start = ((), (), s32[]{:S(2)}) async-start(), calls=%async_computation.17 | async-start | bytes 9732096 | tf_op jit(solution)/shard_map/reduce_scatter | solution.py:395
  875.6 771.9 %reduce-scatter.23.cloned.1.call-start = ((), (), s32[]{:S(2)}) async-start(), calls=%async_computation.18 | async-start | bytes 9732096 | tf_op jit(solution)/shard_map/reduce_scatter | solution.py:397
  (74 other events, 629.3 us)
Sparse Core Ops, SparseCore 0:
  9.9 435.1 all-gather.6
  446.8 39.6 all-gather.8
  488.2 21.5 all-gather.10
  511.3 51.4 all-gather.12
  564.3 50.5 all-gather.14
  725.8 68.6 reduce-scatter.12
  832.0 41.2 all-reduce.32
  876.9 25.8 reduce-scatter.24
  907.1 54.5 all-reduce.34
  964.5 70.2 reduce-scatter.14
  1040.3 94.7 reduce-scatter.26
  1141.7 98.1 reduce-scatter.18
  1246.1 118.0 reduce-scatter.16
  1371.6 134.8 reduce-scatter.20
  1512.8 134.6 reduce-scatter.22
where the time goes:
time: 1660 us; the launch traced here: 1650 us
  waiting for transfers between devices  1080 us (65%)
  matrix products  213 us (13%)
  blocking collectives  173 us (10%)
  local copies, waits for them, and re-layouts  115 us (7%)
  other arithmetic  54.5 us (3%)
  between operations  17.9 us (1%)
    all_gather x1, waiting for transfers between devices, local(): lax.all_gather(kernel_gen, 'img', axis=0, tiled=True)  290 us
    reduce_scatter x1, waiting for transfers between devices, local(): lax.psum_scatter(grad_fc1, ('grp', 'img'), scatter_dimension=0, tiled=True)  142 us
    reduce_scatter x1, waiting for transfers between devices, local(): lax.psum_scatter(grad_fc2, ('grp', 'img'), scatter_dimension=0, tiled=True)  141 us
    reduce_scatter x1, waiting for transfers between devices, local(): lax.psum_scatter(grad_qkv, ('grp', 'img'), scatter_dimension=0, tiled=True)  124 us
    reduce_scatter x1, waiting for transfers between devices, local(): lax.psum_scatter(grad_proj, ('grp', 'img'), scatter_dimension=0, tiled=True)  105 us
    unnamed x17, waiting for transfers between devices  100 us
    unnamed x2, blocking collectives  70.6 us
    reduce_scatter x1, waiting for transfers between devices, local(): lax.psum_scatter(grad_kernels, 'img', scatter_dimension=1, tiled=True)  67.6 us
  transfers between devices with their start and end apart: 15, of which 11 were waited for; matrix products, arithmetic and copies ran while one was open for 15% of the time, Pallas kernels for 0%

commit v1 on v0

v1 whole, which is shorter than its diff:
```python
import functools

import jax
import jax.numpy as jnp
from jax import lax
from jax.experimental import pallas as pl
from jax.experimental.pallas import tpu as pltpu
from jax.sharding import PartitionSpec as P

HEADS = 12
WHEADS = 4
WAVES = 256


norm_eps = 1e-06
hyper_eps = 1e-05
highest_precision = lax.Precision.HIGHEST


def layer_norm(values, norm_gain, norm_shift, epsilon):
    centre = values - jnp.mean(values, axis=-1, keepdims=True)
    spread = jnp.mean(centre * centre, axis=-1, keepdims=True)
    return centre * lax.rsqrt(spread + epsilon) * norm_gain + norm_shift


def gelu_exact(values):
    return jax.nn.gelu(values, approximate=False)


def wave_embed(indices, hyper_width):
    half_model_width = hyper_width // 2
    wavelength = 400.0 + 2100.0 * indices.astype(jnp.float32) / (WAVES - 1)
    frequency = 1.0 / 10000.0 ** (
        jnp.arange(half_model_width, dtype=jnp.float32) / half_model_width
    )
    angles = wavelength[:, None] * frequency[None, :]
    return jnp.concatenate([jnp.sin(angles), jnp.cos(angles)], axis=-1)


def hyper_forward(params, indices, band_total):
    (
        tokens,
        bias_tok,
        qkv_w,
        qv_b,
        out_w,
        out_b,
        gain_one,
        shift_one,
        ff_in,
        ff_in_b,
        ff_out,
        ff_out_b,
        gain_two,
        shift_two,
    ) = params
    hyper_width = tokens.shape[1]
    slot_count = indices.shape[0]
    token_rows = tokens.shape[0]
    head_dim = hyper_width // WHEADS
    waves = wave_embed(indices, hyper_width)
    joined = jnp.concatenate([tokens, waves, bias_tok[None, :]], axis=0)
    query_rows = joined[token_rows:]
    queries = (
        jnp.dot(query_rows, qkv_w[:, :hyper_width], precision=highest_precision)
        + qv_b[:hyper_width]
    ).reshape(slot_count + 1, WHEADS, head_dim)
    key_rows = jnp.dot(
        joined, qkv_w[:, hyper_width : 2 * hyper_width], precision=highest_precision
    ).reshape(-1, WHEADS, head_dim)
    values = (
        jnp.dot(joined, qkv_w[:, 2 * hyper_width :], precision=highest_precision)
        + qv_b[hyper_width:]
    ).reshape(-1, WHEADS, head_dim)
    scores = jnp.einsum(
        "qhd,khd->hqk", queries, key_rows, precision=highest_precision
    ) * head_dim ** (-0.5)
    offsets = jnp.arange(joined.shape[0]) - token_rows
    usable = (offsets < band_total) | (offsets == slot_count)
    scores = jnp.where(usable[None, None, :], scores, -1e30)
    weights = jax.nn.softmax(scores, axis=-1)
    mixture = jnp.einsum("hqk,khd->qhd", weights, values, precision=highest_precision).reshape(
        slot_count + 1, hyper_width
    )
    normed_one = layer_norm(
        query_rows + jnp.dot(mixture, out_w, precision=highest_precision) + out_b,
        gain_one,
        shift_one,
        hyper_eps,
    )
    hidden = gelu_exact(jnp.dot(normed_one, ff_in, precision=highest_precision) + ff_in_b)
    normed_two = layer_norm(
        normed_one + jnp.dot(hidden, ff_out, precision=highest_precision) + ff_out_b,
        gain_two,
        shift_two,
        hyper_eps,
    )
    return (normed_two[:slot_count] + waves, normed_two[slot_count])


BOTH = ("grp", "img")


def torus_block():
    return lax.axis_size("grp") == 4 and lax.axis_size("img") == 8


def flipped(index, bit):
    return index ^ bit


def swap(value, bit):
    return lax.ppermute(value, BOTH, [(i, i ^ bit) for i in range(32)])


def along_z(value, step, senders):
    moves = [(i, i + 2 * step) for i in range(32) if (i % 8) // 2 in senders]
    return lax.ppermute(value, BOTH, moves)


def pick(value, index, axis=0):
    return lax.dynamic_index_in_dim(value, index, axis, keepdims=False)


def add_low(left, right):
    return (left.astype(jnp.float32) + right.astype(jnp.float32)).astype(jnp.bfloat16)


def line_scatter(chunks):
    z = (lax.axis_index("img") // 2).astype(jnp.int32)
    up = down = None
    for step in range(1, 4):
        up_term = pick(chunks, jnp.clip(4 - step + z, 0, 3))
        down_term = pick(chunks, jnp.clip(z - 4 + step, 0, 3))
        if step > 1:
            up_term = add_low(up_term, up)
            down_term = add_low(down_term, down)
        up = along_z(up_term, 1, range(step))
        down = along_z(down_term, -1, range(4 - step, 4))
    own = pick(chunks, z)
    return own.astype(jnp.float32) + up.astype(jnp.float32) + down.astype(jnp.float32)


def line_gather(own):
    z = (lax.axis_index("img") // 2).astype(jnp.int32)
    up = down = own
    by_offset = {0: own}
    for step in range(1, 4):
        up = along_z(up, 1, range(step - 1, 3))
        down = along_z(down, -1, range(1, 5 - step))
        by_offset[-step] = up
        by_offset[step] = down
    rows = []
    for place in range(4):
        row = by_offset[place]
        for z_at in range(1, 4):
            row = jnp.where(z == z_at, by_offset[place - z_at], row)
        rows.append(row)
    return jnp.stack(rows)


def scatter_all(value):
    if not torus_block():
        return lax.psum_scatter(value, BOTH, scatter_dimension=0, tiled=True)[0].astype(jnp.float32)
    core = lax.axis_index("img") % 2
    x = lax.axis_index("grp") % 2
    y = lax.axis_index("grp") // 2
    value = value.reshape((2, 2, 4, 2) + value.shape[1:])
    value = add_low(pick(value, core, 3), swap(pick(value, 1 - core, 3), 1))
    first, second = value[:, :, :2], value[:, :, 2:]
    first_in = swap(pick(first, 1 - x, 1), 8)
    second_in = swap(pick(second, 1 - y, 0), 16)
    first = add_low(pick(first, x, 1), first_in)
    second = add_low(pick(second, y, 0), second_in)
    first_in = swap(pick(first, 1 - y), 16)
    second_in = swap(pick(second, 1 - x), 8)
    first = add_low(pick(first, y), first_in)
    second = add_low(pick(second, x), second_in)
    return line_scatter(jnp.concatenate([first, second]))


def scatter_shards(value):
    if not torus_block():
        return lax.psum_scatter(value, "img", scatter_dimension=0, tiled=True)[0].astype(jnp.float32)
    core = lax.axis_index("img") % 2
    value = value.reshape((4, 2) + value.shape[1:])
    value = add_low(pick(value, core, 1), swap(pick(value, 1 - core, 1), 1))
    return line_scatter(value)


def gather_shards(value):
    if not torus_block():
        return lax.all_gather(value, "img", axis=0, tiled=False)
    core = lax.axis_index("img") % 2
    line = line_gather(value)
    other = swap(line, 1)
    both = jnp.stack([jnp.where(core == 0, line, other), jnp.where(core == 0, other, line)], axis=1)
    return both.reshape((8,) + value.shape)


def lane_half(shape):
    return lax.broadcasted_iota(jnp.int32, shape, len(shape) - 1) % 128 < 64


def attention_forward_kernel(tokens, projected_ref, attended_ref, probs_ref):
    width = projected_ref.shape[1] // 3
    rows = projected_ref.shape[0]
    low_half = lane_half((rows, 128))
    real_key = lax.broadcasted_iota(jnp.int32, (rows, rows), 0) < tokens
    for pair in range(width // 128):
        at = pair * 128
        queries = projected_ref[:, at : at + 128] * jnp.bfloat16(0.125)
        key_rows = projected_ref[:, width + at : width + at + 128]
        values = projected_ref[:, 2 * width + at : 2 * width + at + 128]
        halves = []
        for half in range(2):
            chosen = low_half if half == 0 else ~low_half
            own_queries = jnp.where(chosen, queries, jnp.bfloat16(0))
            scores = lax.dot_general(
                key_rows, own_queries, (((1,), (1,)), ((), ())), preferred_element_type=jnp.float32
            )
            scores = jnp.where(real_key, scores, -1e30)
            raised = jnp.exp(scores - jnp.max(scores, axis=0, keepdims=True))
            probs = raised * (1.0 / jnp.sum(raised, axis=0, keepdims=True))
            probs = probs.astype(jnp.bfloat16)
            probs_ref[2 * pair + half] = probs
            halves.append(
                lax.dot_general(
                    probs, values, (((0,), (0,)), ((), ())), preferred_element_type=jnp.float32
                )
            )
        attended_ref[:, at : at + 128] = jnp.where(low_half, halves[0], halves[1]).astype(
            jnp.bfloat16
        )


def attention_forward(projected, images, tokens):
    rows = projected.shape[0] // images
    width = projected.shape[1] // 3
    heads = width // 64
    return pl.pallas_call(
        functools.partial(attention_forward_kernel, tokens),
        grid=(images,),
        in_specs=[pl.BlockSpec((rows, 3 * width), lambda i: (i, 0))],
        out_specs=[
            pl.BlockSpec((rows, width), lambda i: (i, 0)),
            pl.BlockSpec((None, heads, rows, rows), lambda i: (i, 0, 0, 0)),
        ],
        out_shape=[
            jax.ShapeDtypeStruct((images * rows, width), jnp.bfloat16),
            jax.ShapeDtypeStruct((images, heads, rows, rows), jnp.bfloat16),
        ],
        compiler_params=pltpu.CompilerParams(vmem_limit_bytes=24 << 20),
        cost_estimate=pl.CostEstimate(
            flops=images * heads * rows * rows * 64 * 4,
            bytes_accessed=images * rows * (8 * width + 2 * heads * rows),
            transcendentals=images * heads * rows * rows,
        ),
        name="attention_forward",
    )(projected)


def attention_backward_kernel(projected_ref, probs_ref, grad_ref, out_ref, sums_ref):
    width = projected_ref.shape[1] // 3
    rows = projected_ref.shape[0]
    low_half = lane_half((rows, 128))

    @pl.when(pl.program_id(0) == 0)
    def _():
        sums_ref[...] = jnp.zeros_like(sums_ref)

    for pair in range(width // 128):
        at = pair * 128
        queries = projected_ref[:, at : at + 128]
        key_rows = projected_ref[:, width + at : width + at + 128]
        values = projected_ref[:, 2 * width + at : 2 * width + at + 128]
        grads = grad_ref[:, at : at + 128]
        found = []
        for half in range(2):
            chosen = low_half if half == 0 else ~low_half
            probs = probs_ref[2 * pair + half]
            own_grads = jnp.where(chosen, grads, jnp.bfloat16(0))
            grad_values = jnp.dot(probs, grads, preferred_element_type=jnp.float32)
            grad_probs = lax.dot_general(
                values, own_grads, (((1,), (1,)), ((), ())), preferred_element_type=jnp.float32
            )
            wide = probs.astype(jnp.float32)
            weighted = grad_probs * wide
            total = jnp.sum(weighted, axis=0, keepdims=True)
            grad_scores = (weighted - wide * total).astype(jnp.bfloat16)
            grad_keys = jnp.dot(grad_scores, queries, preferred_element_type=jnp.float32) * 0.125
            grad_queries = (
                lax.dot_general(
                    grad_scores,
                    key_rows,
                    (((0,), (0,)), ((), ())),
                    preferred_element_type=jnp.float32,
                )
                * 0.125
            )
            found.append((grad_queries, grad_keys, grad_values))
        for kind in range(3):
            joined = jnp.where(low_half, found[0][kind], found[1][kind]).astype(jnp.bfloat16)
            place = slice(kind * width + at, kind * width + at + 128)
            out_ref[:, place] = joined
            sums_ref[:, place] += jnp.sum(
                joined.astype(jnp.float32).reshape(rows // 8, 8, 128), axis=0
            )


def attention_backward(projected, probs, grad_attended, images):
    rows = projected.shape[0] // images
    width = projected.shape[1] // 3
    heads = width // 64
    return pl.pallas_call(
        attention_backward_kernel,
        grid=(images,),
        in_specs=[
            pl.BlockSpec((rows, 3 * width), lambda i: (i, 0)),
            pl.BlockSpec((None, heads, rows, rows), lambda i: (i, 0, 0, 0)),
            pl.BlockSpec((rows, width), lambda i: (i, 0)),
        ],
        out_specs=[
            pl.BlockSpec((rows, 3 * width), lambda i: (i, 0)),
            pl.BlockSpec((8, 3 * width), lambda i: (0, 0)),
        ],
        out_shape=[
            jax.ShapeDtypeStruct((images * rows, 3 * width), jnp.bfloat16),
            jax.ShapeDtypeStruct((8, 3 * width), jnp.float32),
        ],
        compiler_params=pltpu.CompilerParams(vmem_limit_bytes=24 << 20),
        cost_estimate=pl.CostEstimate(
            flops=images * heads * rows * rows * 64 * 10,
            bytes_accessed=images * rows * (14 * width + 2 * heads * rows),
            transcendentals=0,
        ),
        name="attention_backward",
    )(projected, probs, grad_attended)


def ordered_gather(value, axis):
    total = lax.axis_size(axis)
    at = lax.axis_index(axis)
    slots = jnp.arange(total).reshape((total,) + (1,) * value.ndim)
    gathered = jnp.where(slots == at, value[None], jnp.zeros((), value.dtype))
    for shift in range(1, total):
        moved = lax.ppermute(value, axis, [(i, (i + shift) % total) for i in range(total)])
        gathered = jnp.where(slots == (at - shift) % total, moved[None], gathered)
    return gathered


def local(
    pixels,
    cotangent,
    band_count,
    wave_index,
    weight_tokens,
    bias_token,
    hyper_qkv,
    hyper_qv_bias,
    hyper_out,
    hyper_out_bias,
    hyper_norm1_gain,
    hyper_norm1_bias,
    hyper_ff1,
    hyper_ff1_bias,
    hyper_ff2,
    hyper_ff2_bias,
    hyper_norm2_gain,
    hyper_norm2_bias,
    kernel_gen,
    kernel_gen_bias,
    conv_bias_gen,
    conv_bias_gen_bias,
    norm1_gain,
    norm1_bias,
    qkv_weight,
    qv_bias,
    proj_weight,
    proj_bias,
    norm2_gain,
    norm2_bias,
    fc1_weight,
    fc1_bias,
    fc2_weight,
    fc2_bias,
):
    group_total = lax.axis_size("grp")
    shard_total = lax.axis_size("img")
    group_at = lax.axis_index("grp")
    shard_at = lax.axis_index("img")
    small_lengths = [
        member.shape[0]
        for member in (
            conv_bias_gen_bias,
            norm1_gain,
            norm1_bias,
            qv_bias,
            proj_bias,
            norm2_gain,
            norm2_bias,
            fc1_bias,
            fc2_bias,
        )
    ]
    small_flat = jnp.concatenate(
        [
            conv_bias_gen_bias,
            norm1_gain,
            norm1_bias,
            qv_bias,
            proj_bias,
            norm2_gain,
            norm2_bias,
            fc1_bias,
            fc2_bias,
        ]
    )
    hyper_wide = conv_bias_gen.shape[1]
    qkv_full = lax.all_gather(qkv_weight, "img", axis=0, tiled=True)
    proj_full = lax.all_gather(proj_weight, "img", axis=0, tiled=True)
    fc1_full = lax.all_gather(fc1_weight, "img", axis=0, tiled=True)
    fc2_full = lax.all_gather(fc2_weight, "img", axis=0, tiled=True)
    images = pixels.shape[0]
    slot_count = pixels.shape[1]
    tokens = pixels.shape[2]
    patch = pixels.shape[3]
    model_width = cotangent.shape[2]
    padded = -(-tokens // 16) * 16
    row_count = images * padded

    def pad_rows(value):
        return jnp.pad(value, ((0, 0), (0, padded - tokens), (0, 0))).reshape(row_count, -1)

    band_total = band_count[0]
    band_mask = (jnp.arange(slot_count) < band_total).astype(jnp.float32)
    hyper_params = (
        weight_tokens,
        bias_token,
        hyper_qkv,
        hyper_qv_bias,
        hyper_out,
        hyper_out_bias,
        hyper_norm1_gain,
        hyper_norm1_bias,
        hyper_ff1,
        hyper_ff1_bias,
        hyper_ff2,
        hyper_ff2_bias,
        hyper_norm2_gain,
        hyper_norm2_bias,
    )
    hidden, bias_row = hyper_forward(hyper_params, wave_index[0], band_total)
    table = jnp.concatenate([band_count, wave_index[0]])
    tables = ordered_gather(table, "grp")
    (hidden_all, bias_row_all), hyper_pull = jax.vjp(
        lambda params: jax.vmap(lambda indices, total: hyper_forward(params, indices, total))(
            tables[:, 1:], tables[:, 0]
        ),
        hyper_params,
    )
    hidden_low = hidden.astype(jnp.bfloat16)
    kernel_rows = (
        jnp.einsum("be,pde->bpd", hidden_low, kernel_gen, preferred_element_type=jnp.float32)
        + kernel_gen_bias.astype(jnp.float32)[None]
    )
    kernel_shard = (kernel_rows * band_mask[:, None, None]).astype(jnp.bfloat16)
    cb_rows = conv_bias_gen.shape[0]
    small_flat = jnp.concatenate([conv_bias_gen.reshape(-1), small_flat])
    small_rows = -(-small_flat.shape[0] // (8 * model_width)) * 8
    small_flat = jnp.pad(small_flat, (0, small_rows * model_width - small_flat.shape[0]))
    shard_patch = kernel_gen.shape[0]
    kernel_rows_here = slot_count * shard_patch
    gathered = gather_shards(
        jnp.concatenate(
            [
                kernel_shard.reshape(kernel_rows_here, model_width),
                small_flat.reshape(small_rows, model_width),
            ]
        )
    )
    patch_kernels = (
        gathered[:, :kernel_rows_here]
        .reshape(shard_total, slot_count, shard_patch, model_width)
        .transpose(1, 0, 2, 3)
        .reshape(slot_count * patch, model_width)
    )
    small_vectors = gathered[:, kernel_rows_here:].reshape(shard_total, small_rows * model_width)
    cb_weight = small_vectors[:, : cb_rows * hyper_wide].reshape(shard_total * cb_rows, hyper_wide)
    unpacked = []
    small_at = cb_rows * hyper_wide
    for length in small_lengths:
        unpacked.append(small_vectors[:, small_at : small_at + length].reshape(-1))
        small_at += length
    (
        cb_shift,
        gain_one,
        shift_one,
        qv_full,
        proj_shift,
        gain_two,
        shift_two,
        fc1_shift,
        fc2_shift,
    ) = unpacked
    conv_shift = jnp.dot(
        cb_weight.astype(jnp.float32), bias_row, precision=highest_precision
    ) + cb_shift.astype(jnp.float32)
    pixel_rows = pad_rows(pixels.transpose(0, 2, 1, 3).reshape(images, tokens, slot_count * patch))
    stream = jnp.dot(pixel_rows, patch_kernels, preferred_element_type=jnp.float32) + conv_shift
    normed_one, norm_one_pull = jax.vjp(
        lambda values, norm_gain, norm_shift: layer_norm(values, norm_gain, norm_shift, norm_eps),
        stream,
        gain_one.astype(jnp.float32),
        shift_one.astype(jnp.float32),
    )
    normed_low = normed_one.astype(jnp.bfloat16)
    full_bias = jnp.concatenate(
        [
            qv_full[:model_width].astype(jnp.float32),
            jnp.zeros((model_width,), jnp.float32),
            qv_full[model_width:].astype(jnp.float32),
        ]
    )
    projected = (
        jnp.dot(normed_low, qkv_full, preferred_element_type=jnp.float32) + full_bias
    ).astype(jnp.bfloat16)
    attended, attn_probs = attention_forward(projected, images, tokens)
    middle = (
        stream
        + jnp.dot(attended, proj_full, preferred_element_type=jnp.float32)
        + proj_shift.astype(jnp.float32)
    )
    normed_two, norm_two_pull = jax.vjp(
        lambda values, norm_gain, norm_shift: layer_norm(values, norm_gain, norm_shift, norm_eps),
        middle,
        gain_two.astype(jnp.float32),
        shift_two.astype(jnp.float32),
    )
    normed_two_low = normed_two.astype(jnp.bfloat16)
    gate_in = jnp.dot(
        normed_two_low, fc1_full, preferred_element_type=jnp.float32
    ) + fc1_shift.astype(jnp.float32)
    activated, gelu_pull = jax.vjp(gelu_exact, gate_in)
    activated_low = activated.astype(jnp.bfloat16)
    block_out = (
        middle
        + jnp.dot(activated_low, fc2_full, preferred_element_type=jnp.float32)
        + fc2_shift.astype(jnp.float32)
    )
    upstream_low = pad_rows(cotangent)
    upstream = upstream_low.astype(jnp.float32)
    grad_fc2_shift = jnp.sum(upstream_low.astype(jnp.float32), axis=0)
    grad_fc2 = jnp.einsum(
        "tf,td->fd", activated_low, upstream_low, preferred_element_type=jnp.float32
    )
    grad_activated = jnp.einsum(
        "td,fd->tf", upstream_low, fc2_full, preferred_element_type=jnp.float32
    )
    (grad_gate,) = gelu_pull(grad_activated)
    gate_low = grad_gate.astype(jnp.bfloat16)
    grad_fc1_shift = jnp.sum(gate_low.astype(jnp.float32), axis=0)
    grad_fc1 = jnp.einsum("td,tf->df", normed_two_low, gate_low, preferred_element_type=jnp.float32)
    fc1_low = grad_fc1.astype(jnp.bfloat16)
    early_blocks = [
        fc1_low[:, at : at + model_width].reshape(group_total * shard_total, -1, model_width)
        for at in range(0, fc1_low.shape[1], model_width)
    ] + [grad_fc2.astype(jnp.bfloat16).reshape(group_total * shard_total, -1, model_width)]
    gate_low, early_block = lax.optimization_barrier(
        (gate_low, jnp.concatenate(early_blocks, axis=1))
    )
    early_sum = lax.psum_scatter(early_block, BOTH, scatter_dimension=0, tiled=True)[0]
    grad_normed_two = jnp.einsum(
        "tf,df->td", gate_low, fc1_full, preferred_element_type=jnp.float32
    )
    grad_middle_part, grad_gain_two, grad_shift_two = norm_two_pull(grad_normed_two)
    grad_middle = upstream + grad_middle_part
    middle_low = grad_middle.astype(jnp.bfloat16)
    grad_proj_shift = jnp.sum(middle_low.astype(jnp.float32), axis=0)
    grad_proj = jnp.einsum("td,te->de", attended, middle_low, preferred_element_type=jnp.float32)
    grad_attended = jnp.einsum(
        "te,de->td", middle_low, proj_full, preferred_element_type=jnp.float32
    ).astype(jnp.bfloat16)
    grad_projected, projected_sums = attention_backward(
        projected, attn_probs, grad_attended, images
    )
    projected_sums = jnp.sum(projected_sums, axis=0)
    grad_qv = jnp.concatenate([projected_sums[:model_width], projected_sums[2 * model_width :]])
    grad_qkv = jnp.einsum(
        "td,te->de", normed_low, grad_projected, preferred_element_type=jnp.float32
    )
    grad_normed_one = jnp.einsum(
        "te,de->td", grad_projected, qkv_full, preferred_element_type=jnp.float32
    )
    grad_stream_part, grad_gain_one, grad_shift_one = norm_one_pull(grad_normed_one)
    residual_reduced = (grad_middle + grad_stream_part).astype(jnp.bfloat16)
    grad_conv_shift = jnp.sum(residual_reduced.astype(jnp.float32), axis=0)
    grad_kernels = jnp.einsum(
        "tk,td->kd", pixel_rows, residual_reduced, preferred_element_type=jnp.float32
    ).astype(jnp.bfloat16)
    grad_pixels = jnp.einsum(
        "td,kd->tk", residual_reduced, patch_kernels, preferred_element_type=jnp.float32
    )
    grad_pixels = (
        grad_pixels.reshape(images, padded, slot_count, patch)[:, :tokens].transpose(0, 2, 1, 3)
    )
    grad_bias_row_part = jnp.dot(
        grad_conv_shift, cb_weight.astype(jnp.float32), precision=highest_precision
    )
    group_kernels = scatter_shards(
        grad_kernels.reshape(slot_count, shard_total, shard_patch, model_width).transpose(1, 0, 2, 3)
    )
    grad_pre = group_kernels * band_mask[:, None, None]
    grad_hidden_part = jnp.einsum(
        "bpd,pde->be", grad_pre, kernel_gen.astype(jnp.float32), precision=highest_precision
    )
    code_grads = jnp.concatenate([grad_hidden_part, grad_bias_row_part[None]])
    code_grads = jnp.sum(ordered_gather(code_grads, "img"), axis=0)
    code_grads = ordered_gather(code_grads, "grp")
    (hyper_total,) = hyper_pull((code_grads[:, :slot_count], code_grads[:, slot_count]))
    group_width = model_width // group_total
    swapped = lax.all_to_all(
        grad_pre.reshape(slot_count, shard_patch, group_total, group_width).transpose(2, 0, 1, 3),
        "grp",
        0,
        0,
    ).reshape(group_total * slot_count, shard_patch, group_width)
    code_all = hidden_all.astype(jnp.bfloat16).astype(jnp.float32)
    grad_gen = jnp.einsum(
        "kpd,ke->pde",
        swapped,
        code_all.reshape(group_total * slot_count, hyper_wide),
        precision=highest_precision,
    )
    grad_gen_shift = jnp.sum(swapped, axis=0)
    device_total = group_total * shard_total
    own_group = (jnp.arange(group_total) == group_at).astype(jnp.float32)
    vectors = [
        grad_gain_one,
        grad_shift_one,
        grad_qv,
        grad_proj_shift,
        grad_gain_two,
        grad_shift_two,
        grad_fc1_shift,
        grad_fc2_shift,
    ] + [grad_conv_shift * own_group[group] for group in range(group_total)]
    vector_block = jnp.concatenate(
        [member.reshape(device_total, -1) for member in vectors], axis=1
    ).astype(jnp.bfloat16)
    vector_lengths = [member.shape[0] // device_total for member in vectors]
    block_rows = model_width // device_total

    def blocks_of(value):
        value = value.astype(jnp.bfloat16)
        return [
            value[:, at : at + model_width].reshape(device_total, -1, model_width)
            for at in range(0, value.shape[1], model_width)
        ]

    late = blocks_of(grad_qkv) + blocks_of(grad_proj)
    late_rows = sum(member.shape[1] for member in late)
    extra = -(-vector_block.shape[1] // model_width)
    extra += -(late_rows + extra) % 8
    vector_block = jnp.pad(
        vector_block, ((0, 0), (0, extra * model_width - vector_block.shape[1]))
    ).reshape(device_total, extra, model_width)
    late_out = scatter_all(jnp.concatenate(late + [vector_block], axis=1))
    early_out = early_sum.astype(jnp.float32)

    def columns_of(value, total):
        return jnp.concatenate(
            [value[at * block_rows : (at + 1) * block_rows] for at in range(total)], axis=1
        )

    fc1_out = columns_of(early_out, grad_fc1.shape[1] // model_width)
    fc2_out = early_out[fc1_out.size // model_width :]
    qkv_out = columns_of(late_out, 3)
    proj_out = late_out[3 * block_rows : 4 * block_rows]
    vector_out = late_out[4 * block_rows :].reshape(-1)
    parts = []
    vector_at = 0
    for length in vector_lengths:
        parts.append(vector_out[vector_at : vector_at + length])
        vector_at += length
    conv_parts = jnp.stack(parts[8:])
    grad_cb_weight = jnp.dot(conv_parts.T, bias_row_all, precision=highest_precision)
    reduced = (
        grad_cb_weight,
        jnp.sum(conv_parts, axis=0),
        parts[0],
        parts[1],
        qkv_out,
        parts[2],
        proj_out,
        parts[3],
        parts[4],
        parts[5],
        fc1_out,
        parts[6],
        fc2_out,
        parts[7],
    )
    return (
        block_out.reshape(images, padded, model_width)[:, :tokens],
        grad_pixels,
        hyper_total[0],
        hyper_total[1],
        hyper_total[2],
        hyper_total[3],
        hyper_total[4],
        hyper_total[5],
        hyper_total[6],
        hyper_total[7],
        hyper_total[8],
        hyper_total[9],
        hyper_total[10],
        hyper_total[11],
        hyper_total[12],
        hyper_total[13],
        grad_gen,
        grad_gen_shift,
        reduced[0],
        reduced[1],
        reduced[2],
        reduced[3],
        reduced[4],
        reduced[5],
        reduced[6],
        reduced[7],
        reduced[8],
        reduced[9],
        reduced[10],
        reduced[11],
        reduced[12],
        reduced[13],
    )


def solution(mesh):
    return jax.shard_map(
        local,
        mesh=mesh,
        in_specs=(
            P(("grp", "img"), None, None, None),
            P(("grp", "img"), None, None),
            P("grp"),
            P("grp", None),
            P(),
            P(),
            P(),
            P(),
            P(),
            P(),
            P(),
            P(),
            P(),
            P(),
            P(),
            P(),
            P(),
            P(),
            P("img", None, None),
            P("img", None),
            P("img", None),
            P("img"),
            P("img"),
            P("img"),
            P("img", None),
            P("img"),
            P("img", None),
            P("img"),
            P("img"),
            P("img"),
            P("img", None),
            P("img"),
            P("img", None),
            P("img"),
        ),
        out_specs=(
            P(("grp", "img"), None, None),
            P(("grp", "img"), None, None, None),
            P(),
            P(),
            P(),
            P(),
            P(),
            P(),
            P(),
            P(),
            P(),
            P(),
            P(),
            P(),
            P(),
            P(),
            P("img", "grp", None),
            P("img", "grp"),
            P(("grp", "img"), None),
            P(("grp", "img")),
            P(("grp", "img")),
            P(("grp", "img")),
            P(("grp", "img"), None),
            P(("grp", "img")),
            P(("grp", "img"), None),
            P(("grp", "img")),
            P(("grp", "img")),
            P(("grp", "img")),
            P(("grp", "img"), None),
            P(("grp", "img")),
            P(("grp", "img"), None),
            P(("grp", "img")),
        ),
        check_vma=False,
    )
```

time: 1660 us -> 518 us (0.31)
  waiting for transfers between devices: 1080 us -> 88.3 us
  blocking collectives: 173 us -> 0 us
  starting transfers between devices: 1.32 us -> 75.9 us
  matrix products: 213 us -> 162 us
  local copies, waits for them, and re-layouts: 115 us -> 81.6 us
  Pallas kernels: 0 us -> 22.5 us
    reduce_scatter x6 -> x1, waiting for transfers between devices: 636 us -> 0.01 us  [local(): lax.psum_scatter(early_block, BOTH, scatter_dimension=0, tiled=True)[0]]
    all_gather x5 -> x4, waiting for transfers between devices: 343 us -> 16.1 us  [the longest x1 16.1 us: local(): fc2_full = lax.all_gather(fc2_weight, 'img', axis=0, tiled=True)]
    unnamed x17 -> x5, waiting for transfers between devices: 100 us -> 2.09 us
    all_gather x3 -> x0, blocking collectives: 87.7 us -> none  [the longest x1 34.8 us: local(): lax.all_gather(kernel_gen_bias, 'img', axis=0, tiled=True)]
    ppermute x0 -> x38, starting transfers between devices: none -> 71.1 us  [the longest x18 47.1 us: along_z(): return lax.ppermute(value, BOTH, moves)]
    unnamed x2 -> x0, blocking collectives: 70.6 us -> none
    ppermute x0 -> x38, waiting for transfers between devices: none -> 70.1 us  [the longest x18 56.3 us: along_z(): return lax.ppermute(value, BOTH, moves)]
    dot_general x11 -> x6, matrix products: 77.2 us -> 23.5 us  [the longest x1 5.95 us: local(): jnp.dot(pixel_rows, patch_kernels, preferred_element_type=jnp.float32)]
  transfers between devices with their start and end apart: 15 -> 44, of which waited for: 11 -> 8; matrix products, arithmetic and copies ran while one was open for 15% -> 36% of each run, Pallas kernels for 0% -> 1%
where the time goes in v1:
time: 518 us; the launch traced here: 508 us
  matrix products  162 us (31%)
  waiting for transfers between devices  88.3 us (17%)
  local copies, waits for them, and re-layouts  81.6 us (16%)
  starting transfers between devices  75.9 us (15%)
  other arithmetic  60.3 us (12%)
  Pallas kernels  22.5 us (4%)
  between operations  17.8 us (3%)
    ppermute x18, waiting for transfers between devices, along_z(): return lax.ppermute(value, BOTH, moves)  56.3 us
    ppermute x18, starting transfers between devices, along_z(): return lax.ppermute(value, BOTH, moves)  47.1 us
    unnamed x320, local copies, waits for them, and re-layouts  32.6 us
    dot_general x1, matrix products, local(): jnp.einsum('td,fd->tf', upstream_low, fc2_full, preferred_element_type=jn...  31.5 us
    ppermute x13, starting transfers between devices, ordered_gather(): lax.ppermute(value, axis, [(i, (i + shift) % total) for i in range(total)])  20.3 us
    all_gather x1, waiting for transfers between devices, local(): fc2_full = lax.all_gather(fc2_weight, 'img', axis=0, tiled=True)  16.1 us
    pallas_call x1, Pallas kernels, attention_backward(): pl.pallas_call(attention_backward_kernel, grid=(images,), in_specs=[pl.Bl...  15.3 us
    convert_element_type x1, other arithmetic, local(): activated_low = activated.astype(jnp.bfloat16)  11.7 us
  transfers between devices with their start and end apart: 44, of which 8 were waited for; matrix products, arithmetic and copies ran while one was open for 36% of the time, Pallas kernels for 1%

profile of v1, /device:TPU:0, one launch (start us, length us, event | category | flops | bytes accessed | tf_op | source)
XLA Modules:
  0.0 508.2 jit_solution(10628815163998319551)
XLA Ops:
  9.6 6.9 %concatenate.75 = bf16[13536]{0:T(1024)(128)(2,1)S(1)} concatenate(bf16[12288]{0:T(1024)(128)(2,1)} %bitcast.376, bf16[96]{0:T(256)(128)(2,1)} %param.55, bf16[96]{0:T(256)(128)(2,1)} %param.56, bf16[96]{0:T(256)(128)(2,1)} %param.57, bf16[192]{0:T(256)(128)(2,1)} %param.59, bf16[96]{0:T(256)(128)(2,1)} %param.61, bf16[96]{0:T(256)(128)(2,1)} %param.62, bf16[96]{0:T(256)(128)(2,1)} %param.63, ...), dimensions={0} | concatenate | bytes 54144 | tf_op jit(solution)/shard_map/concatenate | solution.py:469
  27.9 4.6 fusion.12
  34.1 5.7 %collective-permute-start = (bf16[280,768]{1,0:T(8,128)(2,1)}, bf16[280,768]{1,0:T(8,128)(2,1)}, u32[]{:S(2)}, u32[]{:S(2)}) collective-permute-start(bf16[280,768]{1,0:T(8,128)(2,1)} %pad_maximum_fusion.2), channel_id=1, source_target_pairs={{0,2},{1,3},{2,4},{3,5},{4,6},{5,7},{8,10},{9,11},{10,12},{11,13},... | collective-permute-start | bytes 1290248 | tf_op jit(solution)/shard_map/ppermute | solution.py:118
  48.8 4.9 reshape.769
  53.7 4.1 pad.40
  70.9 20.2 %collective-permute-done.4 = bf16[280,768]{1,0:T(8,128)(2,1)} collective-permute-done((bf16[280,768]{1,0:T(8,128)(2,1)}, bf16[280,768]{1,0:T(8,128)(2,1)}, u32[]{:S(2)}, u32[]{:S(2)}) %collective-permute-start.4) | collective-permute-done | bytes 430112 | tf_op jit(solution)/shard_map/ppermute | solution.py:118
  92.8 26.0 %collective-permute-done.5 = bf16[280,768]{1,0:T(8,128)(2,1)S(1)} collective-permute-done((bf16[280,768]{1,0:T(8,128)(2,1)}, bf16[280,768]{1,0:T(8,128)(2,1)S(1)}, u32[]{:S(2)}, u32[]{:S(2)}) %collective-permute-start.5) | collective-permute-done | bytes 430112 | tf_op jit(solution)/shard_map/ppermute | solution.py:118
  118.9 1.9 select_bitcast_fusion.5
  126.8 1.9 slice.310
  129.3 4.0 copy.212
  134.6 5.9 %add_reduce_fusion = (f32[832]{0:T(1024)S(1)}, f32[832,768]{1,0:T(8,128)S(1)}) fusion(f32[768]{0:T(1024)S(1)} %add.526, bf16[832,2048]{1,0:T(8,128)(2,1)} %bitcast.350, bf16[2048,768]{1,0:T(8,128)(2,1)} %bitcast.353), kind=kOutput, calls=%fused_computation.48 | convolution fusion | flops 2618522880 | bytes 9115904 | tf_op jit(solution)/shard_map/dot_general | solution.py:510
  143.2 6.2 %add_convert_fusion.1.projected_ref = bf16[832,2304]{1,0:T(8,128)(2,1)S(1)} fusion(bf16[768,2304]{1,0:T(8,128)(2,1)} %all-gather.5.cloned.1.call-done, f32[2304]{0:T(1024)S(1)} %pad_maximum_fusion.16, f32[832,768]{1,0:T(8,128)} %copy-done.11, f32[768]{0:T(1024)S(1)} %reshape.811, f32[768]{0:T(1024)S(1)} %reshape.810, f32[832]{0:T(1024)S(1)} %fusion.214, ...), kind=kOutput, calls=%fused_computation.17 | convolution fusion | flops 2952069120 | bytes 9953792 | tf_op jit(solution)/shard_map/dot_general | solution.py:526
  149.4 7.2 %attention_forward.1 = (bf16[832,768]{1,0:T(8,128)(2,1)S(1)}, bf16[4,12,208,208]{3,2,1,0:T(8,128)(2,1)S(1)}) custom-call(bf16[832,2304]{1,0:T(8,128)(2,1)S(1)} %add_convert_fusion.1.projected_ref), custom_call_target="tpu_custom_call" | custom-call | flops 531628032 | bytes 9265152 | tf_op jit(solution)/shard_map/attention_forward/pallas_call | solution.py:241
  156.6 2.3 copy-done.1
  158.9 1.8 copy-done.2
  160.7 3.9 fusion.295
  166.7 11.5 %fusion.275 = f32[832,3072]{1,0:T(8,128)} fusion(bf16[768,3072]{1,0:T(8,128)(2,1)} %all-gather.9.cloned.1.call-done, f32[832,768]{1,0:T(8,128)} %copy-done.9, f32[768]{0:T(1024)S(1)} %reshape.816, f32[768]{0:T(1024)S(1)} %reshape.815, f32[832]{0:T(1024)S(1)} %fusion.215, f32[832]{0:T(1024)S(1)} %broadcast_multiply_fusion), kind=kOutput, calls=%fused_computation.527 | convolution fusion | flops 3929063424 | bytes 17510912 | tf_op jit(solution)/shard_map/dot_general | solution.py:541
  178.2 16.1 %all-gather.11.cloned.1.call-done = bf16[3072,768]{1,0:T(8,128)(2,1)} async-done(((bf16[384,768]{1,0:T(8,128)(2,1)}), bf16[3072,768]{1,0:T(8,128)(2,1)}) %all-gather.11.cloned.1.call-update) | async-done | bytes 4718608 | tf_op jit(solution)/shard_map/all_gather | solution.py:423
  194.3 31.5 %fusion.276 = (bf16[3072]{0:T(1024)(128)(2,1)S(1)}, bf16[832,3072]{1,0:T(8,128)(2,1)}, f32[832,3072]{1,0:T(8,128)}) fusion(f32[832,3072]{1,0:T(8,128)} %fusion.275, f32[3072]{0:T(1024)S(1)} %reshape.817, bf16[832,768]{1,0:T(8,128)(2,1)S(1)} %bitcast.332, bf16[3072,768]{1,0:T(8,128)(2,1)} %all-gather.11.cloned.1.call-done), kind=kOutput, calls=%fused_computation.528 | convolution fusion | flops 4115002368 | bytes 31574016 | tf_op jit(solution)/shard_map/td,fd->tf/dot_general | solution.py:557
  225.8 11.7 %multiply_convert_fusion = bf16[832,3072]{1,0:T(8,128)(2,1)} fusion(f32[832,3072]{1,0:T(8,128)} %get-tuple-element.220, f32[832,3072]{1,0:T(8,128)} %fusion.275, f32[3072]{0:T(1024)S(1)} %reshape.817), kind=kLoop, calls=%fused_computation.3 | loop fusion | flops 10223616 | bytes 25571328 | tf_op jit(solution)/shard_map/convert_element_type | solution.py:545
  237.5 8.7 %convolution_convert_fusion.2 = bf16[768,3072]{1,0:T(8,128)(2,1)S(1)} fusion(bf16[832,3072]{1,0:T(8,128)(2,1)} %get-tuple-element.39, f32[832,768]{1,0:T(8,128)} %copy-done.9, f32[768]{0:T(1024)S(1)} %reshape.816, f32[768]{0:T(1024)S(1)} %reshape.815, f32[832]{0:T(1024)S(1)} %fusion.215, f32[832]{0:T(1024)S(1)} %broadcast_multiply_fusion), kind=kOutput, calls=%fused_computation.22 | convolution fusion | flops 3931422720 | bytes 12399104 | tf_op jit(solution)/shard_map/td,tf->df/dot_general | solution.py:563
  249.1 5.5 %convolution_convert_fusion.1 = bf16[3072,768]{1,0:T(8,128)(2,1)S(1)} fusion(bf16[832,3072]{1,0:T(8,128)(2,1)S(1)} %copy-done.20, bf16[832,768]{1,0:T(8,128)(2,1)S(1)} %bitcast.333), kind=kOutput, calls=%fused_computation.21 | convolution fusion | flops 3928227840 | bytes 11108352 | tf_op jit(solution)/shard_map/tf,td->fd/dot_general | solution.py:554
  258.0 2.4 constant_dynamic-update-slice_fusion
  260.4 9.4 %multiply_reduce_fusion = (bf16[768]{0:T(1024)(128)(2,1)S(1)}, f32[832]{0:T(1024)S(1)}, bf16[768]{0:T(1024)(128)(2,1)S(1)}, f32[832,768]{1,0:T(8,128)S(1)}) fusion(f32[832,768]{1,0:T(8,128)} %copy-done.9, f32[832]{0:T(1024)S(1)} %fusion.215, f32[832]{0:T(1024)S(1)} %broadcast_multiply_fusion, f32[768]{0:T(1024)S(1)} %reshape.815, ...), kind=kOutput, calls=%fused_computation.31 | convolution fusion | flops 3930978048 | bytes 14958336 | tf_op jit(solution)/shard_map/tf,df->td/dot_general | solution.py:573
  274.9 15.3 %attention_backward.1 = (bf16[832,2304]{1,0:T(8,128)(2,1)S(1)}, f32[8,2304]{1,0:T(8,128)S(1)}) custom-call(bf16[832,2304]{1,0:T(8,128)(2,1)S(1)} %copy-done.3, bf16[4,12,208,208]{3,2,1,0:T(8,128)(2,1)S(1)} %bitcast.326, bf16[832,768]{1,0:T(8,128)(2,1)S(1)} %convolution_convert_fusion.4.grad_ref), custom_call_target="tpu_custom_call" | custom-call | flops 1329070080 | bytes 13099008 | tf_op jit(solution)/shard_map/attention_backward/pallas_call | solution.py:315
  290.4 6.0 %convolution_convert_fusion = bf16[768,2304]{1,0:T(8,128)(2,1)} fusion(bf16[832,2304]{1,0:T(8,128)(2,1)S(1)} %get-tuple-element.41, f32[832,768]{1,0:T(8,128)S(1)} %copy-done.12, f32[768]{0:T(1024)S(1)} %copy-done.122, f32[768]{0:T(1024)S(1)} %copy-done.101, f32[832]{0:T(1024)S(1)} %copy-done.103, f32[832]{0:T(1024)S(1)} %copy-done.81, f32[768]{0:T(1024)S(1)} %copy-done.79), kind=kOutput, calls=%fused_computation.20 | convolution fusion | flops 2950004736 | bytes 9944576 | tf_op jit(solution)/shard_map/td,te->de/dot_general | solution.py:589
  296.4 3.7 multiply_reduce_fusion.1
  303.7 3.8 convolution_convert_fusion.3
  309.2 2.0 copy.291
  312.3 2.5 multiply_convert_fusion.1
  315.5 2.2 fusion.285
  321.9 2.4 fusion.7
  324.4 2.6 collective-permute-start.8
  327.2 1.9 dynamic-slice_bitcast_fusion
  331.0 4.1 collective-permute-done.8
  336.2 5.0 collective-permute-start.9
  341.2 9.3 %add_add_fusion.3 = f32[832,768]{1,0:T(8,128)S(1)} fusion(f32[832,768]{1,0:T(8,128)} %copy-done.9, bf16[832,3072]{1,0:T(8,128)(2,1)} %multiply_convert_fusion, bf16[3072,768]{1,0:T(8,128)(2,1)} %all-gather.11.cloned.1.call-done, f32[768]{0:T(1024)S(1)} %copy-done.120), kind=kOutput, calls=%fused_computation.38 | convolution fusion | flops 3927146496 | bytes 14945280 | tf_op jit(solution)/shard_map/dot_general | solution.py:548
  351.5 2.7 convolution_bitcast_fusion
  354.2 3.5 collective-permute-start.10
  359.6 2.4 copy.261
  361.9 4.7 copy.244
  366.7 2.5 fusion.6
  369.2 2.8 collective-permute-done.13
  372.3 2.6 convolution_bitcast_fusion.11
  375.0 3.2 collective-permute-start.19
  378.5 2.1 collective-permute-start.18
  383.0 2.3 collective-permute-start.15
  391.3 2.4 collective-permute-start.21
  396.9 2.5 copy.292
  399.4 4.6 all-to-all-start
  404.1 2.2 collective-permute-done.23
  410.6 2.0 fusion.300
  412.8 2.7 multiply_reduce_fusion.8
  421.2 1.8 fusion.64
  424.8 2.1 bitcast_reduce_fusion
  443.9 11.6 %collective-permute-done.29 = bf16[2,104,768]{2,1,0:T(8,128)(2,1)S(1)} collective-permute-done((bf16[2,104,768]{2,1,0:T(8,128)(2,1)S(1)}, bf16[2,104,768]{2,1,0:T(8,128)(2,1)S(1)}, u32[]{:S(2)}, u32[]{:S(2)}) %collective-permute-start.29) | collective-permute-done | bytes 319520 | tf_op jit(solution)/shard_map/ppermute | solution.py:113
  455.9 3.1 collective-permute-start.32
  460.2 2.1 convolution_bitcast_fusion.2
  462.3 3.1 collective-permute-done.32
  465.6 4.4 collective-permute-start.33
  470.9 2.8 convolution_bitcast_fusion.1
  473.8 2.0 reduce_sum.483
  477.2 11.8 %collective-permute-start.34 = (bf16[104,768]{1,0:T(8,128)(2,1)S(1)}, bf16[104,768]{1,0:T(8,128)(2,1)S(1)}, u32[]{:S(2)}, u32[]{:S(2)}) collective-permute-start(bf16[104,768]{1,0:T(8,128)(2,1)S(1)} %get-tuple-element.252), channel_id=1, source_target_pairs={{0,2},{1,3},{2,4},{3,5},{4,6},{5,7},{8,10},{9,11},{10,12},{11,13},... | collective-permute-start | bytes 479240 | tf_op jit(solution)/shard_map/ppermute | solution.py:118
  489.0 5.6 %convolution_bitcast_fusion.3 = f32[32,192,128]{2,1,0:T(8,128)} fusion(f32[4,8,32,192]{3,1,2,0:T(8,128)} %all-to-all-done, f32[4,8,64]{2,1,0:T(8,128)S(1)} %copy-done.52, f32[4,8,64]{2,1,0:T(8,128)S(1)} %copy-done.50, f32[4,9,128]{2,1,0:T(8,128)S(1)} %copy-done.77), kind=kOutput, calls=%fused_computation.50 | convolution fusion | flops 302002176 | bytes 3981312 | tf_op jit(solution)/shard_map/kpd,ke->pde/dot_general | solution.py:629
  (596 shorter events, 129.6 us)
Async XLA Ops:
  7.3 18.6 %copy-start.141 = (f32[128]{0:T(128)S(1)}, f32[128]{0:T(128)}, u32[]{:S(2)}) copy-start(f32[128]{0:T(128)} %param.49) | copy-start | bytes 1540
  7.3 18.6 %copy-start.27 = (f32[2048,128]{1,0:T(8,128)S(1)}, f32[2048,128]{1,0:T(8,128)}, u32[]{:S(2)}) copy-start(f32[2048,128]{1,0:T(8,128)} %param.48) | copy-start | bytes 3145732
  7.3 135.3 %all-gather.5.cloned.1.call-start = ((), (), s32[]{:S(2)}) async-start(), calls=%async_computation.2 | async-start | bytes 3981312 | tf_op jit(solution)/shard_map/all_gather | solution.py:420
  8.1 152.7 %all-gather.7.cloned.1.call-start = ((), (), s32[]{:S(2)}) async-start(), calls=%async_computation.3 | async-start | bytes 1327104 | tf_op jit(solution)/shard_map/all_gather | solution.py:421
  8.8 157.9 %all-gather.9.cloned.1.call-start = ((), (), s32[]{:S(2)}) async-start(), calls=%async_computation.4 | async-start | bytes 5308416 | tf_op jit(solution)/shard_map/all_gather | solution.py:422
  9.5 184.7 %all-gather.11.cloned.1.call-start = ((), (), s32[]{:S(2)}) async-start(), calls=%async_computation.5 | async-start | bytes 5308416 | tf_op jit(solution)/shard_map/all_gather | solution.py:423
  34.1 32.3 %collective-permute-start = (bf16[280,768]{1,0:T(8,128)(2,1)}, bf16[280,768]{1,0:T(8,128)(2,1)}, u32[]{:S(2)}, u32[]{:S(2)}) collective-permute-start(bf16[280,768]{1,0:T(8,128)(2,1)} %pad_maximum_fusion.2), channel_id=1, source_target_pairs={{0,2},{1,3},{2,4},{3,5},{4,6},{5,7},{8,10},{9,11},{10,12},{11,13},... | collective-permute-start | bytes 1290248 | tf_op jit(solution)/shard_map/ppermute | solution.py:118
  39.8 27.2 %collective-permute-start.3 = (bf16[280,768]{1,0:T(8,128)(2,1)}, bf16[280,768]{1,0:T(8,128)(2,1)}, u32[]{:S(2)}, u32[]{:S(2)}) collective-permute-start(bf16[280,768]{1,0:T(8,128)(2,1)} %pad_maximum_fusion.2), channel_id=1, source_target_pairs={{2,0},{3,1},{4,2},{5,3},{6,4},{7,5},{10,8},{11,9},{12,10},{13,11},... | collective-permute-start | bytes 1290248 | tf_op jit(solution)/shard_map/ppermute | solution.py:118
  41.7 20.9 %collective-permute-start.26 = (s32[9]{0:T(128)}, s32[9]{0:T(128)}, u32[]{:S(2)}, u32[]{:S(2)}) collective-permute-start(s32[9]{0:T(128)} %pad_add_fusion.2), channel_id=1, source_target_pairs={{0,8},{8,16},{16,24},{24,0},{1,9},{9,17},{17,25},{25,1},{2,10},{10... | collective-permute-start | bytes 116 | tf_op jit(solution)/shard_map/ppermute | solution.py:347
  43.2 19.4 %collective-permute-start.25 = (s32[9]{0:T(128)}, s32[9]{0:T(128)}, u32[]{:S(2)}, u32[]{:S(2)}) collective-permute-start(s32[9]{0:T(128)} %pad_add_fusion.2), channel_id=1, source_target_pairs={{0,16},{8,24},{16,0},{24,8},{1,17},{9,25},{17,1},{25,9},{2,18},{10... | collective-permute-start | bytes 116 | tf_op jit(solution)/shard_map/ppermute | solution.py:347
  44.7 17.9 %collective-permute-start.24 = (s32[9]{0:T(128)}, s32[9]{0:T(128)}, u32[]{:S(2)}, u32[]{:S(2)}) collective-permute-start(s32[9]{0:T(128)} %pad_add_fusion.2), channel_id=1, source_target_pairs={{0,24},{8,0},{16,8},{24,16},{1,25},{9,1},{17,9},{25,17},{2,26},{10... | collective-permute-start | bytes 116 | tf_op jit(solution)/shard_map/ppermute | solution.py:347
  46.2 452.5 %reduce-scatter.2.cloned.1.call-start = ((), (), s32[]{:S(2)}) async-start(), calls=%async_computation.6 | async-start | bytes 9732096 | tf_op jit(solution)/shard_map/reduce_scatter | solution.py:572
  64.0 54.8 %copy-start.31 = (bf16[8,32,768]{2,1,0:T(8,128)(2,1)S(1)}, bf16[8,32,768]{2,1,0:T(8,128)(2,1)}, u32[]{:S(2)}) copy-start(bf16[8,32,768]{2,1,0:T(8,128)(2,1)} %copy-done.30) | copy-start | bytes 1179652
  64.0 54.8 %copy-start.61 = (bf16[24,768]{1,0:T(8,128)(2,1)S(1)}, bf16[24,768]{1,0:T(8,128)(2,1)}, u32[]{:S(2)}) copy-start(bf16[24,768]{1,0:T(8,128)(2,1)} %reshape.777) | copy-start | bytes 110596
  64.8 56.0 %copy-start.36 = (f32[4,137,128]{1,2,0:T(8,128)}, f32[4,137,128]{1,2,0:T(8,128)S(1)}, u32[]{:S(2)}) copy-start(f32[4,137,128]{1,2,0:T(8,128)S(1)} %fusion.47) | copy-start | bytes 841732
  65.4 55.4 %copy-start.56 = (f32[4,9,4,32]{3,2,1,0:T(4,128)}, f32[4,9,4,32]{3,2,1,0:T(4,128)S(1)}, u32[]{:S(2)}) copy-start(f32[4,9,4,32]{3,2,1,0:T(4,128)S(1)} %reshape.857) | copy-start | bytes 55300
  65.6 55.2 %copy-start.38 = (f32[4,137,128]{1,2,0:T(8,128)}, f32[4,137,128]{1,2,0:T(8,128)S(1)}, u32[]{:S(2)}) copy-start(f32[4,137,128]{1,2,0:T(8,128)S(1)} %copy.220) | copy-start | bytes 841732
  66.1 54.7 %copy-start.69 = (f32[4,4,9]{2,1,0:T(4,128)}, f32[4,4,9]{2,1,0:T(4,128)S(1)}, u32[]{:S(2)}) copy-start(f32[4,4,9]{2,1,0:T(4,128)S(1)} %get-tuple-element.315) | copy-start | bytes 1732
  66.4 58.8 %copy-start.90 = (f32[4,4,9]{2,1,0:T(4,128)}, f32[4,4,9]{2,1,0:T(4,128)S(1)}, u32[]{:S(2)}) copy-start(f32[4,4,9]{2,1,0:T(4,128)S(1)} %fusion.49) | copy-start | bytes 1732
  66.4 3.8 collective-permute-start.1
  67.1 24.0 %collective-permute-start.4 = (bf16[280,768]{1,0:T(8,128)(2,1)}, bf16[280,768]{1,0:T(8,128)(2,1)}, u32[]{:S(2)}, u32[]{:S(2)}) collective-permute-start(bf16[280,768]{1,0:T(8,128)(2,1)} %collective-permute-done.3), channel_id=1, source_target_pairs={{2,0},{3,1},{4,2},{5,3},{10,8},{11,9},{12,10},{13,11},{18,16},{19,... | collective-permute-start | bytes 1290248 | tf_op jit(solution)/shard_map/ppermute | solution.py:118
  69.2 51.9 %copy-start.62 = (f32[4,9,128]{2,1,0:T(8,128)}, f32[4,9,128]{2,1,0:T(8,128)S(1)}, u32[]{:S(2)}) copy-start(f32[4,9,128]{2,1,0:T(8,128)S(1)} %reshape.858) | copy-start | bytes 55300
  70.2 53.3 %copy-start.43 = (f32[4,9,128]{2,1,0:T(8,128)}, f32[4,9,128]{2,1,0:T(8,128)S(1)}, u32[]{:S(2)}) copy-start(f32[4,9,128]{2,1,0:T(8,128)S(1)} %get-tuple-element.318) | copy-start | bytes 55300
  70.2 22.6 %collective-permute-start.2 = (bf16[280,768]{1,0:T(8,128)(2,1)S(1)}, bf16[280,768]{1,0:T(8,128)(2,1)S(1)}, u32[]{:S(2)}, u32[]{:S(2)}) collective-permute-start(bf16[280,768]{1,0:T(8,128)(2,1)S(1)} %collective-permute-done.1), channel_id=1, source_target_pairs={{4,6},{5,7},{12,14},{13,15},{20,22},{21,23},{28,30},{29,31}} | collective-permute-start | bytes 1290248 | tf_op jit(solution)/shard_map/ppermute | solution.py:118
  91.1 27.8 %collective-permute-start.5 = (bf16[280,768]{1,0:T(8,128)(2,1)}, bf16[280,768]{1,0:T(8,128)(2,1)S(1)}, u32[]{:S(2)}, u32[]{:S(2)}) collective-permute-start(bf16[280,768]{1,0:T(8,128)(2,1)} %collective-permute-done.4), channel_id=1, source_target_pairs={{2,0},{3,1},{10,8},{11,9},{18,16},{19,17},{26,24},{27,25}} | collective-permute-start | bytes 1290248 | tf_op jit(solution)/shard_map/ppermute | solution.py:118
  92.6 30.9 %copy-start.67 = (f32[4,9]{1,0:T(4,128)}, f32[4,9]{1,0:T(4,128)S(1)}, u32[]{:S(2)}) copy-start(f32[4,9]{1,0:T(4,128)S(1)} %broadcast_multiply_fusion.3) | copy-start | bytes 436
  92.8 26.1 %copy-start.97 = (f32[4,9]{1,0:T(4,128)}, f32[4,9]{1,0:T(4,128)S(1)}, u32[]{:S(2)}) copy-start(f32[4,9]{1,0:T(4,128)S(1)} %multiply_reduce_fusion.12) | copy-start | bytes 436
  92.8 30.7 %copy-start.71 = (f32[4,9]{1,0:T(4,128)}, f32[4,9]{1,0:T(4,128)S(1)}, u32[]{:S(2)}) copy-start(f32[4,9]{1,0:T(4,128)S(1)} %fusion.226) | copy-start | bytes 436
  121.1 4.7 collective-permute-start.6
  134.6 26.1 %copy-start.78 = (f32[768]{0:T(1024)}, f32[768]{0:T(1024)S(1)}, u32[]{:S(2)}) copy-start(f32[768]{0:T(1024)S(1)} %add.526) | copy-start | bytes 9220
  166.7 27.6 %copy-start.8 = (bf16[4,208,768]{2,1,0:T(8,128)(2,1)S(1)}, bf16[4,208,768]{2,1,0:T(8,128)(2,1)}, u32[]{:S(2)}) copy-start(bf16[4,208,768]{2,1,0:T(8,128)(2,1)} %pad.42.clone) | copy-start | bytes 3833860
  311.3 10.7 %collective-permute-start.7 = (bf16[4,8,32,768]{3,1,2,0:T(8,128)(2,1)}, bf16[4,8,32,768]{3,1,2,0:T(8,128)(2,1)}, u32[]{:S(2)}, u32[]{:S(2)}) collective-permute-start(bf16[4,8,32,768]{3,1,2,0:T(8,128)(2,1)} %bitcast.321), channel_id=1, source_target_pairs={{0,1},{1,0},{2,3},{3,2},{4,5},{5,4},{6,7},{7,6},{8,9},{9,8},{10,11... | collective-permute-start | bytes 4718600 | tf_op jit(solution)/shard_map/ppermute | solution.py:113
  324.4 10.7 %collective-permute-start.8 = (bf16[8,32,768]{2,0,1:T(8,128)(2,1)S(1)}, bf16[8,32,768]{2,0,1:T(8,128)(2,1)}, u32[]{:S(2)}, u32[]{:S(2)}) collective-permute-start(bf16[8,32,768]{2,0,1:T(8,128)(2,1)S(1)} %get-tuple-element.246), channel_id=1, source_target_pairs={{0,2},{1,3},{8,10},{9,11},{16,18},{17,19},{24,26},{25,27}} | collective-permute-start | bytes 1179656 | tf_op jit(solution)/shard_map/ppermute | solution.py:118
  330.3 36.3 %collective-permute-start.27 = (bf16[2,2,4,104,768]{4,3,2,1,0:T(8,128)(2,1)}, bf16[2,2,4,104,768]{4,3,2,1,0:T(8,128)(2,1)}, u32[]{:S(2)}, u32[]{:S(2)}) collective-permute-start(bf16[2,2,4,104,768]{4,3,2,1,0:T(8,128)(2,1)} %dynamic-slice_bitcast_fusion), channel_id=1, source_target_pairs={{0,1},{1,0},{2,3},{3,2},{4,5},{5,4},{6,7},{7,6},{8,9},{9,8},{10,11... | collective-permute-start | bytes 7667720 | tf_op jit(solution)/shard_map/ppermute | solution.py:113
  330.4 20.2 %collective-permute-start.11 = (bf16[8,32,768]{2,0,1:T(8,128)(2,1)S(1)}, bf16[8,32,768]{2,0,1:T(8,128)(2,1)S(1)}, u32[]{:S(2)}, u32[]{:S(2)}) collective-permute-start(bf16[8,32,768]{2,0,1:T(8,128)(2,1)S(1)} %get-tuple-element.247), channel_id=1, source_target_pairs={{6,4},{7,5},{14,12},{15,13},{22,20},{23,21},{30,28},{31,29}} | collective-permute-start | bytes 1179656 | tf_op jit(solution)/shard_map/ppermute | solution.py:118
  336.2 14.3 %collective-permute-start.9 = (bf16[8,32,768]{2,0,1:T(8,128)(2,1)S(1)}, bf16[8,32,768]{2,0,1:T(8,128)(2,1)S(1)}, u32[]{:S(2)}, u32[]{:S(2)}) collective-permute-start(bf16[8,32,768]{2,0,1:T(8,128)(2,1)S(1)} %fusion.28), channel_id=1, source_target_pairs={{0,2},{1,3},{2,4},{3,5},{8,10},{9,11},{10,12},{11,13},{16,18},{17,... | collective-permute-start | bytes 1179656 | tf_op jit(solution)/shard_map/ppermute | solution.py:118
  350.7 7.0 %collective-permute-start.12 = (bf16[8,32,768]{2,0,1:T(8,128)(2,1)S(1)}, bf16[8,32,768]{2,0,1:T(8,128)(2,1)S(1)}, u32[]{:S(2)}, u32[]{:S(2)}) collective-permute-start(bf16[8,32,768]{2,0,1:T(8,128)(2,1)S(1)} %get-tuple-element.245), channel_id=1, source_target_pairs={{4,2},{5,3},{6,4},{7,5},{12,10},{13,11},{14,12},{15,13},{20,18},{2... | collective-permute-start | bytes 1179656 | tf_op jit(solution)/shard_map/ppermute | solution.py:118
  354.2 15.0 %collective-permute-start.10 = (bf16[8,32,768]{2,0,1:T(8,128)(2,1)S(1)}, bf16[8,32,768]{2,0,1:T(8,128)(2,1)S(1)}, u32[]{:S(2)}, u32[]{:S(2)}) collective-permute-start(bf16[8,32,768]{2,0,1:T(8,128)(2,1)S(1)} %get-tuple-element.244), channel_id=1, source_target_pairs={{0,2},{1,3},{2,4},{3,5},{4,6},{5,7},{8,10},{9,11},{10,12},{11,13},... | collective-permute-start | bytes 1179656 | tf_op jit(solution)/shard_map/ppermute | solution.py:118
  357.8 14.2 %collective-permute-start.13 = (bf16[8,32,768]{2,0,1:T(8,128)(2,1)S(1)}, bf16[8,32,768]{2,0,1:T(8,128)(2,1)S(1)}, u32[]{:S(2)}, u32[]{:S(2)}) collective-permute-start(bf16[8,32,768]{2,0,1:T(8,128)(2,1)S(1)} %fusion.27), channel_id=1, source_target_pairs={{2,0},{3,1},{4,2},{5,3},{6,4},{7,5},{10,8},{11,9},{12,10},{13,11},... | collective-permute-start | bytes 1179656 | tf_op jit(solution)/shard_map/ppermute | solution.py:118
  375.0 8.0 %collective-permute-start.20 = (f32[9,128]{1,0:T(8,128)S(1)}, f32[9,128]{1,0:T(8,128)S(1)}, u32[]{:S(2)}, u32[]{:S(2)}) collective-permute-start(f32[9,128]{1,0:T(8,128)S(1)} %pad_maximum_fusion.18), channel_id=1, source_target_pairs={{0,1},{1,2},{2,3},{3,4},{4,5},{5,6},{6,7},{7,0},{8,9},{9,10},{10,1... | collective-permute-start | bytes 13832 | tf_op jit(solution)/shard_map/ppermute | solution.py:347
  375.0 10.2 %collective-permute-start.19 = (f32[9,128]{1,0:T(8,128)S(1)}, f32[9,128]{1,0:T(8,128)S(1)}, u32[]{:S(2)}, u32[]{:S(2)}) collective-permute-start(f32[9,128]{1,0:T(8,128)S(1)} %pad_maximum_fusion.18), channel_id=1, source_target_pairs={{0,2},{1,3},{2,4},{3,5},{4,6},{5,7},{6,0},{7,1},{8,10},{9,11},{10,... | collective-permute-start | bytes 13832 | tf_op jit(solution)/shard_map/ppermute | solution.py:347
  378.5 9.0 %collective-permute-start.18 = (f32[9,128]{1,0:T(8,128)S(1)}, f32[9,128]{1,0:T(8,128)S(1)}, u32[]{:S(2)}, u32[]{:S(2)}) collective-permute-start(f32[9,128]{1,0:T(8,128)S(1)} %pad_maximum_fusion.18), channel_id=1, source_target_pairs={{0,3},{1,4},{2,5},{3,6},{4,7},{5,0},{6,1},{7,2},{8,11},{9,12},{10,... | collective-permute-start | bytes 13832 | tf_op jit(solution)/shard_map/ppermute | solution.py:347
  380.5 8.5 %collective-permute-start.17 = (f32[9,128]{1,0:T(8,128)S(1)}, f32[9,128]{1,0:T(8,128)S(1)}, u32[]{:S(2)}, u32[]{:S(2)}) collective-permute-start(f32[9,128]{1,0:T(8,128)S(1)} %pad_maximum_fusion.18), channel_id=1, source_target_pairs={{0,4},{1,5},{2,6},{3,7},{4,0},{5,1},{6,2},{7,3},{8,12},{9,13},{10,... | collective-permute-start | bytes 13832 | tf_op jit(solution)/shard_map/ppermute | solution.py:347
  382.3 6.7 %collective-permute-start.16 = (f32[9,128]{1,0:T(8,128)S(1)}, f32[9,128]{1,0:T(8,128)S(1)}, u32[]{:S(2)}, u32[]{:S(2)}) collective-permute-start(f32[9,128]{1,0:T(8,128)S(1)} %pad_maximum_fusion.18), channel_id=1, source_target_pairs={{0,5},{1,6},{2,7},{3,0},{4,1},{5,2},{6,3},{7,4},{8,13},{9,14},{10,... | collective-permute-start | bytes 13832 | tf_op jit(solution)/shard_map/ppermute | solution.py:347
  383.0 6.0 %collective-permute-start.15 = (f32[9,128]{1,0:T(8,128)S(1)}, f32[9,128]{1,0:T(8,128)S(1)}, u32[]{:S(2)}, u32[]{:S(2)}) collective-permute-start(f32[9,128]{1,0:T(8,128)S(1)} %pad_maximum_fusion.18), channel_id=1, source_target_pairs={{0,6},{1,7},{2,0},{3,1},{4,2},{5,3},{6,4},{7,5},{8,14},{9,15},{10,... | collective-permute-start | bytes 13832 | tf_op jit(solution)/shard_map/ppermute | solution.py:347
  385.2 3.8 collective-permute-start.14
  387.5 50.9 %collective-permute-start.28 = (bf16[2,2,104,768]{3,2,1,0:T(8,128)(2,1)}, bf16[2,2,104,768]{3,2,1,0:T(8,128)(2,1)}, u32[]{:S(2)}, u32[]{:S(2)}) collective-permute-start(bf16[2,2,104,768]{3,2,1,0:T(8,128)(2,1)} %dynamic-slice_bitcast_fusion.2), channel_id=1, source_target_pairs={{0,8},{1,9},{2,10},{3,11},{4,12},{5,13},{6,14},{7,15},{8,0},{9,1},... | collective-permute-start | bytes 1916936 | tf_op jit(solution)/shard_map/ppermute | solution.py:113
  389.2 17.0 %collective-permute-start.23 = (f32[9,128]{1,0:T(8,128)S(1)}, f32[9,128]{1,0:T(8,128)S(1)}, u32[]{:S(2)}, u32[]{:S(2)}) collective-permute-start(f32[9,128]{1,0:T(8,128)S(1)} %select_reduce_fusion), channel_id=1, source_target_pairs={{0,8},{8,16},{16,24},{24,0},{1,9},{9,17},{17,25},{25,1},{2,10},{10... | collective-permute-start | bytes 13832 | tf_op jit(solution)/shard_map/ppermute | solution.py:347
  389.8 16.4 %collective-permute-start.22 = (f32[9,128]{1,0:T(8,128)S(1)}, f32[9,128]{1,0:T(8,128)S(1)}, u32[]{:S(2)}, u32[]{:S(2)}) collective-permute-start(f32[9,128]{1,0:T(8,128)S(1)} %select_reduce_fusion), channel_id=1, source_target_pairs={{0,16},{8,24},{16,0},{24,8},{1,17},{9,25},{17,1},{25,9},{2,18},{10... | collective-permute-start | bytes 13832 | tf_op jit(solution)/shard_map/ppermute | solution.py:347
  391.3 15.0 %collective-permute-start.21 = (f32[9,128]{1,0:T(8,128)S(1)}, f32[9,128]{1,0:T(8,128)S(1)}, u32[]{:S(2)}, u32[]{:S(2)}) collective-permute-start(f32[9,128]{1,0:T(8,128)S(1)} %select_reduce_fusion), channel_id=1, source_target_pairs={{0,24},{8,0},{16,8},{24,16},{1,25},{9,1},{17,9},{25,17},{2,26},{10... | collective-permute-start | bytes 13832 | tf_op jit(solution)/shard_map/ppermute | solution.py:347
  394.5 46.0 %collective-permute-start.30 = (bf16[2,2,104,768]{3,2,1,0:T(8,128)(2,1)}, bf16[2,2,104,768]{3,2,1,0:T(8,128)(2,1)}, u32[]{:S(2)}, u32[]{:S(2)}) collective-permute-start(bf16[2,2,104,768]{3,2,1,0:T(8,128)(2,1)} %dynamic-slice_bitcast_fusion.1), channel_id=1, source_target_pairs={{0,16},{1,17},{2,18},{3,19},{4,20},{5,21},{6,22},{7,23},{8,24},{9,... | collective-permute-start | bytes 1916936 | tf_op jit(solution)/shard_map/ppermute | solution.py:113
  399.4 74.3 %all-to-all-start = ((f32[4,8,32,192]{3,1,2,0:T(8,128)}), f32[4,8,32,192]{3,1,2,0:T(8,128)}, u32[]{:S(2)}, u32[]{:S(2)}) async-start(f32[4,8,32,192]{3,1,2,0:T(8,128)} %bitcast.347), calls=%async_computation | async-start | bytes 2097152 | tf_op jit(solution)/shard_map/all_to_all | solution.py:622
  439.8 20.4 %copy-start.77 = (f32[4,9,128]{2,1,0:T(8,128)S(1)}, f32[4,9,128]{2,1,0:T(8,128)}, u32[]{:S(2)}) copy-start(f32[4,9,128]{2,1,0:T(8,128)} %get-tuple-element.275) | copy-start | bytes 55300
  439.8 20.4 %copy-start.26 = (f32[4,9,2048]{2,1,0:T(8,128)S(1)}, f32[4,9,2048]{2,1,0:T(8,128)}, u32[]{:S(2)}) copy-start(f32[4,9,2048]{2,1,0:T(8,128)} %copy-done.25) | copy-start | bytes 884740
  439.9 20.4 %copy-start.96 = (f32[128]{0:T(128)S(1)}, f32[128]{0:T(128)}, u32[]{:S(2)}) copy-start(f32[128]{0:T(128)} %param.44) | copy-start | bytes 1540
  439.9 20.4 %copy-start.112 = (f32[128]{0:T(128)S(1)}, f32[128]{0:T(128)}, u32[]{:S(2)}) copy-start(f32[128]{0:T(128)} %param.45) | copy-start | bytes 1540
  439.9 15.7 %collective-permute-start.29 = (bf16[2,104,768]{2,1,0:T(8,128)(2,1)S(1)}, bf16[2,104,768]{2,1,0:T(8,128)(2,1)S(1)}, u32[]{:S(2)}, u32[]{:S(2)}) collective-permute-start(bf16[2,104,768]{2,1,0:T(8,128)(2,1)S(1)} %dynamic-slice_bitcast_fusion.6), channel_id=1, source_target_pairs={{0,16},{1,17},{2,18},{3,19},{4,20},{5,21},{6,22},{7,23},{8,24},{9,... | collective-permute-start | bytes 958472 | tf_op jit(solution)/shard_map/ppermute | solution.py:113
  442.0 13.6 %collective-permute-start.31 = (bf16[2,104,768]{2,1,0:T(8,128)(2,1)S(1)}, bf16[2,104,768]{2,1,0:T(8,128)(2,1)S(1)}, u32[]{:S(2)}, u32[]{:S(2)}) collective-permute-start(bf16[2,104,768]{2,1,0:T(8,128)(2,1)S(1)} %dynamic-slice_bitcast_fusion.5), channel_id=1, source_target_pairs={{0,8},{1,9},{2,10},{3,11},{4,12},{5,13},{6,14},{7,15},{8,0},{9,1},... | collective-permute-start | bytes 958472 | tf_op jit(solution)/shard_map/ppermute | solution.py:113
  455.9 9.5 %collective-permute-start.32 = (bf16[104,768]{1,0:T(8,128)(2,1)S(1)}, bf16[104,768]{1,0:T(8,128)(2,1)S(1)}, u32[]{:S(2)}, u32[]{:S(2)}) collective-permute-start(bf16[104,768]{1,0:T(8,128)(2,1)S(1)} %get-tuple-element.256), channel_id=1, source_target_pairs={{0,2},{1,3},{8,10},{9,11},{16,18},{17,19},{24,26},{25,27}} | collective-permute-start | bytes 479240 | tf_op jit(solution)/shard_map/ppermute | solution.py:118
  459.0 6.4 %collective-permute-start.35 = (bf16[104,768]{1,0:T(8,128)(2,1)S(1)}, bf16[104,768]{1,0:T(8,128)(2,1)S(1)}, u32[]{:S(2)}, u32[]{:S(2)}) collective-permute-start(bf16[104,768]{1,0:T(8,128)(2,1)S(1)} %get-tuple-element.257), channel_id=1, source_target_pairs={{6,4},{7,5},{14,12},{15,13},{22,20},{23,21},{30,28},{31,29}} | collective-permute-start | bytes 479240 | tf_op jit(solution)/shard_map/ppermute | solution.py:118
  465.6 10.1 %collective-permute-start.33 = (bf16[104,768]{1,0:T(8,128)(2,1)S(1)}, bf16[104,768]{1,0:T(8,128)(2,1)S(1)}, u32[]{:S(2)}, u32[]{:S(2)}) collective-permute-start(bf16[104,768]{1,0:T(8,128)(2,1)S(1)} %get-tuple-element.254), channel_id=1, source_target_pairs={{0,2},{1,3},{2,4},{3,5},{8,10},{9,11},{10,12},{11,13},{16,18},{17,... | collective-permute-start | bytes 479240 | tf_op jit(solution)/shard_map/ppermute | solution.py:118
  470.0 5.7 %collective-permute-start.36 = (bf16[104,768]{1,0:T(8,128)(2,1)S(1)}, bf16[104,768]{1,0:T(8,128)(2,1)S(1)}, u32[]{:S(2)}, u32[]{:S(2)}) collective-permute-start(bf16[104,768]{1,0:T(8,128)(2,1)S(1)} %get-tuple-element.255), channel_id=1, source_target_pairs={{4,2},{5,3},{6,4},{7,5},{12,10},{13,11},{14,12},{15,13},{20,18},{2... | collective-permute-start | bytes 479240 | tf_op jit(solution)/shard_map/ppermute | solution.py:118
  475.9 18.7 %collective-permute-start.37 = (bf16[104,768]{1,0:T(8,128)(2,1)S(1)}, bf16[104,768]{1,0:T(8,128)(2,1)S(1)}, u32[]{:S(2)}, u32[]{:S(2)}) collective-permute-start(bf16[104,768]{1,0:T(8,128)(2,1)S(1)} %get-tuple-element.253), channel_id=1, source_target_pairs={{2,0},{3,1},{4,2},{5,3},{6,4},{7,5},{10,8},{11,9},{12,10},{13,11},... | collective-permute-start | bytes 479240 | tf_op jit(solution)/shard_map/ppermute | solution.py:118
  477.2 17.4 %collective-permute-start.34 = (bf16[104,768]{1,0:T(8,128)(2,1)S(1)}, bf16[104,768]{1,0:T(8,128)(2,1)S(1)}, u32[]{:S(2)}, u32[]{:S(2)}) collective-permute-start(bf16[104,768]{1,0:T(8,128)(2,1)S(1)} %get-tuple-element.252), channel_id=1, source_target_pairs={{0,2},{1,3},{2,4},{3,5},{4,6},{5,7},{8,10},{9,11},{10,12},{11,13},... | collective-permute-start | bytes 479240 | tf_op jit(solution)/shard_map/ppermute | solution.py:118
  (133 other events, 1009.4 us)
Sparse Core Ops, SparseCore 0:
  9.8 48.9 all-gather.4
  60.5 27.9 all-gather.6
  90.1 53.9 all-gather.8
  145.6 48.6 all-gather.10
  330.5 157.4 reduce-scatter.1

commit v2 on v1

v2 whole, which is shorter than its diff:
```python
import functools

import jax
import jax.numpy as jnp
from jax import lax
from jax.experimental import pallas as pl
from jax.experimental.pallas import tpu as pltpu
from jax.sharding import PartitionSpec as P

HEADS = 12
WHEADS = 4
WAVES = 256


norm_eps = 1e-06
hyper_eps = 1e-05
highest_precision = lax.Precision.HIGHEST


def layer_norm(values, norm_gain, norm_shift, epsilon):
    centre = values - jnp.mean(values, axis=-1, keepdims=True)
    spread = jnp.mean(centre * centre, axis=-1, keepdims=True)
    return centre * lax.rsqrt(spread + epsilon) * norm_gain + norm_shift


def gelu_exact(values):
    return jax.nn.gelu(values, approximate=False)


def wave_embed(indices, hyper_width):
    half_model_width = hyper_width // 2
    wavelength = 400.0 + 2100.0 * indices.astype(jnp.float32) / (WAVES - 1)
    frequency = 1.0 / 10000.0 ** (
        jnp.arange(half_model_width, dtype=jnp.float32) / half_model_width
    )
    angles = wavelength[:, None] * frequency[None, :]
    return jnp.concatenate([jnp.sin(angles), jnp.cos(angles)], axis=-1)


def hyper_forward(params, indices, band_total):
    (
        tokens,
        bias_tok,
        qkv_w,
        qv_b,
        out_w,
        out_b,
        gain_one,
        shift_one,
        ff_in,
        ff_in_b,
        ff_out,
        ff_out_b,
        gain_two,
        shift_two,
    ) = params
    hyper_width = tokens.shape[1]
    slot_count = indices.shape[0]
    token_rows = tokens.shape[0]
    head_dim = hyper_width // WHEADS
    waves = wave_embed(indices, hyper_width)
    joined = jnp.concatenate([tokens, waves, bias_tok[None, :]], axis=0)
    query_rows = joined[token_rows:]
    queries = (
        jnp.dot(query_rows, qkv_w[:, :hyper_width], precision=highest_precision)
        + qv_b[:hyper_width]
    ).reshape(slot_count + 1, WHEADS, head_dim)
    key_rows = jnp.dot(
        joined, qkv_w[:, hyper_width : 2 * hyper_width], precision=highest_precision
    ).reshape(-1, WHEADS, head_dim)
    values = (
        jnp.dot(joined, qkv_w[:, 2 * hyper_width :], precision=highest_precision)
        + qv_b[hyper_width:]
    ).reshape(-1, WHEADS, head_dim)
    scores = jnp.einsum(
        "qhd,khd->hqk", queries, key_rows, precision=highest_precision
    ) * head_dim ** (-0.5)
    offsets = jnp.arange(joined.shape[0]) - token_rows
    usable = (offsets < band_total) | (offsets == slot_count)
    scores = jnp.where(usable[None, None, :], scores, -1e30)
    weights = jax.nn.softmax(scores, axis=-1)
    mixture = jnp.einsum("hqk,khd->qhd", weights, values, precision=highest_precision).reshape(
        slot_count + 1, hyper_width
    )
    normed_one = layer_norm(
        query_rows + jnp.dot(mixture, out_w, precision=highest_precision) + out_b,
        gain_one,
        shift_one,
        hyper_eps,
    )
    hidden = gelu_exact(jnp.dot(normed_one, ff_in, precision=highest_precision) + ff_in_b)
    normed_two = layer_norm(
        normed_one + jnp.dot(hidden, ff_out, precision=highest_precision) + ff_out_b,
        gain_two,
        shift_two,
        hyper_eps,
    )
    return (normed_two[:slot_count] + waves, normed_two[slot_count])


BOTH = ("grp", "img")


def torus_block():
    return lax.axis_size("grp") == 4 and lax.axis_size("img") == 8


def flipped(index, bit):
    return index ^ bit


def swap(value, bit):
    return lax.ppermute(value, BOTH, [(i, i ^ bit) for i in range(32)])


def along_z(value, step, senders):
    moves = [(i, i + 2 * step) for i in range(32) if (i % 8) // 2 in senders]
    return lax.ppermute(value, BOTH, moves)


def pick(value, index, axis=0):
    return lax.dynamic_index_in_dim(value, index, axis, keepdims=False)


def add_low(left, right):
    return (left.astype(jnp.float32) + right.astype(jnp.float32)).astype(jnp.bfloat16)


def z_index():
    return (lax.axis_index("img") // 2).astype(jnp.int32)


def scatter_step(chunks, held, step):
    z = z_index()
    up_term = pick(chunks, jnp.clip(4 - step + z, 0, 3))
    down_term = pick(chunks, jnp.clip(z - 4 + step, 0, 3))
    if held is not None:
        up_term = add_low(up_term, held[0])
        down_term = add_low(down_term, held[1])
    return along_z(up_term, 1, range(step)), along_z(down_term, -1, range(4 - step, 4))


def scatter_end(chunks, held):
    own = pick(chunks, z_index())
    return own.astype(jnp.float32) + held[0].astype(jnp.float32) + held[1].astype(jnp.float32)


def gather_step(held, step):
    return along_z(held[0], 1, range(step - 1, 3)), along_z(held[1], -1, range(1, 5 - step))


def gather_end(own, steps):
    z = z_index()
    by_offset = {0: own}
    for at, (up, down) in enumerate(steps):
        by_offset[-1 - at] = up
        by_offset[1 + at] = down
    rows = []
    for place in range(4):
        row = by_offset[place]
        for z_at in range(1, 4):
            row = jnp.where(z == z_at, by_offset[place - z_at], row)
        rows.append(row)
    return jnp.stack(rows)


def in_order(bit, own, other, axis):
    return jnp.stack(
        [jnp.where(bit == 0, own, other), jnp.where(bit == 0, other, own)], axis=axis
    )


def together(*values):
    return lax.optimization_barrier(values)


def core_half(value, axis):
    core = lax.axis_index("img") % 2
    return pick(value, core, axis), pick(value, 1 - core, axis)


def gather_small(value):
    if not torus_block():
        return lax.all_gather(value, "img", axis=0, tiled=False)
    shard = lax.axis_index("img")
    value = in_order(shard % 2, value, swap(value, 1), 0)
    value = in_order(shard // 2 % 2, value, swap(value, 2), 0)
    value = in_order(shard // 4, value, swap(value, 4), 0)
    return value.reshape((8,) + value.shape[3:])


def gather_hidden(fc1_weight, fc2_weight):
    shard, hidden = fc1_weight.shape
    width = fc2_weight.shape[1]
    part = hidden // 4
    if not torus_block():
        fc1 = lax.all_gather(fc1_weight, "img", axis=0, tiled=True)
        fc2 = lax.all_gather(fc2_weight, "img", axis=0, tiled=True)
        fc1 = fc1.reshape(8, -1, 4, part).transpose(2, 0, 1, 3)
        fc2 = fc2.reshape(8, 4, -1, width).transpose(1, 0, 2, 3)
        return jnp.concatenate([fc1, fc2], axis=2)
    group = lax.axis_index("grp")
    own = jnp.concatenate(
        [
            lax.dynamic_slice_in_dim(fc1_weight, group * part, part, 1),
            lax.dynamic_slice_in_dim(fc2_weight, group * shard, shard, 0),
        ]
    )
    return lax.all_gather(own, BOTH, axis=0, tiled=False).reshape(4, 8, 2 * shard, width)


def gather_kernels(kernels, rows_call):
    if not torus_block():
        kernels = lax.all_gather(kernels, "img", axis=0, tiled=False)
        kernels = kernels.reshape((-1, 2) + kernels.shape[1:])
        return core_half(kernels, 1) + (rows_call(None),)
    one = gather_step((kernels, kernels), 1)
    rows = rows_call(kernels)
    one, rows = together(one, rows)
    two = gather_step(one, 2)
    three = gather_step(two, 3)
    line = gather_end(kernels, [one, two, three])
    return line, swap(line, 1), rows


def start_late(late, later):
    if not torus_block():
        late = lax.psum_scatter(late, BOTH, scatter_dimension=0, tiled=True)[0]
        return late.astype(jnp.float32), later
    keep, send = core_half(late.reshape((2, 2, 4, 2) + late.shape[1:]), 3)
    send_in = swap(send, 1)
    keep, later = together(keep, later)
    return (keep, send_in), later


def reduce_late(grad_kernels, late, code_call, fill_calls, gen_call):
    if not torus_block():
        kernels = lax.psum_scatter(grad_kernels, "img", scatter_dimension=0, tiled=True)[0]
        kernels = kernels.astype(jnp.float32)
        code = jnp.sum(ordered_gather(code_call(kernels), "img"), axis=0)
        filled = [call(None) for call in fill_calls] + [gen_call(kernels)]
        return lambda tie: late, ordered_gather(code, "grp"), filled
    group = lax.axis_index("grp")
    x, y = group % 2, group // 2
    shape = grad_kernels.shape
    keep, send = core_half(grad_kernels.reshape(4, 2, shape[1] * shape[2], shape[3]), 1)
    send_in = swap(send, 1)
    late = add_low(*late)
    send_in, late = together(send_in, late)
    chunks = add_low(keep, send_in)
    kernels_one = scatter_step(chunks, None, 1)
    first, second = late[:, :, :2], late[:, :, 2:]
    first_in = swap(pick(first, 1 - x, 1), 8)
    second_in = swap(pick(second, 1 - y, 0), 16)
    filled = [fill_calls[0](chunks)]
    kernels_one, filled[0] = together(kernels_one, filled[0])
    kernels_two = scatter_step(chunks, kernels_one, 2)
    filled.append(fill_calls[1](kernels_one))
    kernels_two, first_in, second_in, filled[1] = together(
        kernels_two, first_in, second_in, filled[1]
    )
    kernels_three = scatter_step(chunks, kernels_two, 3)
    first = add_low(pick(first, x, 1), first_in)
    second = add_low(pick(second, y, 0), second_in)
    first_in = swap(pick(first, 1 - y), 16)
    second_in = swap(pick(second, 1 - x), 8)
    kernels = scatter_end(chunks, kernels_three).reshape(shape[1:])
    code = code_call(kernels)
    code = code + swap(code, 1)
    code = code + swap(code, 2)
    code, kernels, first_in, second_in = together(code, kernels, first_in, second_in)
    code_in = swap(code, 4)
    late = jnp.concatenate(
        [add_low(pick(first, y), first_in), add_low(pick(second, x), second_in)]
    )
    late_one = scatter_step(late, None, 1)
    code = code + code_in
    code = in_order(x, code, swap(code, 8), 0)
    code = in_order(y, code, swap(code, 16), 0).reshape((4,) + code.shape[1:])
    code, kernels, late_one = together(code, kernels, late_one)
    late_two = scatter_step(late, late_one, 2)
    filled.append(gen_call(kernels))

    def late_end(tie):
        late_here, _ = together(late_two, tie)
        return scatter_end(late, scatter_step(late, late_here, 3))

    return late_end, code, filled


def lane_half(shape):
    return lax.broadcasted_iota(jnp.int32, shape, len(shape) - 1) % 128 < 64


def attention_forward_kernel(tokens, projected_ref, attended_ref, probs_ref):
    _, rows, width = projected_ref.shape
    low_half = lane_half((rows, 128))
    real_key = lax.broadcasted_iota(jnp.int32, (rows, rows), 0) < tokens
    for pair in range(width // 128):
        at = pair * 128
        queries = projected_ref[0, :, at : at + 128] * jnp.bfloat16(0.125)
        key_rows = projected_ref[1, :, at : at + 128]
        values = projected_ref[2, :, at : at + 128]
        halves = []
        for half in range(2):
            chosen = low_half if half == 0 else ~low_half
            own_queries = jnp.where(chosen, queries, jnp.bfloat16(0))
            scores = lax.dot_general(
                key_rows, own_queries, (((1,), (1,)), ((), ())), preferred_element_type=jnp.float32
            )
            scores = jnp.where(real_key, scores, -1e30)
            raised = jnp.exp(scores - jnp.max(scores, axis=0, keepdims=True))
            probs = raised * (1.0 / jnp.sum(raised, axis=0, keepdims=True))
            probs = probs.astype(jnp.bfloat16)
            probs_ref[2 * pair + half] = probs
            halves.append(
                lax.dot_general(
                    probs, values, (((0,), (0,)), ((), ())), preferred_element_type=jnp.float32
                )
            )
        attended_ref[:, at : at + 128] = jnp.where(low_half, halves[0], halves[1]).astype(
            jnp.bfloat16
        )


def attention_forward(projected, images, tokens):
    _, total, width = projected.shape
    rows = total // images
    heads = width // 64
    return pl.pallas_call(
        functools.partial(attention_forward_kernel, tokens),
        grid=(images,),
        in_specs=[pl.BlockSpec((3, rows, width), lambda i: (0, i, 0))],
        out_specs=[
            pl.BlockSpec((rows, width), lambda i: (i, 0)),
            pl.BlockSpec((None, heads, rows, rows), lambda i: (i, 0, 0, 0)),
        ],
        out_shape=[
            jax.ShapeDtypeStruct((images * rows, width), jnp.bfloat16),
            jax.ShapeDtypeStruct((images, heads, rows, rows), jnp.bfloat16),
        ],
        compiler_params=pltpu.CompilerParams(vmem_limit_bytes=48 << 20),
        cost_estimate=pl.CostEstimate(
            flops=images * heads * rows * rows * 64 * 4,
            bytes_accessed=images * rows * (8 * width + 2 * heads * rows),
            transcendentals=images * heads * rows * rows,
        ),
        name="attention_forward",
    )(projected)


def attention_backward_kernel(projected_ref, probs_ref, grad_ref, out_ref, sums_ref):
    _, rows, width = projected_ref.shape
    low_half = lane_half((rows, 128))

    @pl.when(pl.program_id(0) == 0)
    def _():
        sums_ref[...] = jnp.zeros_like(sums_ref)

    for pair in range(width // 128):
        at = pair * 128
        queries = projected_ref[0, :, at : at + 128]
        key_rows = projected_ref[1, :, at : at + 128]
        values = projected_ref[2, :, at : at + 128]
        grads = grad_ref[:, at : at + 128]
        found = []
        for half in range(2):
            chosen = low_half if half == 0 else ~low_half
            probs = probs_ref[2 * pair + half]
            own_grads = jnp.where(chosen, grads, jnp.bfloat16(0))
            grad_values = jnp.dot(probs, grads, preferred_element_type=jnp.float32)
            grad_probs = lax.dot_general(
                values, own_grads, (((1,), (1,)), ((), ())), preferred_element_type=jnp.float32
            )
            wide = probs.astype(jnp.float32)
            weighted = grad_probs * wide
            total = jnp.sum(weighted, axis=0, keepdims=True)
            grad_scores = (weighted - wide * total).astype(jnp.bfloat16)
            grad_keys = jnp.dot(grad_scores, queries, preferred_element_type=jnp.float32) * 0.125
            grad_queries = (
                lax.dot_general(
                    grad_scores,
                    key_rows,
                    (((0,), (0,)), ((), ())),
                    preferred_element_type=jnp.float32,
                )
                * 0.125
            )
            found.append((grad_queries, grad_keys, grad_values))
        for kind in range(3):
            joined = jnp.where(low_half, found[0][kind], found[1][kind]).astype(jnp.bfloat16)
            place = slice(at, at + 128)
            out_ref[kind, :, place] = joined
            sums_ref[kind, :, place] += jnp.sum(
                joined.astype(jnp.float32).reshape(rows // 8, 8, 128), axis=0
            )


def attention_backward(projected, probs, grad_attended, images):
    _, total, width = projected.shape
    rows = total // images
    heads = width // 64
    return pl.pallas_call(
        attention_backward_kernel,
        grid=(images,),
        in_specs=[
            pl.BlockSpec((3, rows, width), lambda i: (0, i, 0)),
            pl.BlockSpec((None, heads, rows, rows), lambda i: (i, 0, 0, 0)),
            pl.BlockSpec((rows, width), lambda i: (i, 0)),
        ],
        out_specs=[
            pl.BlockSpec((3, rows, width), lambda i: (0, i, 0)),
            pl.BlockSpec((3, 8, width), lambda i: (0, 0, 0)),
        ],
        out_shape=[
            jax.ShapeDtypeStruct((3, total, width), jnp.bfloat16),
            jax.ShapeDtypeStruct((3, 8, width), jnp.float32),
        ],
        compiler_params=pltpu.CompilerParams(vmem_limit_bytes=48 << 20),
        cost_estimate=pl.CostEstimate(flops=0, bytes_accessed=0, transcendentals=0),
        name="attention_backward",
    )(projected, probs, grad_attended)


SLOT_ROWS = 16


def exact_dot(left, right, contract=((1,), (0,))):
    return lax.dot_general(
        left,
        right,
        (contract, ((), ())),
        precision=highest_precision,
        preferred_element_type=jnp.float32,
    )


def rows_norm(values, norm_gain, norm_shift, epsilon):
    centre = values - jnp.mean(values, axis=-1, keepdims=True)
    spread = jnp.mean(centre * centre, axis=-1, keepdims=True)
    return centre * lax.rsqrt(spread + epsilon) * norm_gain + norm_shift


def gelu_rows(values):
    return values * (0.5 + 0.5 * lax.erf(values * 0.7071067811865476))


def hyper_rows(params, waves, usable, slots):
    (
        tokens,
        bias_tok,
        qkv_w,
        qv_b,
        out_w,
        out_b,
        gain_one,
        shift_one,
        ff_in,
        ff_in_b,
        ff_out,
        ff_out_b,
        gain_two,
        shift_two,
    ) = params
    width = tokens.shape[1]
    head_dim = width // WHEADS
    total = waves.shape[0]
    place = lax.broadcasted_iota(jnp.int32, (total, 1), 0) & (SLOT_ROWS - 1)
    query_rows = jnp.where(place == slots, jnp.broadcast_to(bias_tok, (total, width)), waves)
    joined = jnp.concatenate([tokens, query_rows], axis=0)
    queries = exact_dot(query_rows, qkv_w[:, :width]) + qv_b[:, :width]
    key_rows = exact_dot(joined, qkv_w[:, width : 2 * width])
    values = exact_dot(joined, qkv_w[:, 2 * width :]) + qv_b[:, width:]
    head_at = lax.broadcasted_iota(jnp.int32, (1, width), 1)
    mixture = jnp.zeros((total, width), jnp.float32)
    for head in range(WHEADS):
        own = ((head_at >= head * head_dim) & (head_at < (head + 1) * head_dim)).astype(jnp.float32)
        scores = exact_dot(queries * own, key_rows, ((1,), (1,))) * head_dim ** (-0.5)
        scores = jnp.where(usable > 0, scores, -1e30)
        raised = jnp.exp(scores - lax.stop_gradient(jnp.max(scores, axis=-1, keepdims=True)))
        weights = raised / jnp.sum(raised, axis=-1, keepdims=True)
        mixture = mixture + exact_dot(weights, values) * own
    first = rows_norm(query_rows + exact_dot(mixture, out_w) + out_b, gain_one, shift_one, hyper_eps)
    hidden = gelu_rows(exact_dot(first, ff_in) + ff_in_b)
    return rows_norm(first + exact_dot(hidden, ff_out) + ff_out_b, gain_two, shift_two, hyper_eps)


def usable_rows(band_counts, slots, token_rows):
    groups = band_counts.shape[0]
    total = groups * SLOT_ROWS
    row = jnp.arange(total)
    own_group = row[:, None] // SLOT_ROWS == row[None, :] // SLOT_ROWS
    place = row % SLOT_ROWS
    present = (place < jnp.repeat(band_counts, SLOT_ROWS)) | (place == slots)
    return jnp.concatenate(
        [jnp.ones((total, token_rows)), (own_group & present[None, :]).astype(jnp.float32)], axis=1
    )


def hyper_params_2d(params):
    return tuple(member[None] if member.ndim == 1 else member for member in params)


def wave_rows(indices, width):
    groups, slots = indices.shape
    waves = jax.vmap(lambda row: wave_embed(row, width))(indices)
    return jnp.pad(waves, ((0, 0), (0, SLOT_ROWS - slots), (0, 0))).reshape(-1, width)


def hyper_forward_kernel(slots, waves_ref, usable_ref, *refs):
    refs[-1][...] = hyper_rows(
        tuple(ref[...] for ref in refs[:-1]), waves_ref[...], usable_ref[...], slots
    )


def hyper_backward_kernel(slots, waves_ref, usable_ref, grads_ref, *refs):
    count = len(refs) // 2
    waves, usable = waves_ref[...], usable_ref[...]
    _, pull = jax.vjp(
        lambda params: hyper_rows(params, waves, usable, slots),
        tuple(ref[...] for ref in refs[:count]),
    )
    (found,) = pull(grads_ref[...])
    for ref, value in zip(refs[count:], found):
        ref[...] = value


def hyper_forward_call(params, waves, usable, slots):
    return pl.pallas_call(
        functools.partial(hyper_forward_kernel, slots),
        out_shape=jax.ShapeDtypeStruct(waves.shape, jnp.float32),
        name="hyper_forward",
    )(waves, usable, *params)


def hyper_backward_call(params, waves, usable, grads, slots):
    return pl.pallas_call(
        functools.partial(hyper_backward_kernel, slots),
        out_shape=[jax.ShapeDtypeStruct(member.shape, jnp.float32) for member in params],
        name="hyper_backward",
    )(waves, usable, grads, *params)


def embed_kernel(
    bands, small_at, core_ref, line_ref, other_ref, pixels_ref, kernels_ref, stream_ref, normed_ref, rows_ref
):
    chips, _, width = line_ref.shape
    part = kernels_ref.shape[0] // (2 * chips * bands)
    shard = width // (2 * chips)

    @pl.when(pl.program_id(0) == 0)
    def _():
        for core in range(2):
            low_ref, high_ref = (line_ref, other_ref) if core == 0 else (other_ref, line_ref)

            @pl.when((core_ref[0] == 0) == (core == 0))
            def _():
                for chip in range(chips):
                    for band in range(bands):
                        place = (band * chips + chip) * 2 * part
                        here = slice(band * part, (band + 1) * part)
                        kernels_ref[place : place + part] = low_ref[chip, here]
                        kernels_ref[place + part : place + 2 * part] = high_ref[chip, here]
                    for which, ref in enumerate((low_ref, high_ref)):
                        small = ref[chip, small_at : small_at + 16, :shard].astype(jnp.float32)
                        at = (chip * 2 + which) * shard
                        rows_ref[:, at : at + shard] = small

    shift = rows_ref[0:1] + rows_ref[1:2]
    stream = (
        jnp.dot(pixels_ref[...], kernels_ref[...], preferred_element_type=jnp.float32) + shift
    )
    stream_ref[...] = stream
    centre = stream - jnp.mean(stream, axis=-1, keepdims=True)
    spread = jnp.mean(centre * centre, axis=-1, keepdims=True)
    normed = centre * lax.rsqrt(spread + norm_eps) * rows_ref[2:3] + rows_ref[3:4]
    normed_ref[...] = normed.astype(jnp.bfloat16)


def embed(core, line, other, pixel_rows, images, bands, small_at):
    width = line.shape[2]
    total, depth = pixel_rows.shape
    rows = total // images
    part_spec = pl.BlockSpec(line.shape, lambda i, core_ref: (0, 0, 0))
    row = pl.BlockSpec((rows, width), lambda i, core_ref: (i, 0))
    return pl.pallas_call(
        functools.partial(embed_kernel, bands, small_at),
        grid_spec=pltpu.PrefetchScalarGridSpec(
            num_scalar_prefetch=1,
            grid=(images,),
            in_specs=[
                part_spec,
                part_spec,
                pl.BlockSpec((rows, depth), lambda i, core_ref: (i, 0)),
            ],
            out_specs=[pl.BlockSpec((depth, width), lambda i, core_ref: (0, 0)), row, row],
            scratch_shapes=[pltpu.VMEM((16, width), jnp.float32)],
        ),
        out_shape=[
            jax.ShapeDtypeStruct((depth, width), jnp.bfloat16),
            jax.ShapeDtypeStruct((total, width), jnp.float32),
            jax.ShapeDtypeStruct((total, width), jnp.bfloat16),
        ],
        compiler_params=pltpu.CompilerParams(vmem_limit_bytes=48 << 20),
        cost_estimate=pl.CostEstimate(
            flops=2 * total * width * depth,
            bytes_accessed=total * (2 * depth + 6 * width) + 4 * depth * width,
            transcendentals=total,
        ),
        name="embed",
    )(core, line, other, pixel_rows)


def first_backward_kernel(
    projected_ref,
    query_ref,
    key_ref,
    value_ref,
    stream_ref,
    residual_ref,
    gain_ref,
    pixels_ref,
    out_ref,
    kernels_ref,
    sums_ref,
    total_ref,
):
    rows, width = stream_ref.shape
    shards, bands, part, _ = kernels_ref.shape

    @pl.when(pl.program_id(0) == 0)
    def _():
        sums_ref[...] = jnp.zeros_like(sums_ref)
        total_ref[...] = jnp.zeros_like(total_ref)

    def folded(value):
        return jnp.sum(value.reshape(rows // 8, 8, width), axis=0)

    grads = sum(
        lax.dot_general(
            projected_ref[at],
            ref[...],
            (((1,), (1,)), ((), ())),
            preferred_element_type=jnp.float32,
        )
        for at, ref in enumerate((query_ref, key_ref, value_ref))
    )
    stream = stream_ref[...]
    centre = stream - jnp.mean(stream, axis=-1, keepdims=True)
    spread = jnp.mean(centre * centre, axis=-1, keepdims=True)
    scale = lax.rsqrt(spread + norm_eps)
    normed = centre * scale
    sums_ref[0] += folded(grads * normed)
    sums_ref[1] += folded(grads)
    grads = grads * gain_ref[...]
    grads = scale * (
        grads
        - jnp.mean(grads, axis=-1, keepdims=True)
        - normed * jnp.mean(grads * normed, axis=-1, keepdims=True)
    )
    low = (residual_ref[...] + grads).astype(jnp.bfloat16)
    out_ref[...] = low
    sums_ref[2] += folded(low.astype(jnp.float32))
    total_ref[...] += lax.dot_general(
        pixels_ref[...], low, (((0,), (0,)), ((), ())), preferred_element_type=jnp.float32
    )

    @pl.when(pl.program_id(0) == pl.num_programs(0) - 1)
    def _():
        for shard in range(shards):
            for band in range(bands):
                place = (band * shards + shard) * part
                kernels_ref[shard, band] = total_ref[place : place + part].astype(jnp.bfloat16)


def first_backward(grad_projected, weights, stream, residual, gain, pixel_rows, images, shards, bands):
    total, width = stream.shape
    rows = total // images
    depth = pixel_rows.shape[1]
    row = pl.BlockSpec((rows, width), lambda i: (i, 0))
    made = (shards, bands, depth // (shards * bands), width)
    return pl.pallas_call(
        first_backward_kernel,
        grid=(images,),
        in_specs=[
            pl.BlockSpec((3, rows, width), lambda i: (0, i, 0)),
            pl.BlockSpec((width, width), lambda i: (0, 0)),
            pl.BlockSpec((width, width), lambda i: (0, 1)),
            pl.BlockSpec((width, width), lambda i: (0, 2)),
            row,
            row,
            pl.BlockSpec((1, width), lambda i: (0, 0)),
            pl.BlockSpec((rows, depth), lambda i: (i, 0)),
        ],
        out_specs=[
            row,
            pl.BlockSpec(made, lambda i: (0, 0, 0, 0)),
            pl.BlockSpec((3, 8, width), lambda i: (0, 0, 0)),
        ],
        out_shape=[
            jax.ShapeDtypeStruct((total, width), jnp.bfloat16),
            jax.ShapeDtypeStruct(made, jnp.bfloat16),
            jax.ShapeDtypeStruct((3, 8, width), jnp.float32),
        ],
        scratch_shapes=[pltpu.VMEM((depth, width), jnp.float32)],
        compiler_params=pltpu.CompilerParams(vmem_limit_bytes=48 << 20),
        cost_estimate=pl.CostEstimate(flops=0, bytes_accessed=0, transcendentals=0),
        name="first_backward",
    )(grad_projected, weights, weights, weights, stream, residual, gain, pixel_rows)


def mlp_kernel(
    block,
    devices,
    rows_ref,
    upstream_ref,
    first_weight_ref,
    second_weight_ref,
    b1_ref,
    sums_ref,
    out_ref,
    grad_ref,
    packed_ref,
    turned_ref,
    act_ref,
    gate_ref,
    first_ref,
    second_ref,
    sems,
):
    at_step = pl.program_id(0)
    steps = pl.num_programs(0)
    total, width = rows_ref.shape
    eighths, shard, hidden_block = first_weight_ref.shape
    quarters, group, _, _ = second_weight_ref.shape
    w1 = first_weight_ref[...].reshape(width, hidden_block)
    w2 = jnp.concatenate(
        [second_weight_ref[at, eighth] for eighth in range(group) for at in range(quarters)]
    )
    first_rows = width // devices
    second_devices = devices // steps
    second_rows = hidden_block // second_devices

    def copies(step):
        return (
            pltpu.make_async_copy(
                first_ref, packed_ref.at[:, pl.ds(step * first_rows, first_rows), :], sems.at[0]
            ),
            pltpu.make_async_copy(
                second_ref,
                packed_ref.at[
                    pl.ds(step * second_devices, second_devices),
                    pl.ds(steps * first_rows, second_rows),
                    :,
                ],
                sems.at[1],
            ),
        )

    @pl.when(at_step == 0)
    def _():
        out_ref[...] = jnp.zeros_like(out_ref)
        grad_ref[...] = jnp.zeros_like(grad_ref)
        turned_ref[...] = rows_ref[...].T

    for at in range(0, total, block):
        here = slice(at, at + block)
        gate_in = (
            jnp.dot(rows_ref[here], w1, preferred_element_type=jnp.float32) + b1_ref[...]
        )
        grad_act = lax.dot_general(
            upstream_ref[here],
            w2,
            (((1,), (1,)), ((), ())),
            preferred_element_type=jnp.float32,
        )
        chance = 0.5 + 0.5 * lax.erf(gate_in * 0.7071067811865476)
        density = 0.3989422804014327 * jnp.exp(-0.5 * gate_in * gate_in)
        act = (gate_in * chance).astype(jnp.bfloat16)
        gate = (grad_act * (chance + gate_in * density)).astype(jnp.bfloat16)
        act_ref[here] = act
        gate_ref[here] = gate
        wide = gate.astype(jnp.float32)
        part = jnp.sum(wide.reshape(block // 8, 8, wide.shape[1]), axis=0)
        sums_ref[...] = part if at == 0 else sums_ref[...] + part
        out_ref[here] += jnp.dot(act, w2, preferred_element_type=jnp.float32)
        grad_ref[here] += lax.dot_general(
            gate, w1, (((1,), (1,)), ((), ())), preferred_element_type=jnp.float32
        )

    @pl.when(at_step > 0)
    def _():
        for copy in copies(at_step - 1):
            copy.wait()

    first = jnp.dot(turned_ref[...], gate_ref[...], preferred_element_type=jnp.float32)
    first_ref[...] = first.astype(jnp.bfloat16).reshape(first_ref.shape)
    second = lax.dot_general(
        act_ref[...], upstream_ref[...], (((0,), (0,)), ((), ())), preferred_element_type=jnp.float32
    )
    second_ref[...] = second.astype(jnp.bfloat16).reshape(second_ref.shape)
    for copy in copies(at_step):
        copy.start()

    @pl.when(at_step == steps - 1)
    def _():
        for copy in copies(at_step):
            copy.wait()


def mlp(rows, upstream, weights, b1, row_block, devices):
    total, width = rows.shape
    steps, eighths, shard, hidden_block = weights.shape
    shard //= 2
    hidden = steps * hidden_block
    whole = pl.BlockSpec((total, width), lambda i: (0, 0))
    packed_rows = (width * steps + hidden) // devices
    return pl.pallas_call(
        functools.partial(mlp_kernel, row_block, devices),
        grid=(steps,),
        in_specs=[
            whole,
            whole,
            pl.BlockSpec((None, eighths, shard, hidden_block), lambda i: (i, 0, 0, 0)),
            pl.BlockSpec((steps, eighths // steps, shard, width), lambda i: (0, i, 1, 0)),
            pl.BlockSpec((1, hidden_block), lambda i: (0, i)),
        ],
        out_specs=[
            pl.BlockSpec((8, hidden_block), lambda i: (0, i)),
            whole,
            whole,
            pl.BlockSpec(memory_space=pl.ANY),
        ],
        out_shape=[
            jax.ShapeDtypeStruct((8, hidden), jnp.float32),
            jax.ShapeDtypeStruct((total, width), jnp.float32),
            jax.ShapeDtypeStruct((total, width), jnp.float32),
            jax.ShapeDtypeStruct((devices, packed_rows, width), jnp.bfloat16),
        ],
        scratch_shapes=[
            pltpu.VMEM((width, total), jnp.bfloat16),
            pltpu.VMEM((total, hidden_block), jnp.bfloat16),
            pltpu.VMEM((total, hidden_block), jnp.bfloat16),
            pltpu.VMEM((devices, width // devices, width), jnp.bfloat16),
            pltpu.VMEM((devices // steps, hidden // devices, width), jnp.bfloat16),
            pltpu.SemaphoreType.DMA((2,)),
        ],
        compiler_params=pltpu.CompilerParams(vmem_limit_bytes=52 << 20),
        cost_estimate=pl.CostEstimate(
            flops=12 * total * width * hidden,
            bytes_accessed=8 * width * hidden + 12 * total * width,
            transcendentals=2 * total * hidden,
        ),
        name="mlp",
    )(rows, upstream, weights, weights, b1)


def pixel_grad_kernel(grad_ref, kernels_ref, out_ref):
    tokens, bands, patch = out_ref.shape
    for band in range(bands):
        found = lax.dot_general(
            grad_ref[...],
            kernels_ref[band * patch : (band + 1) * patch, :],
            (((1,), (1,)), ((), ())),
            preferred_element_type=jnp.float32,
        )
        out_ref[:, band, :] = found[:tokens]


def pixel_grad(grads, kernels, images, tokens, bands):
    total, width = grads.shape
    patch = kernels.shape[0] // bands
    return pl.pallas_call(
        pixel_grad_kernel,
        grid=(images,),
        in_specs=[
            pl.BlockSpec((total // images, width), lambda i: (i, 0)),
            pl.BlockSpec(kernels.shape, lambda i: (0, 0)),
        ],
        out_specs=pl.BlockSpec((None, tokens, bands, patch), lambda i: (i, 0, 0, 0)),
        out_shape=jax.ShapeDtypeStruct((images, tokens, bands, patch), jnp.float32),
        compiler_params=pltpu.CompilerParams(vmem_limit_bytes=48 << 20),
        cost_estimate=pl.CostEstimate(flops=0, bytes_accessed=0, transcendentals=0),
        name="pixel_grad",
    )(grads, kernels)


def repack(packed, devices):
    few, rows, width = packed.shape
    each = width // few
    more = devices // few
    first = packed[:, : rows // 2].reshape(few, -1, more, each // more, width)
    first = first.transpose(0, 2, 1, 3, 4).reshape(devices, -1, width)
    return jnp.concatenate([first, packed[:, rows // 2 :].reshape(devices, -1, width)], axis=1)


def ordered_gather(value, axis):
    total = lax.axis_size(axis)
    at = lax.axis_index(axis)
    slots = jnp.arange(total).reshape((total,) + (1,) * value.ndim)
    gathered = jnp.where(slots == at, value[None], jnp.zeros((), value.dtype))
    for shift in range(1, total):
        moved = lax.ppermute(value, axis, [(i, (i + shift) % total) for i in range(total)])
        gathered = jnp.where(slots == (at - shift) % total, moved[None], gathered)
    return gathered


def local(
    pixels,
    cotangent,
    band_count,
    wave_index,
    weight_tokens,
    bias_token,
    hyper_qkv,
    hyper_qv_bias,
    hyper_out,
    hyper_out_bias,
    hyper_norm1_gain,
    hyper_norm1_bias,
    hyper_ff1,
    hyper_ff1_bias,
    hyper_ff2,
    hyper_ff2_bias,
    hyper_norm2_gain,
    hyper_norm2_bias,
    kernel_gen,
    kernel_gen_bias,
    conv_bias_gen,
    conv_bias_gen_bias,
    norm1_gain,
    norm1_bias,
    qkv_weight,
    qv_bias,
    proj_weight,
    proj_bias,
    norm2_gain,
    norm2_bias,
    fc1_weight,
    fc1_bias,
    fc2_weight,
    fc2_bias,
):
    group_total = lax.axis_size("grp")
    shard_total = lax.axis_size("img")
    group_at = lax.axis_index("grp")
    shard_at = lax.axis_index("img")
    images = pixels.shape[0]
    slot_count = pixels.shape[1]
    tokens = pixels.shape[2]
    patch = pixels.shape[3]
    model_width = cotangent.shape[2]
    padded = -(-tokens // 16) * 16
    row_count = images * padded

    def pad_rows(value):
        return jnp.pad(value, ((0, 0), (0, padded - tokens), (0, 0))).reshape(row_count, -1)

    band_total = band_count[0]
    band_mask = (jnp.arange(slot_count) < band_total).astype(jnp.float32)
    hyper_params = (
        weight_tokens,
        bias_token,
        hyper_qkv,
        hyper_qv_bias,
        hyper_out,
        hyper_out_bias,
        hyper_norm1_gain,
        hyper_norm1_bias,
        hyper_ff1,
        hyper_ff1_bias,
        hyper_ff2,
        hyper_ff2_bias,
        hyper_norm2_gain,
        hyper_norm2_bias,
    )
    hyper_wide = weight_tokens.shape[1]
    flat_params = hyper_params_2d(hyper_params)
    shard_patch = kernel_gen.shape[0]
    shard_rows = proj_weight.shape[0]
    lanes = hyper_wide
    folds = model_width // lanes
    fold_rows = shard_rows // folds
    small = [
        conv_bias_gen_bias,
        norm1_gain,
        norm1_bias,
        qv_bias,
        proj_bias,
        norm2_gain,
        norm2_bias,
        fc1_bias,
        fc2_bias,
    ]
    kernel_total = slot_count * shard_patch
    tables = ordered_gather(jnp.concatenate([band_count, wave_index[0]]), "grp")
    own_waves = wave_rows(wave_index, hyper_wide)
    own_usable = usable_rows(band_count, slot_count, weight_tokens.shape[0])

    def hyper_call():
        return hyper_forward_call(flat_params, own_waves, own_usable, slot_count)

    def all_call(tie):
        every = tables if tie is None else together(tables, tie)[0]
        waves = wave_rows(every[:, 1:], hyper_wide)
        usable = usable_rows(every[:, 0], slot_count, weight_tokens.shape[0])
        return waves, usable, hyper_forward_call(flat_params, waves, usable, slot_count)

    def kernel_call(rows):
        hidden = (rows[:slot_count] + own_waves[:slot_count]).astype(jnp.bfloat16)
        made = (
            jnp.einsum("be,pde->bpd", hidden, kernel_gen, preferred_element_type=jnp.float32)
            + kernel_gen_bias.astype(jnp.float32)[None]
        )
        made = (made * band_mask[:, None, None]).astype(jnp.bfloat16)
        *members, small_gen, _ = together(*small, conv_bias_gen, rows)
        shift = jnp.dot(
            small_gen.astype(jnp.float32), rows[slot_count], precision=highest_precision
        ) + members[0].astype(jnp.float32)
        upper = lax.optimization_barrier(shift.astype(jnp.bfloat16))
        lower = (shift - upper.astype(jnp.float32)).astype(jnp.bfloat16)
        small_rows = jnp.stack(
            [
                jnp.pad(member, (0, model_width - member.shape[0]))
                for member in [upper, lower] + members[1:]
            ]
        )
        folded = jnp.concatenate(
            [small_gen[at * fold_rows : (at + 1) * fold_rows] for at in range(folds)], axis=1
        )
        packed = jnp.concatenate([jnp.pad(small_rows, ((0, 16 - len(small) - 1), (0, 0))), folded])
        packed = jnp.pad(packed, ((0, -packed.shape[0] % 16), (0, 0)))
        return jnp.concatenate([made.reshape(kernel_total, model_width), packed])

    def rows_call(tie):
        pixels_here, cotangent_here = pixels, cotangent
        if tie is not None:
            pixels_here, cotangent_here, _ = together(pixels, cotangent, tie)
        pixel_rows = pixels_here.transpose(0, 2, 1, 3).reshape(images, tokens, slot_count * patch)
        return pad_rows(pixel_rows), pad_rows(cotangent_here)

    attention_full = lax.all_gather(
        jnp.concatenate([qkv_weight, proj_weight], axis=1), "img", axis=0, tiled=True
    )
    hidden_full = gather_hidden(fc1_weight, fc2_weight)
    line, other, (pixel_rows, upstream_low) = gather_kernels(kernel_call(hyper_call()), rows_call)
    patch_kernels, stream, normed_low = embed(
        (lax.axis_index("img") % 2).astype(jnp.int32).reshape(1),
        line,
        other,
        pixel_rows,
        images,
        slot_count,
        kernel_total,
    )
    found_small = line[:, kernel_total:], other[:, kernel_total:]
    small_line, small_other, _ = together(*found_small, normed_low)
    packed = in_order(lax.axis_index("img") % 2, small_line, small_other, 1)
    packed = packed.reshape((shard_total,) + packed.shape[2:])
    folded = packed[:, 16 : 16 + fold_rows]
    cb_weight = jnp.concatenate(
        [folded[:, :, at : at + lanes] for at in range(0, model_width, lanes)], axis=1
    ).reshape(model_width, lanes)
    gain_one, _, qv_full, proj_shift, gain_two, shift_two, fc1_shift, fc2_shift = (
        packed[:, 2 + at, : member.shape[0]].reshape(-1) for at, member in enumerate(small[1:])
    )
    proj_full = attention_full[:, 3 * model_width :]
    full_bias = jnp.stack(
        [qv_full[:model_width], jnp.zeros((model_width,), jnp.bfloat16), qv_full[model_width:]]
    ).astype(jnp.float32)
    projected = jnp.stack(
        [
            (
                jnp.dot(
                    normed_low,
                    attention_full[:, at * model_width : (at + 1) * model_width],
                    preferred_element_type=jnp.float32,
                )
                + full_bias[at]
            ).astype(jnp.bfloat16)
            for at in range(3)
        ]
    )
    attended, attn_probs = attention_forward(projected, images, tokens)
    all_waves, all_usable, all_rows = all_call(attended)
    attended, all_rows = together(attended, all_rows)
    all_rows = all_rows.reshape(group_total, SLOT_ROWS, hyper_wide)
    hidden_all = all_rows[:, :slot_count] + all_waves.reshape(all_rows.shape)[:, :slot_count]
    bias_row_all = all_rows[:, slot_count]
    middle = (
        stream
        + jnp.dot(attended, proj_full, preferred_element_type=jnp.float32)
        + proj_shift.astype(jnp.float32)
    )
    normed_two, norm_two_pull = jax.vjp(
        lambda values, norm_gain, norm_shift: layer_norm(values, norm_gain, norm_shift, norm_eps),
        middle,
        gain_two.astype(jnp.float32),
        shift_two.astype(jnp.float32),
    )
    normed_two_low = normed_two.astype(jnp.bfloat16)
    upstream = upstream_low.astype(jnp.float32)
    gate_sums, update, grad_normed_two, early_block = mlp(
        normed_two_low,
        upstream_low,
        hidden_full,
        fc1_shift.astype(jnp.float32)[None],
        row_count // 2,
        group_total * shard_total if torus_block() else 32,
    )
    grad_fc2_shift = jnp.sum(upstream, axis=0)
    grad_fc1_shift = jnp.sum(gate_sums, axis=0)
    if not torus_block():
        early_block = repack(early_block, group_total * shard_total)
    early_sum = lax.psum_scatter(early_block, BOTH, scatter_dimension=0, tiled=True)[0]
    grad_middle_part, grad_gain_two, grad_shift_two = norm_two_pull(grad_normed_two)
    grad_middle = upstream + grad_middle_part
    middle_low = grad_middle.astype(jnp.bfloat16)
    grad_proj_shift = jnp.sum(middle_low.astype(jnp.float32), axis=0)
    grad_attended = jnp.einsum(
        "te,de->td", middle_low, proj_full, preferred_element_type=jnp.float32
    ).astype(jnp.bfloat16)
    grad_projected, projected_sums = attention_backward(
        projected, attn_probs, grad_attended, images
    )
    projected_sums = jnp.sum(projected_sums, axis=1)
    grad_qv = jnp.concatenate([projected_sums[0], projected_sums[2]])
    device_total = group_total * shard_total
    block_rows = model_width // device_total

    def blocks_of(value):
        value = value.astype(jnp.bfloat16)
        return [
            value[:, at : at + model_width].reshape(device_total, -1, model_width)
            for at in range(0, value.shape[1], model_width)
        ]

    vectors = [
        grad_qv,
        grad_proj_shift,
        grad_gain_two,
        grad_shift_two,
        grad_fc1_shift,
        grad_fc2_shift,
    ]
    vector_lengths = [member.shape[0] // device_total for member in vectors]

    def late_call():
        grad_qkv = [
            jnp.einsum(
                "td,te->de", normed_low, grad_projected[at], preferred_element_type=jnp.float32
            )
            for at in range(3)
        ]
        grad_proj = jnp.einsum(
            "td,te->de", attended, middle_low, preferred_element_type=jnp.float32
        )
        vector_block = jnp.concatenate(
            [member.reshape(device_total, -1) for member in vectors], axis=1
        ).astype(jnp.bfloat16)
        late = [block for member in grad_qkv + [grad_proj] for block in blocks_of(member)]
        late_rows = sum(member.shape[1] for member in late)
        extra = -(-vector_block.shape[1] // model_width)
        extra += -(late_rows + extra) % 8
        vector_block = jnp.pad(
            vector_block, ((0, 0), (0, extra * model_width - vector_block.shape[1]))
        ).reshape(device_total, extra, model_width)
        return jnp.concatenate(late + [vector_block], axis=1)

    late, grad_projected = start_late(late_call(), grad_projected)
    residual_reduced, shard_kernels, first_sums = first_backward(
        grad_projected,
        attention_full,
        stream,
        grad_middle,
        gain_one.astype(jnp.float32)[None],
        pixel_rows,
        images,
        shard_total,
        slot_count,
    )
    grad_gain_one, grad_shift_one, grad_conv_shift = jnp.sum(first_sums, axis=1)

    def pixels_call(tie):
        grads = residual_reduced if tie is None else together(residual_reduced, tie)[0]
        return pixel_grad(grads, patch_kernels, images, tokens, slot_count).transpose(0, 2, 1, 3)

    def out_call(tie):
        here = update if tie is None else together(update, tie)[0]
        block_out = middle + here + fc2_shift.astype(jnp.float32)
        return block_out.reshape(images, padded, model_width)[:, :tokens]

    grad_bias_row_part = jnp.dot(
        grad_conv_shift, cb_weight.astype(jnp.float32), precision=highest_precision
    )
    def code_call(group_kernels):
        grad_hidden_part = jnp.einsum(
            "bpd,pde->be",
            group_kernels * band_mask[:, None, None],
            kernel_gen.astype(jnp.float32),
            precision=highest_precision,
        )
        return jnp.concatenate(
            [grad_hidden_part, grad_bias_row_part[None]]
            + [
                member.reshape(-1, hyper_wide)
                for member in (grad_conv_shift, grad_gain_one, grad_shift_one)
            ]
        )

    group_width = model_width // group_total
    code_all = hidden_all.astype(jnp.bfloat16).astype(jnp.float32)

    def gen_call(group_kernels):
        grad_pre = group_kernels * band_mask[:, None, None]
        swapped = lax.all_to_all(
            grad_pre.reshape(slot_count, shard_patch, group_total, group_width).transpose(
                2, 0, 1, 3
            ),
            "grp",
            0,
            0,
        ).reshape(group_total * slot_count, shard_patch, group_width)
        grad_gen = jnp.einsum(
            "kpd,ke->pde",
            swapped,
            code_all.reshape(group_total * slot_count, hyper_wide),
            precision=highest_precision,
        )
        return grad_gen, jnp.sum(swapped, axis=0)

    late_end, code_grads, filled = reduce_late(
        shard_kernels, late, code_call, [pixels_call, out_call], gen_call
    )
    grad_pixels, block_out, (grad_gen, grad_gen_shift) = filled
    fold_total = model_width // hyper_wide
    conv_parts, gain_parts, shift_parts = (
        code_grads[:, slot_count + 1 + at * fold_total : slot_count + 1 + (at + 1) * fold_total].reshape(
            group_total, model_width
        )
        for at in range(3)
    )
    code_grads = jnp.pad(
        code_grads[:, : slot_count + 1], ((0, 0), (0, SLOT_ROWS - slot_count - 1), (0, 0))
    ).reshape(-1, hyper_wide)
    hyper_total = hyper_backward_call(flat_params, all_waves, all_usable, code_grads, slot_count)
    late_out = late_end(hyper_total[0])
    *hyper_total, early_sum = together(*hyper_total, early_sum)
    hyper_total = [
        member.reshape(param.shape) for member, param in zip(hyper_total, hyper_params)
    ]
    early_out = early_sum.astype(jnp.float32)

    def columns_of(value, total):
        return jnp.concatenate(
            [value[at * block_rows : (at + 1) * block_rows] for at in range(total)], axis=1
        )

    fc1_out = columns_of(early_out, hidden_full.shape[0])
    fc2_out = early_out[fc1_out.size // model_width :]
    qkv_out = columns_of(late_out, 3)
    proj_out = late_out[3 * block_rows : 4 * block_rows]
    vector_out = late_out[4 * block_rows :].reshape(-1)
    parts = []
    vector_at = 0
    for length in vector_lengths:
        parts.append(vector_out[vector_at : vector_at + length])
        vector_at += length
    device_at = group_at * shard_total + shard_at

    def own_part(value):
        return lax.dynamic_slice_in_dim(value, device_at * block_rows, block_rows, 1)

    conv_parts = own_part(conv_parts)
    grad_cb_weight = jnp.dot(conv_parts.T, bias_row_all, precision=highest_precision)
    reduced = (
        grad_cb_weight,
        jnp.sum(conv_parts, axis=0),
        jnp.sum(own_part(gain_parts), axis=0),
        jnp.sum(own_part(shift_parts), axis=0),
        qkv_out,
        parts[0],
        proj_out,
        parts[1],
        parts[2],
        parts[3],
        fc1_out,
        parts[4],
        fc2_out,
        parts[5],
    )
    return (
        block_out,
        grad_pixels,
        hyper_total[0],
        hyper_total[1],
        hyper_total[2],
        hyper_total[3],
        hyper_total[4],
        hyper_total[5],
        hyper_total[6],
        hyper_total[7],
        hyper_total[8],
        hyper_total[9],
        hyper_total[10],
        hyper_total[11],
        hyper_total[12],
        hyper_total[13],
        grad_gen,
        grad_gen_shift,
        reduced[0],
        reduced[1],
        reduced[2],
        reduced[3],
        reduced[4],
        reduced[5],
        reduced[6],
        reduced[7],
        reduced[8],
        reduced[9],
        reduced[10],
        reduced[11],
        reduced[12],
        reduced[13],
    )


def solution(mesh):
    return jax.shard_map(
        local,
        mesh=mesh,
        in_specs=(
            P(("grp", "img"), None, None, None),
            P(("grp", "img"), None, None),
            P("grp"),
            P("grp", None),
            P(),
            P(),
            P(),
            P(),
            P(),
            P(),
            P(),
            P(),
            P(),
            P(),
            P(),
            P(),
            P(),
            P(),
            P("img", None, None),
            P("img", None),
            P("img", None),
            P("img"),
            P("img"),
            P("img"),
            P("img", None),
            P("img"),
            P("img", None),
            P("img"),
            P("img"),
            P("img"),
            P("img", None),
            P("img"),
            P("img", None),
            P("img"),
        ),
        out_specs=(
            P(("grp", "img"), None, None),
            P(("grp", "img"), None, None, None),
            P(),
            P(),
            P(),
            P(),
            P(),
            P(),
            P(),
            P(),
            P(),
            P(),
            P(),
            P(),
            P(),
            P(),
            P("img", "grp", None),
            P("img", "grp"),
            P(("grp", "img"), None),
            P(("grp", "img")),
            P(("grp", "img")),
            P(("grp", "img")),
            P(("grp", "img"), None),
            P(("grp", "img")),
            P(("grp", "img"), None),
            P(("grp", "img")),
            P(("grp", "img")),
            P(("grp", "img")),
            P(("grp", "img"), None),
            P(("grp", "img")),
            P(("grp", "img"), None),
            P(("grp", "img")),
        ),
        check_vma=False,
    )
```

time: 518 us -> 422 us (0.81)
  matrix products: 162 us -> 37 us
  Pallas kernels: 22.5 us -> 121 us
  local copies, waits for them, and re-layouts: 81.6 us -> 40.6 us
  other arithmetic: 60.3 us -> 32.1 us
  waiting for transfers between devices: 88.3 us -> 94 us
    dot_general x49 -> x11, matrix products: 156 us -> 29.3 us  [the longest x3 10.1 us: late_call(): jnp.einsum('td,te->de', normed_low, grad_projected[at], preferred_element...]
    pallas_call x0 -> x7, Pallas kernels: none -> 95.7 us  [the longest x1 34.7 us: mlp(): pl.pallas_call(functools.partial(mlp_kernel, row_block, devices), grid=(s...]
    ppermute x18, waiting for transfers between devices: 56.3 us -> 77.1 us  [along_z(): return lax.ppermute(value, BOTH, moves)]
    unnamed x320 -> x110, local copies, waits for them, and re-layouts: 32.6 us -> 12.6 us
    ppermute x13 -> x3, starting transfers between devices: 20.3 us -> 4.6 us  [ordered_gather(): lax.ppermute(value, axis, [(i, (i + shift) % total) for i in range(total)])]
    ppermute x7 -> x12, starting transfers between devices: 3.73 us -> 18.2 us  [swap(): return lax.ppermute(value, BOTH, [(i, i ^ bit) for i in range(32)])]
    convert_element_type x7 -> x6, other arithmetic: 13.7 us -> 2.34 us  [the longest x1 1.52 us: local(): normed_two_low = normed_two.astype(jnp.bfloat16)]
    concatenate x6 -> x7, local copies, waits for them, and re-layouts: 9.6 us -> 0.52 us  [the longest x1 0.2 us: code_call(): jnp.concatenate([grad_hidden_part, grad_bias_row_part[None]] + [member.re...]
  transfers between devices with their start and end apart: 44 -> 37, of which waited for: 8 -> 16; matrix products, arithmetic and copies ran while one was open for 36% -> 23% of each run, Pallas kernels for 1% -> 21%
where the time goes in v2:
time: 422 us; the launch traced here: 416 us
  Pallas kernels  121 us (29%)
  waiting for transfers between devices  94 us (22%)
  starting transfers between devices  75.1 us (18%)
  local copies, waits for them, and re-layouts  40.6 us (10%)
  matrix products  37 us (9%)
  other arithmetic  32.1 us (8%)
  between operations  16.1 us (4%)
    ppermute x18, waiting for transfers between devices, along_z(): return lax.ppermute(value, BOTH, moves)  77.1 us
    ppermute x18, starting transfers between devices, along_z(): return lax.ppermute(value, BOTH, moves)  48.7 us
    pallas_call x1, Pallas kernels, mlp(): pl.pallas_call(functools.partial(mlp_kernel, row_block, devices), grid=(s...  34.7 us
    ppermute x12, starting transfers between devices, swap(): return lax.ppermute(value, BOTH, [(i, i ^ bit) for i in range(32)])  18.2 us
    pallas_call x1, Pallas kernels, first_backward(): pl.pallas_call(first_backward_kernel, grid=(images,), in_specs=[pl.BlockS...  17.6 us
    pallas_call x1, Pallas kernels, attention_backward(): pl.pallas_call(attention_backward_kernel, grid=(images,), in_specs=[pl.Bl...  17.4 us
    pallas_call x1, Pallas kernels, hyper_backward_call(): pl.pallas_call(functools.partial(hyper_backward_kernel, slots), out_shape...  15.4 us
    pallas_call x2, Pallas kernels, hyper_forward_call(): pl.pallas_call(functools.partial(hyper_forward_kernel, slots), out_shape=...  14.2 us
  transfers between devices with their start and end apart: 37, of which 16 were waited for; matrix products, arithmetic and copies ran while one was open for 23% of the time, Pallas kernels for 21%

profile of v2, /device:TPU:0, one launch (start us, length us, event | category | flops | bytes accessed | tf_op | source)
XLA Modules:
  0.0 415.7 jit_solution(944149974510168279)
XLA Ops:
  7.3 2.0 pad_maximum_fusion.2
  13.4 6.7 %hyper_forward.2 = f32[16,128]{1,0:T(8,128)} custom-call(f32[16,128]{1,0:T(8,128)} %pad_bitcast_fusion.waves_ref, f32[16,144]{1,0:T(8,128)} %pad_convert_fusion.1.usable_ref, f32[128,128]{1,0:T(8,128)} %refs_0_.5, f32[1,128]{1,0:T(1,128)} %bitcast.296, f32[128,384]{1,0:T(8,128)} %refs_2_.5, f32[1,256]{1,0:T(1,128)} %bitcast.292, f32[128,128]{1,0:T(8,128)} %refs_4_.5, ...), custom_call_target="tpu_custom_call" | custom-call | tf_op jit(solution)/shard_map/hyper_forward/pallas_call | solution.py:529
  21.4 4.6 %fusion.13 = bf16[8,32,768]{2,0,1:T(8,128)(2,1)S(1)} fusion(bf16[32,768,128]{2,1,0:T(8,128)(2,1)} %param.52, f32[8]{0:T(128)S(1)} %compare_convert_fusion, f32[32,768]{1,0:T(8,128)S(1)} %convert_element_type.370, f32[1,8,128]{2,1,0:T(8,128)S(1)} %pad_maximum_fusion.11, f32[16,128]{1,0:T(8,128)} %hyper_forward.2), kind=kOutput, calls=%fused_computation.42 | convolution fusion | flops 50923520 | bytes 6791200 | tf_op jit(solution)/shard_map/be,pde->bpd/dot_general | solution.py:1012
  28.3 6.2 %collective-permute-start = (bf16[288,768]{1,0:T(8,128)(2,1)}, bf16[288,768]{1,0:T(8,128)(2,1)}, u32[]{:S(2)}, u32[]{:S(2)}) collective-permute-start(bf16[288,768]{1,0:T(8,128)(2,1)} %fusion.30), channel_id=1, source_target_pairs={{0,2},{1,3},{2,4},{3,5},{4,6},{5,7},{8,10},{9,11},{10,12},{11,13},... | collective-permute-start | bytes 1327112 | tf_op jit(solution)/shard_map/ppermute | solution.py:118
  35.9 3.6 reshape.644
  39.5 2.1 pad.77
  41.6 20.7 %collective-permute-done.1 = bf16[288,768]{1,0:T(8,128)(2,1)} collective-permute-done((bf16[288,768]{1,0:T(8,128)(2,1)}, bf16[288,768]{1,0:T(8,128)(2,1)}, u32[]{:S(2)}, u32[]{:S(2)}) %collective-permute-start.1) | collective-permute-done | bytes 442400 | tf_op jit(solution)/shard_map/ppermute | solution.py:118
  64.2 16.4 %collective-permute-done.4 = bf16[288,768]{1,0:T(8,128)(2,1)S(1)} collective-permute-done((bf16[288,768]{1,0:T(8,128)(2,1)}, bf16[288,768]{1,0:T(8,128)(2,1)S(1)}, u32[]{:S(2)}, u32[]{:S(2)}) %collective-permute-start.4) | collective-permute-done | bytes 442400 | tf_op jit(solution)/shard_map/ppermute | solution.py:118
  82.6 18.1 %collective-permute-done.5 = bf16[288,768]{1,0:T(8,128)(2,1)S(1)} collective-permute-done((bf16[288,768]{1,0:T(8,128)(2,1)S(1)}, bf16[288,768]{1,0:T(8,128)(2,1)S(1)}, u32[]{:S(2)}, u32[]{:S(2)}) %collective-permute-start.5) | collective-permute-done | bytes 442400 | tf_op jit(solution)/shard_map/ppermute | solution.py:118
  102.0 1.7 select_bitcast_fusion.3
  105.5 1.5 collective-permute-start.8
  107.0 1.7 collective-permute-start.7
  111.6 7.4 %embed.1 = (bf16[2048,768]{1,0:T(8,128)(2,1)}, f32[832,768]{1,0:T(8,128)}, bf16[832,768]{1,0:T(8,128)(2,1)S(1)}) custom-call(s32[1]{0:T(128)} %bitcast.core_ref, bf16[4,288,768]{2,1,0:T(8,128)(2,1)S(1)} %pad_maximum_fusion.1.line_ref, bf16[4,288,768]{2,1,0:T(8,128)(2,1)S(1)} %collective-permute-done.6.other_ref, bf16[832,2048]{1,0:T(8,128)(2,1)} %bitcast.242), custom_call_target="tpu_custom_call" | custom-call | flops 2617245696 | bytes 13533184 | tf_op jit(solution)/shard_map/embed/pallas_call | solution.py:586
  121.5 2.6 fusion.1
  127.1 7.7 %attention_forward.1 = (bf16[832,768]{1,0:T(8,128)(2,1)S(1)}, bf16[4,12,208,208]{3,2,1,0:T(8,128)(2,1)}) custom-call(bf16[3,832,768]{2,1,0:T(8,128)(2,1)S(1)} %pad_maximum_fusion.projected_ref), custom_call_target="tpu_custom_call" | custom-call | flops 531628032 | bytes 9265152 | tf_op jit(solution)/shard_map/attention_forward/pallas_call | solution.py:330
  134.8 2.0 copy-done
  139.6 7.5 %hyper_forward.3 = f32[64,128]{1,0:T(8,128)} custom-call(f32[64,128]{1,0:T(8,128)} %bitcast.275, f32[64,192]{1,0:T(8,128)} %pad_convert_fusion.usable_ref, f32[128,128]{1,0:T(8,128)} %refs_0_.5, f32[1,128]{1,0:T(1,128)} %bitcast.297, f32[128,384]{1,0:T(8,128)} %refs_2_.5, f32[1,256]{1,0:T(1,128)} %bitcast.293, f32[128,128]{1,0:T(8,128)} %refs_4_.5, ...), custom_call_target="tpu_custom_call" | custom-call | tf_op jit(solution)/shard_map/hyper_forward/pallas_call | solution.py:529
  147.1 3.1 fusion.78
  151.7 1.5 add_convert_fusion.1.rows_ref
  153.2 7.1 %all-gather.6.cloned.1.call-done = bf16[6144,768]{1,0:T(8,128)(2,1)} async-done(((bf16[192,768]{1,0:T(8,128)(2,1)}), bf16[6144,768]{1,0:T(8,128)(2,1)}) %all-gather.6.cloned.1.call-update) | async-done | bytes 9437200 | tf_op jit(solution)/shard_map/all_gather | solution.py:209
  161.6 34.7 %mlp.1 = (f32[8,3072]{1,0:T(8,128)S(1)}, f32[832,768]{1,0:T(8,128)}, f32[832,768]{1,0:T(8,128)}, bf16[32,192,768]{2,1,0:T(8,128)(2,1)}) custom-call(bf16[832,768]{1,0:T(8,128)(2,1)S(1)} %copy-done.4, bf16[832,768]{1,0:T(8,128)(2,1)} %bitcast.251, bf16[4,8,192,768]{3,2,1,0:T(8,128)(2,1)} %bitcast.317, bf16[4,8,192,768]{3,2,1,0:T(8,128)(2,1)} %bitcast.318, ...), custom_call_target="tpu_custom_call" | custom-call | flops 23555211264 | bytes 26542080 | tf_op jit(solution)/shard_map/mlp/pallas_call | solution.py:818
  196.4 3.6 multiply_reduce_fusion
  202.3 3.5 convolution_convert_fusion.grad_ref
  205.8 17.4 %attention_backward.1 = (bf16[3,832,768]{2,1,0:T(8,128)(2,1)S(1)}, f32[3,8,768]{2,1,0:T(8,128)S(1)}) custom-call(bf16[3,832,768]{2,1,0:T(8,128)(2,1)} %copy-done, bf16[4,12,208,208]{3,2,1,0:T(8,128)(2,1)} %get-tuple-element.138.probs_ref, bf16[832,768]{1,0:T(8,128)(2,1)S(1)} %convolution_convert_fusion.grad_ref), custom_call_target="tpu_custom_call" | custom-call | tf_op jit(solution)/shard_map/attention_backward/pallas_call | solution.py:403
  223.2 1.9 copy-done.1
  225.2 4.3 %convolution_convert_fusion.4 = bf16[768,768]{1,0:T(8,128)(2,1)} fusion(bf16[832,768]{1,0:T(8,128)(2,1)} %copy-done.9, bf16[3,832,768]{2,1,0:T(8,128)(2,1)} %copy-done.1), kind=kOutput, calls=%fused_computation.24 | convolution fusion | flops 982056960 | bytes 3735552 | tf_op jit(solution)/shard_map/td,te->de/dot_general | solution.py:1150
  230.4 1.5 constant_dynamic-update-slice_fusion.10
  232.1 2.8 convolution_convert_fusion.3
  235.0 3.0 convolution_convert_fusion.2
  238.1 1.5 convolution_convert_fusion.1
  239.7 2.6 dynamic-slice_bitcast_fusion
  242.7 17.6 %first_backward.1 = (bf16[832,768]{1,0:T(8,128)(2,1)S(1)}, bf16[8,8,32,768]{3,2,1,0:T(8,128)(2,1)}, f32[3,8,768]{2,1,0:T(8,128)S(1)}) custom-call(bf16[3,832,768]{2,1,0:T(8,128)(2,1)} %copy-done.1, bf16[768,3072]{1,0:T(8,128)(2,1)} %all-gather.4.cloned.1.call-done.query_ref.key_ref.value_ref, ...), custom_call_target="tpu_custom_call" | custom-call | tf_op jit(solution)/shard_map/first_backward/pallas_call | solution.py:682
  261.4 2.9 dynamic-slice_bitcast_fusion.2
  264.9 2.5 add_convert_fusion
  268.0 1.8 fusion
  272.2 4.1 collective-permute-start.12
  276.5 1.5 collective-permute-start.16
  278.6 6.4 %pixel_grad.1 = f32[4,196,8,256]{3,2,1,0:T(8,128)} custom-call(bf16[832,768]{1,0:T(8,128)(2,1)S(1)} %copy-done.6, bf16[2048,768]{1,0:T(8,128)(2,1)S(1)} %copy-done.2), custom_call_target="tpu_custom_call" | custom-call | tf_op jit(solution)/shard_map/pixel_grad/pallas_call | solution.py:873
  287.1 4.6 %collective-permute-start.14 = (bf16[256,768]{1,0:T(8,128)(2,1)S(1)}, bf16[256,768]{1,0:T(8,128)(2,1)S(1)}, u32[]{:S(2)}, u32[]{:S(2)}) collective-permute-start(bf16[256,768]{1,0:T(8,128)(2,1)S(1)} %get-tuple-element.237), channel_id=1, source_target_pairs={{0,2},{1,3},{2,4},{3,5},{8,10},{9,11},{10,12},{11,13},{16,18},{17,... | collective-permute-start | bytes 1179656 | tf_op jit(solution)/shard_map/ppermute | solution.py:118
  292.2 2.4 copy.102
  294.6 10.3 %collective-permute-done.14 = bf16[256,768]{1,0:T(8,128)(2,1)S(1)} collective-permute-done((bf16[256,768]{1,0:T(8,128)(2,1)S(1)}, bf16[256,768]{1,0:T(8,128)(2,1)S(1)}, u32[]{:S(2)}, u32[]{:S(2)}) %collective-permute-start.14) | collective-permute-done | bytes 393248 | tf_op jit(solution)/shard_map/ppermute | solution.py:118
  305.2 8.1 %collective-permute-start.18 = (bf16[256,768]{1,0:T(8,128)(2,1)S(1)}, bf16[256,768]{1,0:T(8,128)(2,1)S(1)}, u32[]{:S(2)}, u32[]{:S(2)}) collective-permute-start(bf16[256,768]{1,0:T(8,128)(2,1)S(1)} %get-tuple-element.234), channel_id=1, source_target_pairs={{0,2},{1,3},{2,4},{3,5},{4,6},{5,7},{8,10},{9,11},{10,12},{11,13},... | collective-permute-start | bytes 1179656 | tf_op jit(solution)/shard_map/ppermute | solution.py:118
  313.3 1.5 collective-permute-start.19
  316.1 1.7 collective-permute-start.23
  318.1 2.3 collective-permute-start.22
  320.7 3.7 collective-permute-done.19
  324.6 3.0 convolution_bitcast_fusion.1
  329.1 2.0 collective-permute-start.21
  331.1 2.0 collective-permute-done.21
  333.1 1.6 collective-permute-start.24
  334.8 3.0 collective-permute-done.24
  337.8 1.6 collective-permute-start.25
  339.5 2.1 collective-permute-done.25
  341.5 6.3 %collective-permute-start.26 = (f32[2,27,128]{2,1,0:T(8,128)S(1)}, f32[2,27,128]{2,1,0:T(8,128)S(1)}, u32[]{:S(2)}, u32[]{:S(2)}) collective-permute-start(f32[2,27,128]{2,1,0:T(8,128)S(1)} %pad_maximum_fusion.8), channel_id=1, source_target_pairs={{0,16},{1,17},{2,18},{3,19},{4,20},{5,21},{6,22},{7,23},{8,24},{9,... | collective-permute-start | bytes 82952 | tf_op jit(solution)/shard_map/ppermute | solution.py:113
  348.6 3.9 collective-permute-start.27
  352.6 2.7 collective-permute-done.27
  359.6 3.5 all-to-all-start
  364.0 5.5 %collective-permute-start.29 = (bf16[104,768]{1,0:T(8,128)(2,1)S(1)}, bf16[104,768]{1,0:T(8,128)(2,1)S(1)}, u32[]{:S(2)}, u32[]{:S(2)}) collective-permute-start(bf16[104,768]{1,0:T(8,128)(2,1)S(1)} %get-tuple-element.247), channel_id=1, source_target_pairs={{0,2},{1,3},{2,4},{3,5},{8,10},{9,11},{10,12},{11,13},{16,18},{17,... | collective-permute-start | bytes 479240 | tf_op jit(solution)/shard_map/ppermute | solution.py:118
  370.2 15.4 %hyper_backward.1 = (f32[128,128]{1,0:T(8,128)}, f32[1,128]{1,0:T(1,128)}, f32[128,384]{1,0:T(8,128)}, f32[1,256]{1,0:T(1,128)}, f32[128,128]{1,0:T(8,128)}, /*i...) custom-call(f32[64,128]{1,0:T(8,128)} %bitcast.276, ...), custom_call_target="tpu_custom_call" | custom-call | tf_op jit(solution)/shard_map/hyper_backward/pallas_call | solution.py:537
  385.8 4.6 %collective-permute-start.31 = (bf16[104,768]{1,0:T(8,128)(2,1)S(1)}, bf16[104,768]{1,0:T(8,128)(2,1)S(1)}, u32[]{:S(2)}, u32[]{:S(2)}) collective-permute-start(bf16[104,768]{1,0:T(8,128)(2,1)S(1)} %get-tuple-element.244), channel_id=1, source_target_pairs={{0,2},{1,3},{2,4},{3,5},{4,6},{5,7},{8,10},{9,11},{10,12},{11,13},... | collective-permute-start | bytes 479240 | tf_op jit(solution)/shard_map/ppermute | solution.py:118
  390.3 1.5 collective-permute-start.32
  393.1 4.4 %collective-permute-done.32 = bf16[104,768]{1,0:T(8,128)(2,1)S(1)} collective-permute-done((bf16[104,768]{1,0:T(8,128)(2,1)S(1)}, bf16[104,768]{1,0:T(8,128)(2,1)S(1)}, u32[]{:S(2)}, u32[]{:S(2)}) %collective-permute-start.32) | collective-permute-done | bytes 159776 | tf_op jit(solution)/shard_map/ppermute | solution.py:118
  401.4 4.3 %convolution_bitcast_fusion = f32[32,192,128]{2,1,0:T(8,128)} fusion(f32[4,8,32,192]{3,1,2,0:T(8,128)S(1)} %all-to-all-done, f32[4,8,128]{2,1,0:T(8,128)S(1)} %pad_maximum_fusion.9, f32[4,16,128]{2,1,0:T(8,128)S(1)} %bitcast.284), kind=kOutput, calls=%fused_computation.17 | convolution fusion | flops 301998080 | bytes 4227072 | tf_op jit(solution)/shard_map/kpd,ke->pde/dot_general | solution.py:1224
  405.8 1.6 slice.317
  (306 shorter events, 58.2 us)
Async XLA Ops:
  7.2 4.7 %copy-start.42 = (s32[1,8]{1,0:T(1,128)S(1)}, s32[1,8]{1,0:T(1,128)}, u32[]{:S(2)}) copy-start(s32[1,8]{1,0:T(1,128)} %param.37) | copy-start | bytes 100
  7.2 114.3 %all-gather.4.cloned.1.call-start = ((), (), s32[]{:S(2)}) async-start(), calls=%async_computation.2 | async-start | bytes 5308416 | tf_op jit(solution)/shard_map/all_gather | solution.py:1042
  9.2 10.9 %copy-start.26 = (bf16[96,128]{1,0:T(8,128)(2,1)S(1)}, bf16[96,128]{1,0:T(8,128)(2,1)}, u32[]{:S(2)}) copy-start(bf16[96,128]{1,0:T(8,128)(2,1)} %param.54) | copy-start | bytes 73732
  9.2 10.9 %copy-start.31 = (bf16[96]{0:T(256)(128)(2,1)S(1)}, bf16[96]{0:T(256)(128)(2,1)}, u32[]{:S(2)}) copy-start(bf16[96]{0:T(256)(128)(2,1)} %param.55) | copy-start | bytes 580
  9.2 11.9 %copy-start.35 = (bf16[96]{0:T(256)(128)(2,1)S(1)}, bf16[96]{0:T(256)(128)(2,1)}, u32[]{:S(2)}) copy-start(bf16[96]{0:T(256)(128)(2,1)} %param.56) | copy-start | bytes 580
  9.2 11.9 %copy-start.36 = (bf16[96]{0:T(256)(128)(2,1)S(1)}, bf16[96]{0:T(256)(128)(2,1)}, u32[]{:S(2)}) copy-start(bf16[96]{0:T(256)(128)(2,1)} %param.57) | copy-start | bytes 580
  9.2 11.9 %copy-start.37 = (bf16[192]{0:T(256)(128)(2,1)S(1)}, bf16[192]{0:T(256)(128)(2,1)}, u32[]{:S(2)}) copy-start(bf16[192]{0:T(256)(128)(2,1)} %param.59) | copy-start | bytes 1156
  9.2 11.9 %copy-start.38 = (bf16[96]{0:T(256)(128)(2,1)S(1)}, bf16[96]{0:T(256)(128)(2,1)}, u32[]{:S(2)}) copy-start(bf16[96]{0:T(256)(128)(2,1)} %param.61) | copy-start | bytes 580
  9.3 12.0 %copy-start.39 = (bf16[96]{0:T(256)(128)(2,1)S(1)}, bf16[96]{0:T(256)(128)(2,1)}, u32[]{:S(2)}) copy-start(bf16[96]{0:T(256)(128)(2,1)} %param.62) | copy-start | bytes 580
  9.3 12.0 %copy-start.40 = (bf16[96]{0:T(256)(128)(2,1)S(1)}, bf16[96]{0:T(256)(128)(2,1)}, u32[]{:S(2)}) copy-start(bf16[96]{0:T(256)(128)(2,1)} %param.63) | copy-start | bytes 580
  9.3 12.0 %copy-start.30 = (bf16[384]{0:T(512)(128)(2,1)S(1)}, bf16[384]{0:T(512)(128)(2,1)}, u32[]{:S(2)}) copy-start(bf16[384]{0:T(512)(128)(2,1)} %param.65) | copy-start | bytes 2308
  9.3 12.0 %copy-start.41 = (bf16[96]{0:T(256)(128)(2,1)S(1)}, bf16[96]{0:T(256)(128)(2,1)}, u32[]{:S(2)}) copy-start(bf16[96]{0:T(256)(128)(2,1)} %param.67) | copy-start | bytes 580
  9.3 12.1 %copy-start.27 = (bf16[32,768]{1,0:T(8,128)(2,1)S(1)}, bf16[32,768]{1,0:T(8,128)(2,1)}, u32[]{:S(2)}) copy-start(bf16[32,768]{1,0:T(8,128)(2,1)} %param.53) | copy-start | bytes 147460
  9.3 151.0 %all-gather.6.cloned.1.call-start = ((), (), s32[]{:S(2)}) async-start(), calls=%async_computation.4 | async-start | bytes 9732096 | tf_op jit(solution)/shard_map/all_gather | solution.py:209
  11.2 394.6 %reduce-scatter.2.cloned.1.call-start = ((), (), s32[]{:S(2)}) async-start(), calls=%async_computation.3 | async-start | bytes 9732096 | tf_op jit(solution)/shard_map/reduce_scatter | solution.py:1115
  26.0 8.6 %copy-start.24 = (bf16[4,196,768]{2,0,1:T(4,128)(2,1)S(1)}, bf16[4,196,768]{2,0,1:T(4,128)(2,1)}, u32[]{:S(2)}) copy-start(bf16[4,196,768]{2,0,1:T(4,128)(2,1)} %param.35) | copy-start | bytes 3612676
  26.1 9.8 %copy-start.20 = (bf16[8,32,768]{2,1,0:T(8,128)(2,1)}, bf16[8,32,768]{2,1,0:T(8,128)(2,1)S(1)}, u32[]{:S(2)}) copy-start(bf16[8,32,768]{2,1,0:T(8,128)(2,1)S(1)} %copy.89) | copy-start | bytes 1179652
  27.1 35.2 %collective-permute-start.1 = (bf16[288,768]{1,0:T(8,128)(2,1)}, bf16[288,768]{1,0:T(8,128)(2,1)}, u32[]{:S(2)}, u32[]{:S(2)}) collective-permute-start(bf16[288,768]{1,0:T(8,128)(2,1)} %fusion.30), channel_id=1, source_target_pairs={{2,0},{3,1},{4,2},{5,3},{6,4},{7,5},{10,8},{11,9},{12,10},{13,11},... | collective-permute-start | bytes 1327112 | tf_op jit(solution)/shard_map/ppermute | solution.py:118
  28.3 33.9 %collective-permute-start = (bf16[288,768]{1,0:T(8,128)(2,1)}, bf16[288,768]{1,0:T(8,128)(2,1)}, u32[]{:S(2)}, u32[]{:S(2)}) collective-permute-start(bf16[288,768]{1,0:T(8,128)(2,1)} %fusion.30), channel_id=1, source_target_pairs={{0,2},{1,3},{2,4},{3,5},{4,6},{5,7},{8,10},{9,11},{10,12},{11,13},... | collective-permute-start | bytes 1327112 | tf_op jit(solution)/shard_map/ppermute | solution.py:118
  62.2 18.4 %collective-permute-start.4 = (bf16[288,768]{1,0:T(8,128)(2,1)}, bf16[288,768]{1,0:T(8,128)(2,1)S(1)}, u32[]{:S(2)}, u32[]{:S(2)}) collective-permute-start(bf16[288,768]{1,0:T(8,128)(2,1)} %collective-permute-done.1), channel_id=1, source_target_pairs={{2,0},{3,1},{4,2},{5,3},{10,8},{11,9},{12,10},{13,11},{18,16},{19,... | collective-permute-start | bytes 1327112 | tf_op jit(solution)/shard_map/ppermute | solution.py:118
  63.5 18.4 %collective-permute-start.2 = (bf16[288,768]{1,0:T(8,128)(2,1)}, bf16[288,768]{1,0:T(8,128)(2,1)S(1)}, u32[]{:S(2)}, u32[]{:S(2)}) collective-permute-start(bf16[288,768]{1,0:T(8,128)(2,1)} %collective-permute-done), channel_id=1, source_target_pairs={{2,4},{3,5},{4,6},{5,7},{10,12},{11,13},{12,14},{13,15},{18,20},{1... | collective-permute-start | bytes 1327112 | tf_op jit(solution)/shard_map/ppermute | solution.py:118
  80.6 20.1 %collective-permute-start.5 = (bf16[288,768]{1,0:T(8,128)(2,1)S(1)}, bf16[288,768]{1,0:T(8,128)(2,1)S(1)}, u32[]{:S(2)}, u32[]{:S(2)}) collective-permute-start(bf16[288,768]{1,0:T(8,128)(2,1)S(1)} %collective-permute-done.4), channel_id=1, source_target_pairs={{2,0},{3,1},{10,8},{11,9},{18,16},{19,17},{26,24},{27,25}} | collective-permute-start | bytes 1327112 | tf_op jit(solution)/shard_map/ppermute | solution.py:118
  81.9 20.0 %collective-permute-start.3 = (bf16[288,768]{1,0:T(8,128)(2,1)S(1)}, bf16[288,768]{1,0:T(8,128)(2,1)S(1)}, u32[]{:S(2)}, u32[]{:S(2)}) collective-permute-start(bf16[288,768]{1,0:T(8,128)(2,1)S(1)} %collective-permute-done.2), channel_id=1, source_target_pairs={{4,6},{5,7},{12,14},{13,15},{20,22},{21,23},{28,30},{29,31}} | collective-permute-start | bytes 1327112 | tf_op jit(solution)/shard_map/ppermute | solution.py:118
  103.9 7.6 %collective-permute-start.6 = (bf16[4,288,768]{2,1,0:T(8,128)(2,1)S(1)}, bf16[4,288,768]{2,1,0:T(8,128)(2,1)S(1)}, u32[]{:S(2)}, u32[]{:S(2)}) collective-permute-start(bf16[4,288,768]{2,1,0:T(8,128)(2,1)S(1)} %pad_maximum_fusion.1.line_ref), channel_id=1, source_target_pairs={{0,1},{1,0},{2,3},{3,2},{4,5},{5,4},{6,7},{7,6},{8,9},{9,8},{10,11... | collective-permute-start | bytes 5308424 | tf_op jit(solution)/shard_map/ppermute | solution.py:113
  104.1 6.7 %copy-start.33 = (s32[9]{0:T(128)}, s32[9]{0:T(128)S(1)}, u32[]{:S(2)}) copy-start(s32[9]{0:T(128)S(1)} %pad_add_fusion) | copy-start | bytes 112
  104.1 5.7 %collective-permute-start.9 = (s32[9]{0:T(128)S(1)}, s32[9]{0:T(128)S(1)}, u32[]{:S(2)}, u32[]{:S(2)}) collective-permute-start(s32[9]{0:T(128)S(1)} %pad_add_fusion), channel_id=1, source_target_pairs={{0,8},{8,16},{16,24},{24,0},{1,9},{9,17},{17,25},{25,1},{2,10},{10... | collective-permute-start | bytes 116 | tf_op jit(solution)/shard_map/ppermute | solution.py:903
  105.5 4.4 %collective-permute-start.8 = (s32[9]{0:T(128)S(1)}, s32[9]{0:T(128)}, u32[]{:S(2)}, u32[]{:S(2)}) collective-permute-start(s32[9]{0:T(128)S(1)} %pad_add_fusion), channel_id=1, source_target_pairs={{0,16},{8,24},{16,0},{24,8},{1,17},{9,25},{17,1},{25,9},{2,18},{10... | collective-permute-start | bytes 116 | tf_op jit(solution)/shard_map/ppermute | solution.py:903
  107.0 3.8 collective-permute-start.7
  127.1 11.9 %copy-start.29 = (s32[64]{0:T(128)S(1)}, s32[64]{0:T(128)}, u32[]{:S(2)}) copy-start(s32[64]{0:T(128)} %and_select_fusion.1) | copy-start | bytes 772
  127.1 20.0 %copy-start.3 = (f32[832,768]{1,0:T(8,128)S(1)}, f32[832,768]{1,0:T(8,128)}, u32[]{:S(2)}) copy-start(f32[832,768]{1,0:T(8,128)} %get-tuple-element.140.stream_ref) | copy-start | bytes 7667716
  196.3 3.6 copy-start.13
  196.4 4.0 copy-start.16
  202.3 3.5 copy-start.18
  242.3 22.5 %collective-permute-start.11 = (bf16[2,2,4,104,768]{4,3,2,1,0:T(8,128)(2,1)}, bf16[2,2,4,104,768]{4,3,2,1,0:T(8,128)(2,1)}, u32[]{:S(2)}, u32[]{:S(2)}) collective-permute-start(bf16[2,2,4,104,768]{4,3,2,1,0:T(8,128)(2,1)} %get-tuple-element.230), channel_id=1, source_target_pairs={{0,1},{1,0},{2,3},{3,2},{4,5},{5,4},{6,7},{7,6},{8,9},{9,8},{10,11... | collective-permute-start | bytes 7667720 | tf_op jit(solution)/shard_map/ppermute | solution.py:113
  264.3 3.8 collective-permute-start.10
  270.8 14.3 %collective-permute-start.13 = (bf16[256,768]{1,0:T(8,128)(2,1)}, bf16[256,768]{1,0:T(8,128)(2,1)}, u32[]{:S(2)}, u32[]{:S(2)}) collective-permute-start(bf16[256,768]{1,0:T(8,128)(2,1)} %get-tuple-element.238), channel_id=1, source_target_pairs={{6,4},{7,5},{14,12},{15,13},{22,20},{23,21},{30,28},{31,29}} | collective-permute-start | bytes 1179656 | tf_op jit(solution)/shard_map/ppermute | solution.py:118
  272.2 12.9 %collective-permute-start.12 = (bf16[256,768]{1,0:T(8,128)(2,1)}, bf16[256,768]{1,0:T(8,128)(2,1)}, u32[]{:S(2)}, u32[]{:S(2)}) collective-permute-start(bf16[256,768]{1,0:T(8,128)(2,1)} %get-tuple-element.239), channel_id=1, source_target_pairs={{0,2},{1,3},{8,10},{9,11},{16,18},{17,19},{24,26},{25,27}} | collective-permute-start | bytes 1179656 | tf_op jit(solution)/shard_map/ppermute | solution.py:118
  276.5 18.1 %collective-permute-start.16 = (bf16[2,2,104,768]{3,2,1,0:T(8,128)(2,1)S(1)}, bf16[2,2,104,768]{3,2,1,0:T(8,128)(2,1)S(1)}, u32[]{:S(2)}, u32[]{:S(2)}) collective-permute-start(bf16[2,2,104,768]{3,2,1,0:T(8,128)(2,1)S(1)} %dynamic-slice_bitcast_fusion.4), channel_id=1, source_target_pairs={{0,8},{1,9},{2,10},{3,11},{4,12},{5,13},{6,14},{7,15},{8,0},{9,1},... | collective-permute-start | bytes 1916936 | tf_op jit(solution)/shard_map/ppermute | solution.py:113
  278.0 16.6 %collective-permute-start.17 = (bf16[2,2,104,768]{3,2,1,0:T(8,128)(2,1)S(1)}, bf16[2,2,104,768]{3,2,1,0:T(8,128)(2,1)S(1)}, u32[]{:S(2)}, u32[]{:S(2)}) collective-permute-start(bf16[2,2,104,768]{3,2,1,0:T(8,128)(2,1)S(1)} %dynamic-slice_bitcast_fusion.3), channel_id=1, source_target_pairs={{0,16},{1,17},{2,18},{3,19},{4,20},{5,21},{6,22},{7,23},{8,24},{9,... | collective-permute-start | bytes 1916936 | tf_op jit(solution)/shard_map/ppermute | solution.py:113
  278.6 13.0 %copy-start.14 = (f32[832,768]{1,0:T(8,128)S(1)}, f32[832,768]{1,0:T(8,128)}, u32[]{:S(2)}) copy-start(f32[832,768]{1,0:T(8,128)} %copy-done.12) | copy-start | bytes 7667716
  278.6 13.0 %copy-start.23 = (f32[832,768]{1,0:T(8,128)S(1)}, f32[832,768]{1,0:T(8,128)}, u32[]{:S(2)}) copy-start(f32[832,768]{1,0:T(8,128)} %get-tuple-element.159) | copy-start | bytes 7667716
  286.4 8.3 %collective-permute-start.15 = (bf16[256,768]{1,0:T(8,128)(2,1)S(1)}, bf16[256,768]{1,0:T(8,128)(2,1)S(1)}, u32[]{:S(2)}, u32[]{:S(2)}) collective-permute-start(bf16[256,768]{1,0:T(8,128)(2,1)S(1)} %get-tuple-element.236), channel_id=1, source_target_pairs={{4,2},{5,3},{6,4},{7,5},{12,10},{13,11},{14,12},{15,13},{20,18},{2... | collective-permute-start | bytes 1179656 | tf_op jit(solution)/shard_map/ppermute | solution.py:118
  287.1 17.9 %collective-permute-start.14 = (bf16[256,768]{1,0:T(8,128)(2,1)S(1)}, bf16[256,768]{1,0:T(8,128)(2,1)S(1)}, u32[]{:S(2)}, u32[]{:S(2)}) collective-permute-start(bf16[256,768]{1,0:T(8,128)(2,1)S(1)} %get-tuple-element.237), channel_id=1, source_target_pairs={{0,2},{1,3},{2,4},{3,5},{8,10},{9,11},{10,12},{11,13},{16,18},{17,... | collective-permute-start | bytes 1179656 | tf_op jit(solution)/shard_map/ppermute | solution.py:118
  292.2 32.3 %slice-start = ((s8[6291456]{0:T(1024)(128)(4,1)}), s8[2097152]{0:T(1024)(128)(4,1)S(1)}, s32[]{:S(2)}) async-start(s8[6291456]{0:T(1024)(128)(4,1)} %bitcast.240), calls=%async_computation.5 | async-start | bytes 4194304
  294.6 30.0 %slice-start.1 = ((s8[6291456]{0:T(1024)(128)(4,1)}), s8[4194304]{0:T(1024)(128)(4,1)S(1)}, s32[]{:S(2)}) async-start(s8[6291456]{0:T(1024)(128)(4,1)} %bitcast.240), calls=%async_computation.6 | async-start | bytes 8388608
  294.6 18.7 %copy-start.25 = (bf16[2,2,104,768]{3,2,1,0:T(8,128)(2,1)}, bf16[2,2,104,768]{3,2,1,0:T(8,128)(2,1)S(1)}, u32[]{:S(2)}) copy-start(bf16[2,2,104,768]{3,2,1,0:T(8,128)(2,1)S(1)} %collective-permute-done.17) | copy-start | bytes 1916932
  305.2 15.5 %collective-permute-start.18 = (bf16[256,768]{1,0:T(8,128)(2,1)S(1)}, bf16[256,768]{1,0:T(8,128)(2,1)S(1)}, u32[]{:S(2)}, u32[]{:S(2)}) collective-permute-start(bf16[256,768]{1,0:T(8,128)(2,1)S(1)} %get-tuple-element.234), channel_id=1, source_target_pairs={{0,2},{1,3},{2,4},{3,5},{4,6},{5,7},{8,10},{9,11},{10,12},{11,13},... | collective-permute-start | bytes 1179656 | tf_op jit(solution)/shard_map/ppermute | solution.py:118
  313.3 11.1 %collective-permute-start.19 = (bf16[256,768]{1,0:T(8,128)(2,1)S(1)}, bf16[256,768]{1,0:T(8,128)(2,1)S(1)}, u32[]{:S(2)}, u32[]{:S(2)}) collective-permute-start(bf16[256,768]{1,0:T(8,128)(2,1)S(1)} %get-tuple-element.235), channel_id=1, source_target_pairs={{2,0},{3,1},{4,2},{5,3},{6,4},{7,5},{10,8},{11,9},{12,10},{13,11},... | collective-permute-start | bytes 1179656 | tf_op jit(solution)/shard_map/ppermute | solution.py:118
  316.1 16.9 %collective-permute-start.23 = (bf16[2,104,768]{2,1,0:T(8,128)(2,1)S(1)}, bf16[2,104,768]{2,1,0:T(8,128)(2,1)S(1)}, u32[]{:S(2)}, u32[]{:S(2)}) collective-permute-start(bf16[2,104,768]{2,1,0:T(8,128)(2,1)S(1)} %dynamic-slice_bitcast_fusion.7), channel_id=1, source_target_pairs={{0,8},{1,9},{2,10},{3,11},{4,12},{5,13},{6,14},{7,15},{8,0},{9,1},... | collective-permute-start | bytes 958472 | tf_op jit(solution)/shard_map/ppermute | solution.py:113
  318.1 15.0 %collective-permute-start.22 = (bf16[2,104,768]{2,1,0:T(8,128)(2,1)S(1)}, bf16[2,104,768]{2,1,0:T(8,128)(2,1)S(1)}, u32[]{:S(2)}, u32[]{:S(2)}) collective-permute-start(bf16[2,104,768]{2,1,0:T(8,128)(2,1)S(1)} %dynamic-slice_bitcast_fusion.8), channel_id=1, source_target_pairs={{0,16},{1,17},{2,18},{3,19},{4,20},{5,21},{6,22},{7,23},{8,24},{9,... | collective-permute-start | bytes 958472 | tf_op jit(solution)/shard_map/ppermute | solution.py:113
  324.6 6.5 %copy-start.28 = (f32[64,128]{1,0:T(8,128)S(1)}, f32[64,128]{1,0:T(8,128)}, u32[]{:S(2)}) copy-start(f32[64,128]{1,0:T(8,128)} %hyper_forward.3) | copy-start | bytes 98308
  327.8 1.2 collective-permute-start.20
  329.1 4.0 collective-permute-start.21
  333.1 4.7 %collective-permute-start.24 = (f32[27,128]{1,0:T(8,128)S(1)}, f32[27,128]{1,0:T(8,128)S(1)}, u32[]{:S(2)}, u32[]{:S(2)}) collective-permute-start(f32[27,128]{1,0:T(8,128)S(1)} %add.425), channel_id=1, source_target_pairs={{0,4},{1,5},{2,6},{3,7},{4,0},{5,1},{6,2},{7,3},{8,12},{9,13},{10,... | collective-permute-start | bytes 41480 | tf_op jit(solution)/shard_map/ppermute | solution.py:113
  337.8 3.7 collective-permute-start.25
  341.5 11.0 %collective-permute-start.26 = (f32[2,27,128]{2,1,0:T(8,128)S(1)}, f32[2,27,128]{2,1,0:T(8,128)S(1)}, u32[]{:S(2)}, u32[]{:S(2)}) collective-permute-start(f32[2,27,128]{2,1,0:T(8,128)S(1)} %pad_maximum_fusion.8), channel_id=1, source_target_pairs={{0,16},{1,17},{2,18},{3,19},{4,20},{5,21},{6,22},{7,23},{8,24},{9,... | collective-permute-start | bytes 82952 | tf_op jit(solution)/shard_map/ppermute | solution.py:113
  348.0 4.7 %collective-permute-start.28 = (bf16[104,768]{1,0:T(8,128)(2,1)S(1)}, bf16[104,768]{1,0:T(8,128)(2,1)S(1)}, u32[]{:S(2)}, u32[]{:S(2)}) collective-permute-start(bf16[104,768]{1,0:T(8,128)(2,1)S(1)} %get-tuple-element.248), channel_id=1, source_target_pairs={{6,4},{7,5},{14,12},{15,13},{22,20},{23,21},{30,28},{31,29}} | collective-permute-start | bytes 479240 | tf_op jit(solution)/shard_map/ppermute | solution.py:118
  348.6 6.7 %collective-permute-start.27 = (bf16[104,768]{1,0:T(8,128)(2,1)S(1)}, bf16[104,768]{1,0:T(8,128)(2,1)S(1)}, u32[]{:S(2)}, u32[]{:S(2)}) collective-permute-start(bf16[104,768]{1,0:T(8,128)(2,1)S(1)} %get-tuple-element.249), channel_id=1, source_target_pairs={{0,2},{1,3},{8,10},{9,11},{16,18},{17,19},{24,26},{25,27}} | collective-permute-start | bytes 479240 | tf_op jit(solution)/shard_map/ppermute | solution.py:118
  358.4 11.1 %copy-start.32 = (pred[16]{0:T(512)(128)(4,1)S(1)}, pred[16]{0:T(512)(128)(4,1)}, u32[]{:S(2)}) copy-start(pred[16]{0:T(512)(128)(4,1)} %constant.291.clone.1) | copy-start | bytes 52
  359.6 41.1 %all-to-all-start = ((f32[4,8,32,192]{3,1,2,0:T(8,128)}), f32[4,8,32,192]{3,1,2,0:T(8,128)S(1)}, u32[]{:S(2)}, u32[]{:S(2)}) async-start(f32[4,8,32,192]{3,1,2,0:T(8,128)} %bitcast.234), calls=%async_computation.1 | async-start | bytes 2097152 | tf_op jit(solution)/shard_map/all_to_all | solution.py:1216
  363.3 22.2 %collective-permute-start.30 = (bf16[104,768]{1,0:T(8,128)(2,1)S(1)}, bf16[104,768]{1,0:T(8,128)(2,1)S(1)}, u32[]{:S(2)}, u32[]{:S(2)}) collective-permute-start(bf16[104,768]{1,0:T(8,128)(2,1)S(1)} %get-tuple-element.246), channel_id=1, source_target_pairs={{4,2},{5,3},{6,4},{7,5},{12,10},{13,11},{14,12},{15,13},{20,18},{2... | collective-permute-start | bytes 479240 | tf_op jit(solution)/shard_map/ppermute | solution.py:118
  364.0 21.6 %collective-permute-start.29 = (bf16[104,768]{1,0:T(8,128)(2,1)S(1)}, bf16[104,768]{1,0:T(8,128)(2,1)S(1)}, u32[]{:S(2)}, u32[]{:S(2)}) collective-permute-start(bf16[104,768]{1,0:T(8,128)(2,1)S(1)} %get-tuple-element.247), channel_id=1, source_target_pairs={{0,2},{1,3},{2,4},{3,5},{8,10},{9,11},{10,12},{11,13},{16,18},{17,... | collective-permute-start | bytes 479240 | tf_op jit(solution)/shard_map/ppermute | solution.py:118
  385.8 7.3 %collective-permute-start.31 = (bf16[104,768]{1,0:T(8,128)(2,1)S(1)}, bf16[104,768]{1,0:T(8,128)(2,1)S(1)}, u32[]{:S(2)}, u32[]{:S(2)}) collective-permute-start(bf16[104,768]{1,0:T(8,128)(2,1)S(1)} %get-tuple-element.244), channel_id=1, source_target_pairs={{0,2},{1,3},{2,4},{3,5},{4,6},{5,7},{8,10},{9,11},{10,12},{11,13},... | collective-permute-start | bytes 479240 | tf_op jit(solution)/shard_map/ppermute | solution.py:118
  390.3 7.2 %collective-permute-start.32 = (bf16[104,768]{1,0:T(8,128)(2,1)S(1)}, bf16[104,768]{1,0:T(8,128)(2,1)S(1)}, u32[]{:S(2)}, u32[]{:S(2)}) collective-permute-start(bf16[104,768]{1,0:T(8,128)(2,1)S(1)} %get-tuple-element.245), channel_id=1, source_target_pairs={{2,0},{3,1},{4,2},{5,3},{6,4},{7,5},{10,8},{11,9},{12,10},{13,11},... | collective-permute-start | bytes 479240 | tf_op jit(solution)/shard_map/ppermute | solution.py:118
  (18 other events, 35.4 us)
Sparse Core Ops, SparseCore 0:
  10.3 65.8 all-gather.3
  79.8 80.4 all-gather.5
  196.5 141.3 reduce-scatter.1
